TPU v7x, 32 devices: a whole 2x2x4 slice. The times are simulated.
32 devices in a mesh: rep: 2 (over y), shard: 16 (over z, x, core).
Axes of the slice: x: 2, y: 2, z: 4, core: 2. Of those that a mesh axis runs over, the one named last changes fastest.
Arguments:
- block_input: bfloat16 [32768, 768], P(('rep', 'shard')), may hold values from -6 to 6
- history: bfloat16 [4, 32768, 768], P(None, ('rep', 'shard')), may hold values from -6 to 6
- cotangent: bfloat16 [32768, 768], P(('rep', 'shard')), may hold values from -6 to 6
- span_start: int32 [32], P(('rep', 'shard')), may hold values from 0 to 768, as said below
- w_qkv: bfloat16 [768, 2304], P('shard'), may hold values from -0.21875 to 0.21875
- w_out: bfloat16 [768, 768], P('shard'), may hold values from -4 to 4
- w_up: bfloat16 [768, 3072], P('shard'), may hold values from -0.21875 to 0.21875
- w_down: bfloat16 [3072, 768], P('shard'), may hold values from -0.109375 to 0.109375
- ln_gains: bfloat16 [2, 768], P(None, 'shard'), may hold values from 0.5 to 1.5
- ln_biases: bfloat16 [2, 768], P(None, 'shard'), may hold values from -3 to 3
- mix_weights: float32 [5], replicated, may hold values from 0.3 to 1
Outputs:
- next_input: bfloat16 [32768, 768], P(('rep', 'shard'))
- grad_input: float32 [32768, 768], P(('rep', 'shard'))
- grad_history: float32 [4, 32768, 768], P(None, ('rep', 'shard'))
- grad_mix: float32 [5], replicated
- grad_w_qkv: float32 [768, 2304], P('shard')
- grad_w_out: float32 [768, 768], P('shard')
- grad_w_up: float32 [768, 3072], P('shard')
- grad_w_down: float32 [3072, 768], P('shard')
- grad_gains: float32 [2, 768], P(None, 'shard')
- grad_bias_first: float32 [768], P('shard')
- grad_bias_second: float32 [768], P('shard')
Inputs may be any that keep to these rules, and one draw needn't show every extreme that they name: Sequence n's picture span covers positions span_start[n] to span_start[n] + 255 of that sequence.
All inputs are finite; a program needn't handle non-finite values.
Results may differ from a plain program's by a relative error of at most 0.017.
Values may be sent and summed in bfloat16 or wider, within the bound.
A program may use at most 256 MiB of HBM per device.

v0:
```python
import jax
import jax.numpy as jnp
from jax import lax
from jax.sharding import PartitionSpec as P

HEADS = 12
SPAN = 256


eps = 1e-05


def layer_norm(values, gain_row, bias_row):
    average = jnp.mean(values, axis=-1, keepdims=True)
    centered = values - average
    inverse_std = lax.rsqrt(jnp.mean(centered * centered, axis=-1, keepdims=True) + eps)
    normed = centered * inverse_std
    return (normed * gain_row + bias_row, normed, inverse_std)


def layer_norm_back(incoming, normed, inverse_std, gain_row):
    scaled = incoming * gain_row
    inner = (
        scaled
        - jnp.mean(scaled, axis=-1, keepdims=True)
        - normed * jnp.mean(scaled * normed, axis=-1, keepdims=True)
    )
    return (inverse_std * inner, jnp.sum(incoming * normed, axis=0), jnp.sum(incoming, axis=0))


def rotary_tables(length, head_width):
    half_width = head_width // 2
    frequency = jnp.exp(
        -jnp.log(10000.0) * jnp.arange(half_width, dtype=jnp.float32) * (2.0 / head_width)
    )
    angles = jnp.arange(length, dtype=jnp.float32)[:, None] * frequency[None, :]
    angles = jnp.concatenate([angles, angles], axis=-1)[:, None, :]
    return (jnp.cos(angles), jnp.sin(angles))


def rotate(values, cosine, sine):
    half_width = values.shape[-1] // 2
    turned = jnp.concatenate([-values[..., half_width:], values[..., :half_width]], axis=-1)
    return values * cosine + turned * sine


def rotate_back(incoming, cosine, sine):
    half_width = incoming.shape[-1] // 2
    weighted = incoming * sine
    turned = jnp.concatenate([weighted[..., half_width:], -weighted[..., :half_width]], axis=-1)
    return incoming * cosine + turned


def gelu_parts(upper):
    normal_cdf = 0.5 * (1.0 + lax.erf(upper * 0.7071067811865476))
    density = jnp.exp(-0.5 * upper * upper) * 0.3989422804014327
    return (upper * normal_cdf, normal_cdf + upper * density)


def visible(row_pos, col_pos, span_begin):
    row_in = (row_pos >= span_begin) & (row_pos < span_begin + SPAN)
    col_in = (col_pos >= span_begin) & (col_pos < span_begin + SPAN)
    return (col_pos[None, :] <= row_pos[:, None]) | row_in[:, None] & col_in[None, :]


def block_scores(query_block, key_rows, row_pos, col_pos, span_begin):
    factor = query_block.shape[2] ** (-0.5)
    scores = (
        jnp.einsum("qhd,khd->hqk", query_block, key_rows, preferred_element_type=jnp.float32)
        * factor
    )
    return jnp.where(visible(row_pos, col_pos, span_begin)[None], scores, -1e30)


def attend_forward(query_rows, key_rows, value_rows, span_begin):
    length = query_rows.shape[0]
    block_rows = min(512, length)
    block_count = length // block_rows
    col_pos = jnp.arange(length, dtype=jnp.int32)

    def one_block(block_index):
        first_row = block_index * block_rows
        row_pos = first_row + jnp.arange(block_rows, dtype=jnp.int32)
        query_block = lax.dynamic_slice_in_dim(query_rows, first_row, block_rows, 0)
        scores = block_scores(query_block, key_rows, row_pos, col_pos, span_begin)
        row_max = jnp.max(scores, axis=-1, keepdims=True)
        log_sums = row_max + jnp.log(jnp.sum(jnp.exp(scores - row_max), axis=-1, keepdims=True))
        attn_probs = jnp.exp(scores - log_sums).astype(jnp.bfloat16)
        block_out = jnp.einsum(
            "hqk,khd->qhd", attn_probs, value_rows, preferred_element_type=jnp.float32
        )
        return (block_out.astype(jnp.bfloat16), log_sums[..., 0])

    outputs, log_sums = lax.map(one_block, jnp.arange(block_count, dtype=jnp.int32))
    return (outputs.reshape(query_rows.shape), log_sums)


def attend_backward(query_rows, key_rows, value_rows, grad_rows, log_sums, span_begin):
    length = query_rows.shape[0]
    block_rows = min(512, length)
    block_count = length // block_rows
    col_pos = jnp.arange(length, dtype=jnp.int32)
    factor = query_rows.shape[2] ** (-0.5)

    def one_block(running, block_index):
        grad_keys, grad_values = running
        first_row = block_index * block_rows
        row_pos = first_row + jnp.arange(block_rows, dtype=jnp.int32)
        query_block = lax.dynamic_slice_in_dim(query_rows, first_row, block_rows, 0)
        grad_block = lax.dynamic_slice_in_dim(grad_rows, first_row, block_rows, 0)
        scores = block_scores(query_block, key_rows, row_pos, col_pos, span_begin)
        attn_probs = jnp.exp(scores - log_sums[block_index][..., None])
        grad_probs = jnp.einsum(
            "qhd,khd->hqk", grad_block, value_rows, preferred_element_type=jnp.float32
        )
        delta_sum = jnp.sum(attn_probs * grad_probs, axis=-1, keepdims=True)
        grad_scores = (attn_probs * (grad_probs - delta_sum)).astype(jnp.bfloat16)
        grad_query = (
            jnp.einsum("hqk,khd->qhd", grad_scores, key_rows, preferred_element_type=jnp.float32)
            * factor
        )
        grad_keys = (
            grad_keys
            + jnp.einsum(
                "hqk,qhd->khd", grad_scores, query_block, preferred_element_type=jnp.float32
            )
            * factor
        )
        grad_values = grad_values + jnp.einsum(
            "hqk,qhd->khd",
            attn_probs.astype(jnp.bfloat16),
            grad_block,
            preferred_element_type=jnp.float32,
        )
        return ((grad_keys, grad_values), grad_query)

    zero_rows = jnp.zeros(key_rows.shape, jnp.float32)
    (grad_keys, grad_values), grad_queries = lax.scan(
        one_block, (zero_rows, zero_rows), jnp.arange(block_count, dtype=jnp.int32)
    )
    return (grad_queries.reshape(query_rows.shape), grad_keys, grad_values)


def local(
    block_input,
    history,
    cotangent,
    span_start,
    w_qkv,
    w_out,
    w_up,
    w_down,
    ln_gains,
    ln_biases,
    mix_weights,
):
    tokens, model_width = block_input.shape
    seq_count = span_start.shape[0]
    length = tokens // seq_count
    head_count = HEADS
    head_width = model_width // head_count
    past_count = history.shape[0]
    full_qkv, full_out, full_up, full_down, gains_low, biases_low = (
        lax.all_gather(w_qkv, "shard", axis=0, tiled=True),
        lax.all_gather(w_out, "shard", axis=0, tiled=True),
        lax.all_gather(w_up, "shard", axis=0, tiled=True),
        lax.all_gather(w_down, "shard", axis=0, tiled=True),
        lax.all_gather(ln_gains, "shard", axis=1, tiled=True),
        lax.all_gather(ln_biases, "shard", axis=1, tiled=True),
    )
    gains = gains_low.astype(jnp.float32)
    biases = biases_low.astype(jnp.float32)
    inputs_f = block_input.astype(jnp.float32)
    normed1_out, normed1, inverse1 = layer_norm(inputs_f, gains[0], biases[0])
    act1 = normed1_out.astype(jnp.bfloat16)
    projected = jnp.dot(act1, full_qkv, preferred_element_type=jnp.float32)
    cosine, sine = rotary_tables(length, head_width)
    split_shape = (seq_count, length, head_count, head_width)
    q_rot = rotate(projected[:, :model_width].reshape(split_shape), cosine, sine).astype(
        jnp.bfloat16
    )
    k_rot = rotate(
        projected[:, model_width : 2 * model_width].reshape(split_shape), cosine, sine
    ).astype(jnp.bfloat16)
    v_low = projected[:, 2 * model_width :].reshape(split_shape).astype(jnp.bfloat16)

    def forward_sequence(inputs_now):
        query_rows, key_rows, value_rows, span_begin = inputs_now
        return attend_forward(query_rows, key_rows, value_rows, span_begin)

    mixed, log_sums = lax.map(forward_sequence, (q_rot, k_rot, v_low, span_start))
    mixed = mixed.reshape(tokens, model_width)
    middle = inputs_f + jnp.dot(mixed, full_out, preferred_element_type=jnp.float32)
    normed2_out, normed2, inverse2 = layer_norm(middle, gains[1], biases[1])
    act2 = normed2_out.astype(jnp.bfloat16)
    upper = jnp.dot(act2, full_up, preferred_element_type=jnp.float32)
    activated, slope = gelu_parts(upper)
    hidden = activated.astype(jnp.bfloat16)
    output = middle + jnp.dot(hidden, full_down, preferred_element_type=jnp.float32)
    earlier = jnp.einsum("k,ktd->td", mix_weights[:past_count], history.astype(jnp.float32))
    next_input = (earlier + mix_weights[past_count] * output).astype(jnp.bfloat16)
    grad_f = cotangent.astype(jnp.float32)
    grad_history = mix_weights[:past_count][:, None, None] * grad_f[None]
    history_terms = jnp.einsum("ktd,td->k", history, cotangent, preferred_element_type=jnp.float32)
    partial_mix = jnp.concatenate([history_terms, jnp.sum(grad_f * output)[None]])
    grad_mix = lax.psum(partial_mix, ("rep", "shard"))
    full_qkv, full_out, full_up, full_down = (
        lax.all_gather(w_qkv, "shard", axis=0, tiled=True),
        lax.all_gather(w_out, "shard", axis=0, tiled=True),
        lax.all_gather(w_up, "shard", axis=0, tiled=True),
        lax.all_gather(w_down, "shard", axis=0, tiled=True),
    )
    grad_output = mix_weights[past_count] * grad_f
    grad_branch = grad_output.astype(jnp.bfloat16)
    grad_w_down = jnp.einsum("tf,td->fd", hidden, grad_branch, preferred_element_type=jnp.float32)
    grad_hidden = jnp.einsum(
        "td,fd->tf", grad_branch, full_down, preferred_element_type=jnp.float32
    )
    grad_upper = (grad_hidden * slope).astype(jnp.bfloat16)
    grad_w_up = jnp.einsum("td,tf->df", act2, grad_upper, preferred_element_type=jnp.float32)
    grad_act2 = jnp.einsum("tf,df->td", grad_upper, full_up, preferred_element_type=jnp.float32)
    grad_norm2, grad_gain2, grad_bias2 = layer_norm_back(grad_act2, normed2, inverse2, gains[1])
    grad_middle = grad_output + grad_norm2
    grad_attended = grad_middle.astype(jnp.bfloat16)
    grad_w_out = jnp.einsum("ti,tj->ij", mixed, grad_attended, preferred_element_type=jnp.float32)
    grad_mixed = jnp.einsum(
        "tj,ij->ti", grad_attended, full_out, preferred_element_type=jnp.float32
    ).astype(jnp.bfloat16)

    def backward_sequence(inputs_now):
        query_rows, key_rows, value_rows, grad_rows, sums_now, span_begin = inputs_now
        return attend_backward(query_rows, key_rows, value_rows, grad_rows, sums_now, span_begin)

    grad_q, grad_k, grad_v = lax.map(
        backward_sequence,
        (q_rot, k_rot, v_low, grad_mixed.reshape(split_shape), log_sums, span_start),
    )
    grad_q = rotate_back(grad_q, cosine, sine).reshape(tokens, model_width)
    grad_k = rotate_back(grad_k, cosine, sine).reshape(tokens, model_width)
    grad_projected = jnp.concatenate(
        [grad_q, grad_k, grad_v.reshape(tokens, model_width)], axis=1
    ).astype(jnp.bfloat16)
    grad_w_qkv = jnp.einsum("ti,tj->ij", act1, grad_projected, preferred_element_type=jnp.float32)
    grad_act1 = jnp.einsum(
        "tj,ij->ti", grad_projected, full_qkv, preferred_element_type=jnp.float32
    )
    grad_norm1, grad_gain1, grad_bias1 = layer_norm_back(grad_act1, normed1, inverse1, gains[0])
    grad_input = grad_middle + grad_norm1
    grad_gains = jnp.stack([grad_gain1, grad_gain2])
    grad_biases = jnp.stack([grad_bias1, grad_bias2])
    local_grads = (grad_w_qkv, grad_w_out, grad_w_up, grad_w_down, grad_gains, grad_biases)
    owned = (
        lax.psum_scatter(
            local_grads[0].astype(jnp.bfloat16), "shard", scatter_dimension=0, tiled=True
        ).astype(jnp.float32),
        lax.psum_scatter(
            local_grads[1].astype(jnp.bfloat16), "shard", scatter_dimension=0, tiled=True
        ).astype(jnp.float32),
        lax.psum_scatter(
            local_grads[2].astype(jnp.bfloat16), "shard", scatter_dimension=0, tiled=True
        ).astype(jnp.float32),
        lax.psum_scatter(
            local_grads[3].astype(jnp.bfloat16), "shard", scatter_dimension=0, tiled=True
        ).astype(jnp.float32),
        lax.psum_scatter(
            local_grads[4].astype(jnp.bfloat16), "shard", scatter_dimension=1, tiled=True
        ).astype(jnp.float32),
        lax.psum_scatter(
            local_grads[5].astype(jnp.bfloat16), "shard", scatter_dimension=1, tiled=True
        ).astype(jnp.float32),
    )
    owned = (
        lax.psum(owned[0].astype(jnp.bfloat16), "rep").astype(jnp.float32),
        lax.psum(owned[1].astype(jnp.bfloat16), "rep").astype(jnp.float32),
        lax.psum(owned[2].astype(jnp.bfloat16), "rep").astype(jnp.float32),
        lax.psum(owned[3].astype(jnp.bfloat16), "rep").astype(jnp.float32),
        lax.psum(owned[4].astype(jnp.bfloat16), "rep").astype(jnp.float32),
        lax.psum(owned[5].astype(jnp.bfloat16), "rep").astype(jnp.float32),
    )
    return (
        next_input,
        grad_input,
        grad_history,
        grad_mix,
        owned[0],
        owned[1],
        owned[2],
        owned[3],
        owned[4],
        owned[5][0],
        owned[5][1],
    )


def solution(mesh):
    placed = (
        P(("rep", "shard"), None),
        P(None, ("rep", "shard"), None),
        P(("rep", "shard"), None),
        P(("rep", "shard")),
        P("shard", None),
        P("shard", None),
        P("shard", None),
        P("shard", None),
        P(None, "shard"),
        P(None, "shard"),
        P(),
    )
    return jax.shard_map(
        local,
        mesh=mesh,
        in_specs=placed,
        out_specs=(
            P(("rep", "shard"), None),
            P(("rep", "shard"), None),
            P(None, ("rep", "shard"), None),
            P(),
            P("shard", None),
            P("shard", None),
            P("shard", None),
            P("shard", None),
            P(None, "shard"),
            P("shard"),
            P("shard"),
        ),
        check_vma=False,
    )
```

profile of v0, /device:TPU:0, one launch (start us, length us, event | category | flops | bytes accessed | tf_op | source)
XLA Modules:
  0.0 911.4 jit_solution(13864573590740779968)
XLA Ops:
  12.0 23.4 %all-gather = bf16[16,48,2]{1,2,0:T(2,128)(2,1)S(1)} all-gather(bf16[1,48,2]{1,2,0:T(2,128)(2,1)} %bitcast.170), channel_id=1, replica_groups=mesh['rep'=2,'shard'=16] {'shard'}, dimensions={0}, use_global_device_ids=true | all-gather | bytes 3264 | tf_op jit(solution)/shard_map/all_gather | solution.py:168
  35.5 17.7 %all-gather.1 = bf16[16,48,2]{1,2,0:T(2,128)(2,1)S(1)} all-gather(bf16[1,48,2]{1,2,0:T(2,128)(2,1)} %bitcast.171), channel_id=1, replica_groups=mesh['rep'=2,'shard'=16] {'shard'}, dimensions={0}, use_global_device_ids=true | all-gather | bytes 3264 | tf_op jit(solution)/shard_map/all_gather | solution.py:169
  59.3 9.4 %fusion.43 = f32[1,1024,768]{2,0,1:T(1,128)} fusion(bf16[4,1024,768]{2,1,0:T(8,128)(2,1)} %param.16, f32[5]{0:T(128)S(1)} %copy-done.50), kind=kOutput, calls=%fused_computation.65 | convolution fusion | flops 6291456 | bytes 9437204 | tf_op jit(solution)/shard_map/k,ktd->td/dot_general | solution.py:200
  68.7 8.5 copy.101
  77.8 6.3 fusion.79
  102.6 4.3 fusion.62
  106.9 78.3 %while.52 = (s32[]{:T(128)}, bf16[2,512,12,64]{1,3,2,0:T(8,128)(2,1)S(1)}, f32[2,12,512]{2,1,0:T(8,128)S(1)}, s32[2]{0:T(128)S(1)}, s32[]{:T(128)}, /*index=5*/s...) while((s32[]{:T(128)}, ...), condition=%wide.region_5.6_spmd.clone.clone, body=%wide.region_2.5_spmd.clone.clone.sunk | while | flops 1681784320 | bytes 82558176 | solution.py:94
  109.9 12.0 %fusion.130 = (f32[12,512]{1,0:T(8,128)S(1)}, f32[12,512,1024]{2,1,0:T(8,128)}) fusion(pred[512,1024]{1,0:T(8,128)(4,1)S(1)} %fusion.129, bf16[1024,12,64]{0,2,1:T(8,128)(2,1)S(1)} %get-tuple-element.733, bf16[1024,12,64]{0,2,1:T(8,128)(2,1)} %get-tuple-element.732, s32[]{:T(128)S(6)} %select_n.68), kind=kOutput, calls=%fused_computation.5.clone.1 | convolution fusion | flops 824174592 | bytes 28073988 | tf_op jit(solution)/shard_map/while/body/eval_jaxpr/while/body/eval_jaxpr/qhd,khd->hqk/dot_general | solution.py:69
  122.0 12.3 %exponential_reduce_fusion.2 = f32[12,512]{1,0:T(8,128)S(1)} fusion(f32[12,512,1024]{2,1,0:T(8,128)} %get-tuple-element.682, f32[12,512]{1,0:T(8,128)S(1)} %get-tuple-element.683, pred[512,1024]{1,0:T(8,128)(4,1)S(1)} %fusion.129), kind=kLoop, calls=%fused_computation.3.clone.1 | loop fusion | flops 25159680 | bytes 25739264 | tf_op jit(solution)/shard_map/while/body/eval_jaxpr/while/body/eval_jaxpr/reduce_sum | solution.py:87
  134.3 11.7 %fusion.131 = bf16[2,512,12,64]{1,3,2,0:T(8,128)(2,1)S(1)} fusion(bf16[2,512,12,64]{1,3,2,0:T(8,128)(2,1)S(1)} %get-tuple-element.714, s32[]{:T(128)S(6)} %copy.143, bf16[1024,12,64]{0,2,1:T(8,128)(2,1)} %get-tuple-element.734, f32[12,512,1024]{2,1,0:T(8,128)} %get-tuple-element.682, f32[12,512]{1,0:T(8,128)S(1)} %get-tuple-element.684, ...), kind=kOutput, calls=%fused_computation.12.clone.1 | convolution fusion | flops 830865408 | bytes 28082180 | tf_op jit(solution)/shard_map/while/body/eval_jaxpr/while/body/eval_jaxpr/hqk,khd->qhd/dot_general | solution.py:89
  149.1 12.0 %fusion.130 = (f32[12,512]{1,0:T(8,128)S(1)}, f32[12,512,1024]{2,1,0:T(8,128)}) fusion(pred[512,1024]{1,0:T(8,128)(4,1)S(1)} %fusion.129, bf16[1024,12,64]{0,2,1:T(8,128)(2,1)S(1)} %get-tuple-element.733, bf16[1024,12,64]{0,2,1:T(8,128)(2,1)} %get-tuple-element.732, s32[]{:T(128)S(6)} %select_n.68), kind=kOutput, calls=%fused_computation.5.clone.1 | convolution fusion | flops 824174592 | bytes 28073988 | tf_op jit(solution)/shard_map/while/body/eval_jaxpr/while/body/eval_jaxpr/qhd,khd->hqk/dot_general | solution.py:69
  161.1 12.0 %exponential_reduce_fusion.2 = f32[12,512]{1,0:T(8,128)S(1)} fusion(f32[12,512,1024]{2,1,0:T(8,128)} %get-tuple-element.682, f32[12,512]{1,0:T(8,128)S(1)} %get-tuple-element.683, pred[512,1024]{1,0:T(8,128)(4,1)S(1)} %fusion.129), kind=kLoop, calls=%fused_computation.3.clone.1 | loop fusion | flops 25159680 | bytes 25739264 | tf_op jit(solution)/shard_map/while/body/eval_jaxpr/while/body/eval_jaxpr/reduce_sum | solution.py:87
  173.2 11.6 %fusion.131 = bf16[2,512,12,64]{1,3,2,0:T(8,128)(2,1)S(1)} fusion(bf16[2,512,12,64]{1,3,2,0:T(8,128)(2,1)S(1)} %get-tuple-element.714, s32[]{:T(128)S(6)} %copy.143, bf16[1024,12,64]{0,2,1:T(8,128)(2,1)} %get-tuple-element.734, f32[12,512,1024]{2,1,0:T(8,128)} %get-tuple-element.682, f32[12,512]{1,0:T(8,128)S(1)} %get-tuple-element.684, ...), kind=kOutput, calls=%fused_computation.12.clone.1 | convolution fusion | flops 830865408 | bytes 28082180 | tf_op jit(solution)/shard_map/while/body/eval_jaxpr/while/body/eval_jaxpr/hqk,khd->qhd/dot_general | solution.py:89
  196.5 13.6 %multiply_convert_fusion.1 = (bf16[1024,3072]{1,0:T(8,128)(2,1)}, f32[1024,3072]{1,0:T(8,128)}) fusion(bf16[768,3072]{1,0:T(8,128)(2,1)} %all-gather.11.cloned.1.call-done, f32[1024,768]{0,1:T(8,128)} %copy-done.8, f32[768]{0:T(1024)S(1)} %copy-done.45, f32[768]{0:T(1024)S(1)} %copy-done.40, f32[1024]{0:T(1024)S(1)} %add_rsqrt_fusion, ...), kind=kOutput, calls=%fused_computation.62 | convolution fusion | flops 4851499008 | bytes 26753024 | tf_op jit(solution)/shard_map/dot_general | solution.py:196
  210.1 12.8 %fusion.42 = bf16[1024,3072]{1,0:T(8,128)(2,1)S(1)} fusion(f32[1024,3072]{1,0:T(8,128)} %get-tuple-element.553, bf16[3072,768]{1,0:T(8,128)(2,1)} %all-gather.13.cloned.1.call-done, bf16[1024,768]{0,1:T(8,128)(2,1)S(1)} %copy-done.16, f32[]{:T(128)} %bitcast.4), kind=kOutput, calls=%fused_computation.60 | convolution fusion | flops 4865654784 | bytes 25165828 | tf_op jit(solution)/shard_map/td,fd->tf/dot_general | solution.py:216
  222.9 7.3 fusion.85
  233.8 4.6 multiply_reduce_fusion.2
  238.5 12.5 %multiply_reduce_fusion.3 = (f32[]{:T(128)}, bf16[1024,768]{0,1:T(8,128)(2,1)}, f32[1024,768]{0,1:T(8,128)S(1)}) fusion(bf16[1024,768]{0,1:T(8,128)(2,1)S(1)} %copy-done.16, f32[]{:T(128)} %bitcast.4, f32[1,1024,768]{1,2,0:T(8,128)} %copy.101, f32[1024]{0:T(1024)S(1)} %broadcast_multiply_fusion.4, f32[1024,768]{0,1:T(8,128)S(1)} %copy-done.9, ...), kind=kOutput, calls=%fused_computation.104 | convolution fusion | flops 4844421120 | bytes 26758152 | tf_op jit(solution)/shard_map/dot_general | solution.py:199
  256.7 4.4 convolution_convert_fusion.3
  261.1 239.0 %while.53 = (s32[]{:T(128)}, f32[1024,12,64]{0,2,1:T(8,128)}, f32[1024,12,64]{0,2,1:T(8,128)}, f32[2,512,12,64]{1,0,3,2:T(2,128)}, s32[2]{0:T(128)S(1)}, /*index...) while((s32[]{:T(128)}, f32[1024,12,64]{0,2,1:T(8,128)}, ...), condition=%wide.region_12.13_spmd.clone.clone, body=%wide.region_10.12_spmd.clone.clone.sunk | while | flops 4126801408 | bytes 231923056 | solution.py:138
  266.6 11.6 %fusion.141 = f32[12,512,1024]{2,1,0:T(8,128)} fusion(bf16[1024,12,64]{0,2,1:T(8,128)(2,1)S(1)} %get-tuple-element.781, bf16[1024,12,64]{0,2,1:T(8,128)(2,1)} %get-tuple-element.778, s32[]{:T(128)S(6)} %select_n.72), kind=kOutput, calls=%fused_computation.40.clone.1 | convolution fusion | flops 805306368 | bytes 27525124 | tf_op jit(solution)/shard_map/while/body/eval_jaxpr/while/body/eval_jaxpr/qhd,khd->hqk/dot_general | solution.py:69
  278.2 13.5 %bitcast_add_fusion.7 = f32[1024,12,64]{0,2,1:T(8,128)} fusion(f32[1024,12,64]{0,2,1:T(8,128)} %get-tuple-element.758, f32[12,512,1024]{2,1,0:T(8,128)} %fusion.141, f32[12,512]{1,0:T(8,128)S(1)} %dynamic-slice_bitcast_fusion.2, pred[512,1024]{1,0:T(8,128)(4,1)S(1)} %fusion.143, pred[]{:T(512)S(6)} %compare.3, ...), kind=kOutput, calls=%fused_computation.31.clone.1 | convolution fusion | flops 832045056 | bytes 32800772 | tf_op jit(solution)/shard_map/while/body/eval_jaxpr/while/body/eval_jaxpr/hqk,qhd->khd/dot_general | solution.py:129
  291.7 18.2 %multiply_reduce_fusion.9 = (f32[12,512]{1,0:T(8,128)S(1)}, f32[12,512,1024]{2,1,0:T(8,128)}) fusion(f32[12,512,1024]{2,1,0:T(8,128)} %fusion.141, f32[12,512]{1,0:T(8,128)S(1)} %dynamic-slice_bitcast_fusion.2, pred[512,1024]{1,0:T(8,128)(4,1)S(1)} %fusion.143, bf16[1024,12,64]{0,2,1:T(8,128)(2,1)} %get-tuple-element.784, ...), kind=kOutput, calls=%fused_computation.26.clone.1 | convolution fusion | flops 836757504 | bytes 53264388 | tf_op jit(solution)/shard_map/while/body/eval_jaxpr/while/body/eval_jaxpr/qhd,khd->hqk/dot_general | solution.py:113
  309.9 21.3 %multiply_convert_fusion.6 = bf16[12,512,1024]{2,1,0:T(8,128)(2,1)} fusion(f32[12,512,1024]{2,1,0:T(8,128)} %get-tuple-element.698, f32[12,512,1024]{2,1,0:T(8,128)} %fusion.141, f32[12,512]{1,0:T(8,128)S(1)} %get-tuple-element.699, f32[12,512]{1,0:T(8,128)S(1)} %dynamic-slice_bitcast_fusion.2, pred[512,1024]{1,0:T(8,128)(4,1)S(1)} %fusion.143), kind=kLoop, calls=%fused_computation.25.clone.1 | loop fusion | flops 37748736 | bytes 63488000 | tf_op jit(solution)/shard_map/while/body/eval_jaxpr/while/body/eval_jaxpr/convert_element_type | solution.py:117
  331.1 9.7 %multiply_bitcast_fusion.3 = f32[1,512,12,64]{1,3,2,0:T(8,128)} fusion(bf16[12,512,1024]{2,1,0:T(8,128)(2,1)} %multiply_convert_fusion.6, bf16[1024,12,64]{0,2,1:T(8,128)(2,1)S(1)} %get-tuple-element.781), kind=kOutput, calls=%fused_computation.35.clone.1 | convolution fusion | flops 805699584 | bytes 15728640 | tf_op jit(solution)/shard_map/while/body/eval_jaxpr/while/body/eval_jaxpr/hqk,khd->qhd/dot_general | solution.py:119
  340.8 9.0 bitcast_add_fusion.6
  351.4 28.7 %dynamic_update_slice.41 = f32[2,512,12,64]{1,0,3,2:T(2,128)} dynamic-update-slice(f32[2,512,12,64]{1,0,3,2:T(2,128)} %get-tuple-element.759, f32[1,512,12,64]{1,0,3,2:T(1,128)S(1)} %copy.136, s32[]{:T(128)S(6)} %copy.153, s32[]{:T(128)} %constant.129.clone.1..sunk.1, s32[]{:T(128)} %constant.129.clone.1..sunk.1, s32[]{:T(128)} %constant.129.clone.1..sunk.1) | dynamic-update-slice | bytes 3145732 | tf_op jit(solution)/shard_map/while/body/eval_jaxpr/while/body/jit(dynamic_update_index_in_dim)/dynamic_update_slice | solution.py:138
  385.1 11.5 %fusion.141 = f32[12,512,1024]{2,1,0:T(8,128)} fusion(bf16[1024,12,64]{0,2,1:T(8,128)(2,1)S(1)} %get-tuple-element.781, bf16[1024,12,64]{0,2,1:T(8,128)(2,1)} %get-tuple-element.778, s32[]{:T(128)S(6)} %select_n.72), kind=kOutput, calls=%fused_computation.40.clone.1 | convolution fusion | flops 805306368 | bytes 27525124 | tf_op jit(solution)/shard_map/while/body/eval_jaxpr/while/body/eval_jaxpr/qhd,khd->hqk/dot_general | solution.py:69
  396.6 14.2 %bitcast_add_fusion.7 = f32[1024,12,64]{0,2,1:T(8,128)} fusion(f32[1024,12,64]{0,2,1:T(8,128)} %get-tuple-element.758, f32[12,512,1024]{2,1,0:T(8,128)} %fusion.141, f32[12,512]{1,0:T(8,128)S(1)} %dynamic-slice_bitcast_fusion.2, pred[512,1024]{1,0:T(8,128)(4,1)S(1)} %fusion.143, pred[]{:T(512)S(6)} %compare.3, ...), kind=kOutput, calls=%fused_computation.31.clone.1 | convolution fusion | flops 832045056 | bytes 32800772 | tf_op jit(solution)/shard_map/while/body/eval_jaxpr/while/body/eval_jaxpr/hqk,qhd->khd/dot_general | solution.py:129
  410.8 18.1 %multiply_reduce_fusion.9 = (f32[12,512]{1,0:T(8,128)S(1)}, f32[12,512,1024]{2,1,0:T(8,128)}) fusion(f32[12,512,1024]{2,1,0:T(8,128)} %fusion.141, f32[12,512]{1,0:T(8,128)S(1)} %dynamic-slice_bitcast_fusion.2, pred[512,1024]{1,0:T(8,128)(4,1)S(1)} %fusion.143, bf16[1024,12,64]{0,2,1:T(8,128)(2,1)} %get-tuple-element.784, ...), kind=kOutput, calls=%fused_computation.26.clone.1 | convolution fusion | flops 836757504 | bytes 53264388 | tf_op jit(solution)/shard_map/while/body/eval_jaxpr/while/body/eval_jaxpr/qhd,khd->hqk/dot_general | solution.py:113
  428.9 21.2 %multiply_convert_fusion.6 = bf16[12,512,1024]{2,1,0:T(8,128)(2,1)} fusion(f32[12,512,1024]{2,1,0:T(8,128)} %get-tuple-element.698, f32[12,512,1024]{2,1,0:T(8,128)} %fusion.141, f32[12,512]{1,0:T(8,128)S(1)} %get-tuple-element.699, f32[12,512]{1,0:T(8,128)S(1)} %dynamic-slice_bitcast_fusion.2, pred[512,1024]{1,0:T(8,128)(4,1)S(1)} %fusion.143), kind=kLoop, calls=%fused_computation.25.clone.1 | loop fusion | flops 37748736 | bytes 63488000 | tf_op jit(solution)/shard_map/while/body/eval_jaxpr/while/body/eval_jaxpr/convert_element_type | solution.py:117
  450.2 9.7 %multiply_bitcast_fusion.3 = f32[1,512,12,64]{1,3,2,0:T(8,128)} fusion(bf16[12,512,1024]{2,1,0:T(8,128)(2,1)} %multiply_convert_fusion.6, bf16[1024,12,64]{0,2,1:T(8,128)(2,1)S(1)} %get-tuple-element.781), kind=kOutput, calls=%fused_computation.35.clone.1 | convolution fusion | flops 805699584 | bytes 15728640 | tf_op jit(solution)/shard_map/while/body/eval_jaxpr/while/body/eval_jaxpr/hqk,khd->qhd/dot_general | solution.py:119
  459.8 9.9 %bitcast_add_fusion.6 = f32[1024,12,64]{0,2,1:T(8,128)} fusion(f32[1024,12,64]{0,2,1:T(8,128)} %get-tuple-element.757, bf16[12,512,1024]{2,1,0:T(8,128)(2,1)} %multiply_convert_fusion.6, pred[]{:T(512)S(6)} %compare.3, bf16[1024,12,64]{0,2,1:T(8,128)(2,1)} %get-tuple-element.778, s32[]{:T(128)S(6)} %select_n.72), kind=kOutput, calls=%fused_computation.32.clone.1 | convolution fusion | flops 807665664 | bytes 19660804 | tf_op jit(solution)/shard_map/while/body/eval_jaxpr/while/body/eval_jaxpr/hqk,qhd->khd/dot_general | solution.py:124
  471.3 28.7 %dynamic_update_slice.41 = f32[2,512,12,64]{1,0,3,2:T(2,128)} dynamic-update-slice(f32[2,512,12,64]{1,0,3,2:T(2,128)} %get-tuple-element.759, f32[1,512,12,64]{1,0,3,2:T(1,128)S(1)} %copy.136, s32[]{:T(128)S(6)} %copy.153, s32[]{:T(128)} %constant.129.clone.1..sunk.1, s32[]{:T(128)} %constant.129.clone.1..sunk.1, s32[]{:T(128)} %constant.129.clone.1..sunk.1) | dynamic-update-slice | bytes 3145732 | tf_op jit(solution)/shard_map/while/body/eval_jaxpr/while/body/jit(dynamic_update_index_in_dim)/dynamic_update_slice | solution.py:138
  516.8 6.0 convolution_convert_fusion.2
  523.5 9.8 %convolution_convert_fusion.1 = bf16[768,3072]{1,0:T(8,128)(2,1)} fusion(bf16[1024,3072]{1,0:T(8,128)(2,1)} %copy-done.55, f32[1024,768]{0,1:T(8,128)} %copy-done.8, f32[768]{0:T(1024)S(1)} %copy-done.46, f32[768]{0:T(1024)S(1)} %copy-done.41, f32[1024]{0:T(1024)S(1)} %copy-done.43, f32[1024]{0:T(1024)S(1)} %copy-done.39), kind=kOutput, calls=%fused_computation.68 | convolution fusion | flops 4838129664 | bytes 14170112 | tf_op jit(solution)/shard_map/td,tf->df/dot_general | solution.py:220
  534.7 10.9 %convolution_convert_fusion = bf16[3072,768]{1,0:T(8,128)(2,1)} fusion(bf16[1024,3072]{1,0:T(8,128)(2,1)} %get-tuple-element.552, bf16[1024,768]{0,1:T(8,128)(2,1)S(1)} %copy-done.17, f32[]{:T(128)} %bitcast.4), kind=kOutput, calls=%fused_computation.67 | convolution fusion | flops 4836556800 | bytes 12582916 | tf_op jit(solution)/shard_map/tf,td->fd/dot_general | solution.py:215
  549.2 5.3 multiply_reduce_fusion.1
  554.5 6.9 broadcast_multiply_fusion
  561.4 5.6 fusion.86
  576.2 38.4 %psum.49 = f32[5]{0:T(128)} all-reduce(f32[5]{0:T(128)S(1)} %pad_maximum_fusion.7), channel_id=1, replica_groups=mesh['rep'=2,'shard'=16] {'rep','shard'}, use_global_device_ids=true, to_apply=%region_16.17 | all-reduce | flops 5 | bytes 40 | tf_op jit(solution)/shard_map/psum | solution.py:206
  616.2 51.8 %reduce-scatter.15.cloned.1.call-done = bf16[48,3072]{1,0:T(8,128)(2,1)} async-done(((bf16[768,3072]{1,0:T(8,128)(2,1)}), bf16[48,3072]{1,0:T(8,128)(2,1)}) %reduce-scatter.15.cloned.1.call-update) | async-done | bytes 294928 | tf_op jit(solution)/shard_map/reduce_scatter | solution.py:259
  667.9 78.5 %reduce-scatter.17.cloned.1.call-done = bf16[192,768]{1,0:T(8,128)(2,1)} async-done(((bf16[3072,768]{1,0:T(8,128)(2,1)}), bf16[192,768]{1,0:T(8,128)(2,1)}) %reduce-scatter.17.cloned.1.call-update) | async-done | bytes 294928 | tf_op jit(solution)/shard_map/reduce_scatter | solution.py:262
  746.5 5.4 fusion.56
  755.5 47.6 %reduce-scatter.21.cloned.1.call-done = bf16[48,2]{1,0:T(8,128)(2,1)} async-done(((bf16[768,2]{1,0:T(8,128)(2,1)}), bf16[48,2]{1,0:T(8,128)(2,1)}) %reduce-scatter.21.cloned.1.call-update) | async-done | bytes 208
  803.9 55.5 %reduce-scatter.19.cloned.1.call-done = bf16[48,2]{1,0:T(8,128)(2,1)} async-done(((bf16[768,2]{1,0:T(8,128)(2,1)}), bf16[48,2]{1,0:T(8,128)(2,1)}) %reduce-scatter.19.cloned.1.call-update) | async-done | bytes 208
  860.2 4.9 all-reduce
  866.2 31.3 %all-reduce.4.cloned.1.call-done = (bf16[48,2304]{1,0:T(8,128)(2,1)}, bf16[48,768]{1,0:T(8,128)(2,1)}, bf16[48,3072]{1,0:T(8,128)(2,1)}, bf16[192,768]{1,0:T(8,128)(2,1)}) async-done(((bf16[48,2304]{1,0:T(8,128)(2,1)}, bf16[48,768]{1,0:T(8,128)(2,1)}, bf16[48,3072]{1,0:T(8,128)(2,1)}, bf16[192,768]{1,0:T(8,128)(2,1)}), (bf16[48,2304]{1,0:T(8,128)(2,1)}, bf16[48,768]{1,0:T(8,128)(2,1)}, ...) | async-done | bytes 884752 | tf_op jit(solution)/shard_map/psum | solution.py:273
  (245 shorter events, 108.6 us)
Async XLA Ops:
  7.2 70.6 %all-gather.7.cloned.1.call-start = ((), (), s32[]{:S(2)}) async-start(), calls=%async_computation.6 | async-start | bytes 3760128 | tf_op jit(solution)/shard_map/all_gather | solution.py:164
  7.9 183.2 %all-gather.9.cloned.1.call-start = ((), (), s32[]{:S(2)}) async-start(), calls=%async_computation.7 | async-start | bytes 1253376 | tf_op jit(solution)/shard_map/all_gather | solution.py:165
  8.7 187.8 %all-gather.11.cloned.1.call-start = ((), (), s32[]{:S(2)}) async-start(), calls=%async_computation.8 | async-start | bytes 5013504 | tf_op jit(solution)/shard_map/all_gather | solution.py:166
  9.4 200.7 %all-gather.13.cloned.1.call-start = ((), (), s32[]{:S(2)}) async-start(), calls=%async_computation.9 | async-start | bytes 5013504 | tf_op jit(solution)/shard_map/all_gather | solution.py:167
  10.0 606.2 %reduce-scatter.13.cloned.1.call-start = ((), (), s32[]{:S(2)}) async-start(), calls=%async_computation.11 | async-start | bytes 1253376 | tf_op jit(solution)/shard_map/reduce_scatter | solution.py:256
  55.0 46.0 %copy-start.18 = (f32[1024,64]{0,1:T(8,128)}, f32[1024,64]{0,1:T(8,128)S(1)}, u32[]{:S(2)}) copy-start(f32[1024,64]{0,1:T(8,128)S(1)} %get-tuple-element.546) | copy-start | bytes 786436
  55.0 2.6 copy-start.14
  56.9 20.9 %copy-start.2 = (bf16[1024,768]{0,1:T(8,128)(2,1)}, bf16[1024,768]{0,1:T(8,128)(2,1)S(1)}, u32[]{:S(2)}) copy-start(bf16[1024,768]{0,1:T(8,128)(2,1)S(1)} %copy.80) | copy-start | bytes 4718596
  56.9 2.4 copy-start.50
  57.2 20.7 %copy-start.32 = (f32[1024]{0:T(1024)}, f32[1024]{0:T(1024)S(1)}, u32[]{:S(2)}) copy-start(f32[1024]{0:T(1024)S(1)} %broadcast_multiply_fusion.7) | copy-start | bytes 12292
  57.6 20.2 %copy-start.36 = (f32[1024]{0:T(1024)}, f32[1024]{0:T(1024)S(1)}, u32[]{:S(2)}) copy-start(f32[1024]{0:T(1024)S(1)} %add_rsqrt_fusion.1) | copy-start | bytes 12292
  77.8 6.3 copy-start.34
  77.8 6.3 copy-start.47
  91.2 9.5 %copy-start.5 = (f32[1024,768]{0,1:T(8,128)}, f32[1024,768]{0,1:T(8,128)S(1)}, u32[]{:S(2)}) copy-start(f32[1024,768]{0,1:T(8,128)S(1)} %copy.85) | copy-start | bytes 9437188
  102.6 4.3 copy-start.24
  186.4 4.7 copy-start.3
  194.5 43.9 %copy-start.38 = (f32[1024]{0:T(1024)}, f32[1024]{0:T(1024)S(1)}, u32[]{:S(2)}) copy-start(f32[1024]{0:T(1024)S(1)} %broadcast_multiply_fusion.6) | copy-start | bytes 12292
  196.5 41.9 %copy-start.42 = (f32[1024]{0:T(1024)}, f32[1024]{0:T(1024)S(1)}, u32[]{:S(2)}) copy-start(f32[1024]{0:T(1024)S(1)} %add_rsqrt_fusion) | copy-start | bytes 12292
  196.5 13.6 %copy-start.16 = (bf16[1024,768]{0,1:T(8,128)(2,1)S(1)}, bf16[1024,768]{0,1:T(8,128)(2,1)}, u32[]{:S(2)}) copy-start(bf16[1024,768]{0,1:T(8,128)(2,1)} %copy.90) | copy-start | bytes 4718596
  210.1 12.8 %copy-start.52 = (bf16[768,3072]{1,0:T(8,128)(2,1)S(1)}, bf16[768,3072]{1,0:T(8,128)(2,1)}, u32[]{:S(2)}) copy-start(bf16[768,3072]{1,0:T(8,128)(2,1)} %all-gather.11.cloned.1.call-done) | copy-start | bytes 14155780
  222.9 7.3 copy-start.55
  233.8 4.6 copy-start.9
  233.8 4.7 copy-start.10
  252.7 4.0 copy-start.54
  256.6 359.5 %reduce-scatter.11.cloned.1.call-start = ((), (), s32[]{:S(2)}) async-start(), calls=%async_computation.10 | async-start | bytes 3760128 | tf_op jit(solution)/shard_map/reduce_scatter | solution.py:253
  266.6 11.6 %copy-start.13 = (bf16[1024,12,64]{0,2,1:T(8,128)(2,1)S(1)}, bf16[1024,12,64]{0,2,1:T(8,128)(2,1)}, u32[]{:S(2)}) copy-start(bf16[1024,12,64]{0,2,1:T(8,128)(2,1)} %get-tuple-element.783) | copy-start | bytes 4718596 | tf_op jit(solution)/shard_map/while/body/eval_jaxpr/while
  340.8 9.0 copy-start.1
  385.1 11.5 %copy-start.13 = (bf16[1024,12,64]{0,2,1:T(8,128)(2,1)S(1)}, bf16[1024,12,64]{0,2,1:T(8,128)(2,1)}, u32[]{:S(2)}) copy-start(bf16[1024,12,64]{0,2,1:T(8,128)(2,1)} %get-tuple-element.783) | copy-start | bytes 4718596 | tf_op jit(solution)/shard_map/while/body/eval_jaxpr/while
  459.8 9.9 %copy-start.1 = (f32[1,512,12,64]{1,3,2,0:T(8,128)S(1)}, f32[1,512,12,64]{1,3,2,0:T(8,128)}, u32[]{:S(2)}) copy-start(f32[1,512,12,64]{1,3,2,0:T(8,128)} %multiply_bitcast_fusion.3) | copy-start | bytes 4718596 | tf_op jit(solution)/shard_map/while/body/eval_jaxpr/while
  500.2 3.5 copy-start.7
  514.4 2.4 copy-start.26
  514.4 2.4 copy-start.33
  514.4 2.4 copy-start.35
  522.8 145.1 %reduce-scatter.15.cloned.1.call-start = ((), (), s32[]{:S(2)}) async-start(), calls=%async_computation.12 | async-start | bytes 5013504 | tf_op jit(solution)/shard_map/reduce_scatter | solution.py:259
  533.3 213.2 %reduce-scatter.17.cloned.1.call-start = ((), (), s32[]{:S(2)}) async-start(), calls=%async_computation.13 | async-start | bytes 5013504 | tf_op jit(solution)/shard_map/reduce_scatter | solution.py:262
  545.7 3.2 copy-start.15
  545.7 257.4 %reduce-scatter.21.cloned.1.call-start = ((), (), s32[]{:S(2)}) async-start(), calls=%async_computation.15 | async-start | bytes 208896
  549.2 5.3 copy-start.12
  549.2 5.3 copy-start.51
  554.5 6.9 copy-start.49
  554.5 6.9 copy-start.44
  554.5 6.9 copy-start.27
  554.5 6.9 copy-start.29
  554.5 6.9 copy-start.31
  554.5 6.9 copy-start.53
  571.4 43.2 %copy-start.23 = (bf16[1024,768]{0,1:T(8,128)(2,1)S(1)}, bf16[1024,768]{0,1:T(8,128)(2,1)}, u32[]{:S(2)}) copy-start(bf16[1024,768]{0,1:T(8,128)(2,1)} %get-tuple-element.534) | copy-start | bytes 4718596
  574.5 284.9 %reduce-scatter.19.cloned.1.call-start = ((), (), s32[]{:S(2)}) async-start(), calls=%async_computation.14 | async-start | bytes 208896
  576.2 321.4 %all-reduce.4.cloned.1.call-start = ((), (), s32[]{:S(2)}) async-start(), calls=%async_computation.16 | async-start | bytes 1769472 | tf_op jit(solution)/shard_map/psum | solution.py:273
  (21 other events, 32.7 us)
Sparse Core Ops, SparseCore 0:
  10.3 49.9 all-gather.6
  62.5 36.9 all-gather.8
  101.7 51.9 all-gather.10
  155.9 51.6 all-gather.12
  256.8 56.7 reduce-scatter.12
  522.9 66.7 reduce-scatter.10
  593.5 74.3 reduce-scatter.14
  671.8 74.6 reduce-scatter.16
  750.6 52.4 reduce-scatter.20
  807.0 52.3 reduce-scatter.18
  861.9 35.5 all-reduce.3
where the time goes:
time: 926 us; the launch traced here: 911 us
  matrix products  279 us (30%)
  waiting for transfers between devices  267 us (29%)
  local copies, waits for them, and re-layouts  133 us (14%)
  other arithmetic  125 us (13%)
  blocking collectives  84.4 us (9%)
  between operations  15.7 us (2%)
    unnamed x13, waiting for transfers between devices  106 us
    reduce_scatter x1, waiting for transfers between devices, local(): lax.psum_scatter(local_grads[3].astype(jnp.bfloat16), 'shard', scatter_di...  78.5 us
    dynamic_update_slice x4, local copies, waits for them, and re-layouts, attend_backward(): lax.scan(one_block, (zero_rows, zero_rows), jnp.arange(block_count, dtype...  60.6 us
    reduce_scatter x1, waiting for transfers between devices, local(): lax.psum_scatter(local_grads[2].astype(jnp.bfloat16), 'shard', scatter_di...  51.8 us
    dot_general x4, matrix products, block_scores(): jnp.einsum('qhd,khd->hqk', query_block, key_rows, preferred_element_type=...  47.1 us
    convert_element_type x2, other arithmetic, one_block(): grad_scores = (attn_probs * (grad_probs - delta_sum)).astype(jnp.bfloat16)  42.5 us
    psum x1, blocking collectives, local(): grad_mix = lax.psum(partial_mix, ('rep', 'shard'))  38.4 us
    dot_general x2, matrix products, one_block(): jnp.einsum('qhd,khd->hqk', grad_block, value_rows, preferred_element_type...  36.3 us
  transfers between devices with their start and end apart: 11, of which 5 were waited for; matrix products, arithmetic and copies ran while one was open for 52% of the time, Pallas kernels for 0%

commit v1 on v0

v1 whole, which is shorter than its diff:
```python
import functools
import jax
import jax.numpy as jnp
import numpy as np
from jax import lax
from jax.experimental import pallas as pl
from jax.experimental.pallas import tpu as pltpu
from jax.sharding import PartitionSpec as P

BF = jnp.bfloat16
F32 = jnp.float32
HEADS = 12
SPAN = 256
BL = 256
NEG = -1e30
EPS = 1e-05
FB = 256


def dot(a, b):
    return lax.dot_general(a, b, (((1,), (0,)), ((), ())), preferred_element_type=F32)


def dot_bt(a, b):
    return lax.dot_general(a, b, (((1,), (1,)), ((), ())), preferred_element_type=F32)


def dot_at(a, b):
    return lax.dot_general(a, b, (((0,), (0,)), ((), ())), preferred_element_type=F32)


def iota(shape, axis):
    return lax.broadcasted_iota(jnp.int32, shape, axis)


def cols(start, width=128):
    return pl.ds(pl.multiple_of(start, 128), width)


def rows(start, height):
    return pl.ds(pl.multiple_of(start, height), height)


def norm_parts(values):
    average = jnp.mean(values, axis=-1, keepdims=True)
    centered = values - average
    inverse_std = lax.rsqrt(jnp.mean(centered * centered, axis=-1, keepdims=True) + EPS)
    return centered * inverse_std, inverse_std


def norm_back(incoming, normed, inverse_std, gain_row):
    scaled = incoming * gain_row
    inner = (
        scaled
        - jnp.mean(scaled, axis=-1, keepdims=True)
        - normed * jnp.mean(scaled * normed, axis=-1, keepdims=True)
    )
    return inverse_std * inner


def fold8(values):
    return jnp.sum(values.reshape(values.shape[0] // 8, 8, values.shape[1]), axis=0)


def turn(values, low_quarter):
    return jnp.where(low_quarter, pltpu.roll(values, 96, 1), pltpu.roll(values, 32, 1))


def gelu_parts(upper):
    size = jnp.abs(upper)
    t = 1.0 / (1.0 + 0.2316419 * size)
    density = jnp.exp(-0.5 * upper * upper) * 0.3989422804014327
    poly = ((((1.330274429 * t - 1.821255978) * t + 1.781477937) * t - 0.356563782) * t + 0.319381530) * t
    tail = density * poly
    cdf = jnp.where(upper >= 0, 1.0 - tail, tail)
    return upper * cdf, cdf + upper * density


def split3(values):
    high = values.astype(BF)
    rest = values - high.astype(F32)
    mid = rest.astype(BF)
    return high, mid, (rest - mid.astype(F32)).astype(BF)


def block_bias(start, query0, key0, causal, transposed):
    query = query0 + iota((BL, BL), 1 if transposed else 0)
    key = key0 + iota((BL, BL), 0 if transposed else 1)
    inside = (query >= start) & (query < start + SPAN) & (key >= start) & (key < start + SPAN)
    seen = (inside | (key <= query)) if causal else inside
    return jnp.where(seen, 0.0, NEG).astype(F32)


def fill_bias(start, bias_ref, blocks, transposed):
    span_block = start // BL
    for i in range(blocks):
        bias_ref[i] = block_bias(start, i * BL, i * BL, True, transposed)
    extra = block_bias(start, span_block * BL, (span_block + 1) * BL, False, transposed)
    bias_ref[blocks] = jnp.where(span_block + 1 < blocks, extra, NEG)


def attend_forward(start, qkv_ref, bias_ref, out_ref, lse_ref):
    length, width = out_ref.shape
    blocks = length // BL
    fill_bias(start, bias_ref, blocks, False)
    span_block = start // BL
    next_block = jnp.minimum(span_block + 1, blocks - 1)
    first = iota((BL, 128), 1) < 64
    first_all = iota((length, 128), 1) < 64
    zero = jnp.zeros((), BF)
    one = jnp.ones((), BF)

    def pair(h, carry):
        qc, kc, vc = cols(h * 128), cols(width + h * 128), cols(2 * width + h * 128)
        keys = qkv_ref[:, kc]
        values = qkv_ref[:, vc]
        with_ones = (jnp.where(first_all, values, one), jnp.where(first_all, one, values))
        qx = qkv_ref[rows(span_block * BL, BL), qc]
        kx = qkv_ref[rows(next_block * BL, BL), kc]
        vx = qkv_ref[rows(next_block * BL, BL), vc]
        extra = []
        for head in (0, 1):
            mine = first if head == 0 else ~first
            s = dot_bt(jnp.where(mine, qx, zero), kx) + bias_ref[blocks]
            peak = jnp.max(s, axis=1, keepdims=True)
            extra.append((peak, dot(jnp.exp(s - peak).astype(BF), jnp.where(mine, vx, one))))
        for i in range(blocks):
            outs, peaks = [], []
            here = span_block == i
            qi = qkv_ref[pl.ds(i * BL, BL), qc]
            for head in (0, 1):
                mine = first if head == 0 else ~first
                qm = jnp.where(mine, qi, zero)
                extra_peak, extra_out = extra[head]
                diag = dot_bt(qm, keys[i * BL : (i + 1) * BL]) + bias_ref[i]
                peak = jnp.max(diag, axis=1, keepdims=True)
                if i > 0:
                    left = dot_bt(qm, keys[: i * BL])
                    peak = jnp.maximum(peak, jnp.max(left, axis=1, keepdims=True))
                if i < blocks - 1:
                    peak = jnp.maximum(peak, jnp.where(here, extra_peak, NEG))
                out = dot(jnp.exp(diag - peak).astype(BF), with_ones[head][i * BL : (i + 1) * BL])
                if i > 0:
                    out = out + dot(jnp.exp(left - peak).astype(BF), with_ones[head][: i * BL])
                if i < blocks - 1:
                    out = out + jnp.where(here, jnp.exp(extra_peak - peak), 0.0) * extra_out
                outs.append(out)
                peaks.append(peak)
            top = jnp.where(first, outs[0], outs[1])
            total = pltpu.roll(jnp.where(first, outs[1], outs[0]), 64, 1)
            out_ref[pl.ds(i * BL, BL), qc] = (top / total).astype(BF)
            lse_ref[pl.ds(i * BL, BL), qc] = jnp.where(first, peaks[0], peaks[1]) + jnp.log(total)
        return carry

    lax.fori_loop(0, width // 128, pair, 0)


def attend_backward(start, qkv_ref, do_ref, out_ref, lse_ref, cos_ref, sin_ref, bias_ref, dq_ref):
    length, width = out_ref.shape
    blocks = length // BL
    fill_bias(start, bias_ref, blocks, True)
    span_block = start // BL
    next_block = jnp.minimum(span_block + 1, blocks - 1)
    lane_all = iota((length, 128), 1)
    lane = iota((BL, 128), 1)
    first = lane < 64
    low_quarter = (lane % 64) < 32
    zero = jnp.zeros((), BF)
    one = jnp.ones((), BF)

    def extend(values, column, head, lanes):
        a, b, c = split3(-column)
        base = 64 * (1 - head)
        parts = jnp.where(
            lanes == base, a, jnp.where(lanes == base + 1, b, jnp.where(lanes == base + 2, c, zero))
        )
        return jnp.where(lanes < 64, values, parts) if head == 0 else jnp.where(lanes < 64, parts, values)

    def keep(values, head, lanes, other):
        return jnp.where(lanes < 64, values, other) if head == 0 else jnp.where(lanes < 64, other, values)

    def rotate_back(values, cosine, sine):
        return values * cosine - turn(values, low_quarter) * sine

    def pair(h, carry):
        qc, kc, vc = cols(h * 128), cols(width + h * 128), cols(2 * width + h * 128)

        def query_side(at, lanes):
            q = qkv_ref[at, qc]
            do = do_ref[at, qc]
            lse = lse_ref[at, qc]
            product = do.astype(F32) * out_ref[at, qc].astype(F32)
            sides = []
            for head in (0, 1):
                mine = (lanes < 64) if head == 0 else (lanes >= 64)
                delta = jnp.sum(jnp.where(mine, product, 0.0), axis=1, keepdims=True)
                sides.append(
                    (
                        extend(q, lse[:, 64 * head : 64 * head + 1], head, lanes),
                        keep(q, head, lanes, zero),
                        extend(do, delta, head, lanes),
                        keep(do, head, lanes, zero),
                    )
                )
            return sides

        everything = query_side(slice(None), lane_all)
        extra_side = query_side(rows(span_block * BL, BL), lane)
        kx = qkv_ref[rows(next_block * BL, BL), kc]
        vx = qkv_ref[rows(next_block * BL, BL), vc]

        def block(k, v, head, qa, qm, da, dm, bias):
            s = dot_bt(keep(k, head, lane, one), qa)
            if bias is not None:
                s = s + bias
            p = jnp.exp(s)
            ds = (p * dot_bt(keep(v, head, lane, one), da)).astype(BF)
            return dot(p.astype(BF), dm), dot(ds, qm), dot_at(ds, keep(k, head, lane, zero))

        parts = [block(kx, vx, head, *extra_side[head], bias_ref[blocks]) for head in (0, 1)]
        dvx, dkx, dqx = [a + b for a, b in zip(*parts)]
        for j in range(blocks):
            at = slice(j * BL, (j + 1) * BL)
            rest = slice((j + 1) * BL, length)
            kj = qkv_ref[at, kc]
            vj = qkv_ref[at, vc]
            dv = jnp.where(span_block + 1 == j, dvx, 0.0) if j > 0 else None
            dk = jnp.where(span_block + 1 == j, dkx, 0.0) if j > 0 else None
            dq = jnp.where(span_block == j, dqx, 0.0) if j < blocks - 1 else None
            dq_rest = None
            add = lambda old, new: new if old is None else old + new
            for head in (0, 1):
                side = everything[head]
                a, b, c = block(kj, vj, head, *[item[at] for item in side], bias_ref[j])
                dv, dk, dq = add(dv, a), add(dk, b), add(dq, c)
                if j < blocks - 1:
                    a, b, c = block(kj, vj, head, *[item[rest] for item in side], None)
                    dv, dk, dq_rest = add(dv, a), add(dk, b), add(dq_rest, c)
            cosine, sine = cos_ref[at], sin_ref[at]
            if j > 0:
                dq = dq + dq_ref[at]
            qkv_ref[at, vc] = dv.astype(BF)
            qkv_ref[at, kc] = rotate_back(dk, cosine, sine).astype(BF)
            qkv_ref[at, qc] = rotate_back(dq * 0.125, cosine, sine).astype(BF)
            if j < blocks - 1:
                dq_ref[rest] = dq_rest if j == 0 else dq_ref[rest] + dq_rest
        return carry

    lax.fori_loop(0, width // 128, pair, 0)


def first_norm(x_ref, par_ref, act_ref):
    height = 128

    def chunk(r, carry):
        at = rows(r * height, height)
        normed, _ = norm_parts(x_ref[at, :].astype(F32))
        act_ref[at, :] = (normed * par_ref[0:1, :] + par_ref[2:3, :]).astype(BF)
        return carry

    lax.fori_loop(0, x_ref.shape[0] // height, chunk, 0)


def project(act_ref, wq_ref, cos_ref, sin_ref, qkv_ref):
    width = act_ref.shape[1]
    low_quarter = (iota((act_ref.shape[0], 128), 1) % 64) < 32

    def rotated(c, carry):
        out = dot(act_ref[...], wq_ref[:, cols(c * 256, 256)])
        scale = jnp.where(c < width // 256, 0.125, 1.0)
        for half in (0, 1):
            u = out[:, half * 128 : half * 128 + 128]
            u = (u * cos_ref[...] + turn(u, low_quarter) * sin_ref[...]) * scale
            qkv_ref[:, cols(c * 256 + half * 128)] = u.astype(BF)
        return carry

    def plain(c, carry):
        at = cols(2 * width + c * 256, 256)
        qkv_ref[:, at] = dot(act_ref[...], wq_ref[:, at]).astype(BF)
        return carry

    lax.fori_loop(0, 2 * width // 256, rotated, 0)
    lax.fori_loop(0, width // 256, plain, 0)


def attention_out(x_ref, mixed_ref, wo_ref, par_ref, middle_ref, act_ref, actt_ref):
    height = 256

    def chunk(r, carry):
        at = rows(r * height, height)
        middle = x_ref[at, :].astype(F32) + dot(mixed_ref[at, :], wo_ref[...])
        middle_ref[at, :] = middle
        normed, _ = norm_parts(middle)
        act = (normed * par_ref[1:2, :] + par_ref[3:4, :]).astype(BF)
        act_ref[at, :] = act
        actt_ref[:, rows(r * height, height)] = act.T
        return carry

    lax.fori_loop(0, x_ref.shape[0] // height, chunk, 0)


def feed_forward(act_ref, actt_ref, gb_ref, wu_ref, wd_ref, out_ref, dact_ref):
    out_ref[...] = jnp.zeros_like(out_ref)
    dact_ref[...] = jnp.zeros_like(dact_ref)
    feed_forward_blocks(0, wd_ref.shape[0] // FB, act_ref, actt_ref, gb_ref, wu_ref, wd_ref, out_ref, dact_ref)


def feed_forward_blocks(low, high, act_ref, actt_ref, gb_ref, wu_ref, wd_ref, out_ref, dact_ref):
    def block(b, carry):
        c = cols(b * FB, FB)
        r = rows(b * FB, FB)
        wu = wu_ref[:, c]
        wd = wd_ref[r, :]
        hidden, slope = gelu_parts(dot(act_ref[...], wu))
        hidden = hidden.astype(BF)
        out_ref[...] += dot(hidden, wd)
        gu = (dot_bt(gb_ref[...], wd) * slope).astype(BF)
        dact_ref[...] += dot_bt(gu, wu)
        wd_ref[r, :] = dot_at(hidden, gb_ref[...]).astype(BF)
        wu_ref[:, c] = dot(actt_ref[...], gu).astype(BF)
        return carry

    lax.fori_loop(low, high, block, 0)


def branch_grad(mix4, g_ref, gb_ref):
    height = 256

    def chunk(r, carry):
        at = rows(r * height, height)
        gb_ref[at, :] = (mix4 * g_ref[at, :].astype(F32)).astype(BF)
        return carry

    lax.fori_loop(0, g_ref.shape[0] // height, chunk, 0)


def middle_back(mix4, g_ref, earlier_ref, middle_ref, out_ref, dact_ref, mixed_ref, wo_ref, par_ref,
                next_ref, ga_ref, do_ref, go_ref, small_ref):
    height = 256
    width = g_ref.shape[1]
    zero = jnp.zeros((8, width), F32)

    def chunk(r, carry):
        gain, bias, terms = carry
        at = rows(r * height, height)
        g = g_ref[at, :].astype(F32)
        middle = middle_ref[at, :]
        output = middle + out_ref[at, :]
        next_ref[at, :] = (earlier_ref[at, :].astype(F32) + mix4 * output).astype(BF)
        terms = terms + fold8(g * output)
        normed, inverse = norm_parts(middle)
        dact = dact_ref[at, :]
        gain = gain + fold8(dact * normed)
        bias = bias + fold8(dact)
        grad = mix4 * g + norm_back(dact, normed, inverse, par_ref[1:2, :])
        dact_ref[at, :] = grad
        low = grad.astype(BF)
        ga_ref[at, :] = low
        do_ref[at, :] = dot_bt(low, wo_ref[...]).astype(BF)
        return gain, bias, terms

    gain, bias, terms = lax.fori_loop(0, g_ref.shape[0] // height, chunk, (zero, zero, zero))
    small_ref[1:2, :] = jnp.sum(gain, axis=0, keepdims=True)
    small_ref[3:4, :] = jnp.sum(bias, axis=0, keepdims=True)
    small_ref[4:5, :] = jnp.sum(terms, axis=0, keepdims=True)
    go_ref[...] = dot_at(mixed_ref[...], ga_ref[...]).astype(BF)


def project_grad(act_ref, actt_ref, qkv_ref, gq_ref):
    actt_ref[...] = act_ref[...].T

    def block(c, carry):
        at = cols(c * 256, 256)
        gq_ref[:, at] = dot(actt_ref[...], qkv_ref[:, at]).astype(BF)
        return carry

    lax.fori_loop(0, qkv_ref.shape[1] // 256, block, 0)


def first_back(x_ref, qkv_ref, wq_ref, par_ref, dmid_ref, small_ref):
    height = 256
    zero = jnp.zeros((8, x_ref.shape[1]), F32)

    def chunk(r, carry):
        gain, bias = carry
        at = rows(r * height, height)
        dact = dot_bt(qkv_ref[at, :], wq_ref[...])
        normed, inverse = norm_parts(x_ref[at, :].astype(F32))
        gain = gain + fold8(dact * normed)
        bias = bias + fold8(dact)
        dmid_ref[at, :] += norm_back(dact, normed, inverse, par_ref[0:1, :])
        return gain, bias

    gain, bias = lax.fori_loop(0, x_ref.shape[0] // height, chunk, (zero, zero))
    small_ref[0:1, :] = jnp.sum(gain, axis=0, keepdims=True)
    small_ref[2:3, :] = jnp.sum(bias, axis=0, keepdims=True)


def block_kernel(start_ref, mix_ref, x_hbm, g_hbm, earlier_hbm, par_ref, cos_ref, sin_ref, wq_hbm, wo_hbm, wu_hbm, wd_hbm,
                 next_hbm, dx_hbm, gq_hbm, go_hbm, gu_hbm, gd_hbm, small_ref,
                 x, g, gb, act1, act2, actt, mixed, earlier, qkv, lse, middle, out, dact, wq, wo, wu, wd, gq, go, bias, dq, sems):
    loads = [
        pltpu.make_async_copy(a, b, sems.at[i])
        for i, (a, b) in enumerate(
            [(x_hbm, x), (wq_hbm, wq), (g_hbm, g), (earlier_hbm, earlier), (wo_hbm, wo), (wu_hbm, wu), (wd_hbm, wd)]
        )
    ]
    for copy in loads:
        copy.start()
    small_ref[...] = jnp.zeros_like(small_ref)
    start = start_ref[0]
    mix4 = mix_ref[4]
    loads[0].wait()
    first_norm(x, par_ref, act1)
    loads[1].wait()
    project(act1, wq, cos_ref, sin_ref, qkv)
    attend_forward(start, qkv, bias, mixed, lse)
    for copy in loads[2:]:
        copy.wait()
    branch_grad(mix4, g, gb)
    attention_out(x, mixed, wo, par_ref, middle, act2, actt)
    feed_forward(act2, actt, gb, wu, wd, out, dact)
    ga, do, nxt = gb, act2, earlier
    middle_back(mix4, g, earlier, middle, out, dact, mixed, wo, par_ref, nxt, ga, do, go, small_ref)
    stores = [
        pltpu.make_async_copy(a, b, sems.at[i])
        for i, (a, b) in enumerate(
            [(nxt, next_hbm), (wu, gu_hbm), (wd, gd_hbm), (go, go_hbm), (gq, gq_hbm), (dact, dx_hbm)]
        )
    ]
    for copy in stores[:4]:
        copy.start()
    attend_backward(start, qkv, do, mixed, lse, cos_ref, sin_ref, bias, dq)
    project_grad(act1, actt, qkv, gq)
    stores[4].start()
    first_back(x, qkv, wq, par_ref, dact, small_ref)
    stores[5].start()
    for copy in stores:
        copy.wait()


def rotary_tables(length):
    freq = np.exp(-np.log(10000.0) * np.arange(32) / 32.0)
    angles = np.arange(length)[:, None] * freq[None, :]
    c, s = np.cos(angles), np.sin(angles)
    return (
        jnp.asarray(np.concatenate([c, c, c, c], axis=1), F32),
        jnp.asarray(np.concatenate([-s, s, -s, s], axis=1), F32),
    )


def history_kernel(mix_ref, history_ref, g_ref, grad_ref, earlier_ref, terms_ref):
    g = g_ref[...].astype(F32)
    earlier = None
    parts = []
    for k in range(history_ref.shape[0]):
        h = history_ref[k].astype(F32)
        grad_ref[k] = mix_ref[k] * g
        term = mix_ref[k] * h
        earlier = term if earlier is None else earlier + term
        parts.append(jnp.sum(fold8(h * g), axis=0, keepdims=True))
    earlier_ref[...] = earlier.astype(BF)
    new = jnp.concatenate(parts + [jnp.zeros((8 - len(parts), g.shape[1]), F32)], axis=0)

    @pl.when(pl.program_id(0) == 0)
    def _():
        terms_ref[...] = new

    @pl.when(pl.program_id(0) > 0)
    def _():
        terms_ref[...] += new


def history_pass(mix, history, g):
    past, length, width = history.shape
    height = 128
    return pl.pallas_call(
        history_kernel,
        grid=(length // height,),
        in_specs=[
            pl.BlockSpec(memory_space=pltpu.SMEM),
            pl.BlockSpec((past, height, width), lambda i: (0, i, 0)),
            pl.BlockSpec((height, width), lambda i: (i, 0)),
        ],
        out_specs=(
            pl.BlockSpec((past, height, width), lambda i: (0, i, 0)),
            pl.BlockSpec((height, width), lambda i: (i, 0)),
            pl.BlockSpec((8, width), lambda i: (0, 0)),
        ),
        out_shape=(
            jax.ShapeDtypeStruct((past, length, width), F32),
            jax.ShapeDtypeStruct((length, width), BF),
            jax.ShapeDtypeStruct((8, width), F32),
        ),
        name="history_pass",
    )(mix, history, g)


VMEM_LIMIT = 67043328


def block_pass(start, mix, x, g, earlier, par, wq, wo, wu, wd):
    length, width = x.shape
    ff = wd.shape[0]
    cosine, sine = rotary_tables(length)
    smem = pl.BlockSpec(memory_space=pltpu.SMEM)
    vmem = pl.BlockSpec(memory_space=pltpu.VMEM)
    anys = pl.BlockSpec(memory_space=pl.ANY)
    low = pltpu.VMEM((length, width), BF)
    full = pltpu.VMEM((length, width), F32)
    return pl.pallas_call(
        block_kernel,
        in_specs=[smem, smem, anys, anys, anys, vmem, vmem, vmem, anys, anys, anys, anys],
        out_specs=(anys,) * 6 + (vmem,),
        out_shape=(
            jax.ShapeDtypeStruct((length, width), BF),
            jax.ShapeDtypeStruct((length, width), F32),
            jax.ShapeDtypeStruct((width, 3 * width), BF),
            jax.ShapeDtypeStruct((width, width), BF),
            jax.ShapeDtypeStruct((width, ff), BF),
            jax.ShapeDtypeStruct((ff, width), BF),
            jax.ShapeDtypeStruct((8, width), F32),
        ),
        scratch_shapes=[low] * 5
        + [pltpu.VMEM((width, length), BF)]
        + [low] * 2
        + [pltpu.VMEM((length, 3 * width), BF)]
        + [full] * 4
        + [
            pltpu.VMEM((width, 3 * width), BF),
            pltpu.VMEM((width, width), BF),
            pltpu.VMEM((width, ff), BF),
            pltpu.VMEM((ff, width), BF),
            pltpu.VMEM((width, 3 * width), BF),
            pltpu.VMEM((width, width), BF),
            pltpu.VMEM((length // BL + 1, BL, BL), F32),
            pltpu.VMEM((length, 128), F32),
            pltpu.SemaphoreType.DMA((8,)),
        ],
        compiler_params=pltpu.CompilerParams(vmem_limit_bytes=VMEM_LIMIT),
        name="block_pass",
    )(start, mix, x, g, earlier, par, cosine, sine, wq, wo, wu, wd)


def local(block_input, history, cotangent, span_start, w_qkv, w_out, w_up, w_down, ln_gains, ln_biases, mix_weights):
    gather = lambda item, axis: lax.all_gather(item, "shard", axis=axis, tiled=True)
    norms = gather(jnp.concatenate([ln_gains, ln_biases]), 1).astype(F32)
    par = jnp.concatenate([norms, norms])
    grad_history, earlier, terms = history_pass(mix_weights, history, cotangent)
    nxt, grad_input, gq, go, gu, gd, small = block_pass(
        span_start, mix_weights, block_input, cotangent, earlier, par,
        gather(w_qkv, 0), gather(w_out, 0), gather(w_up, 0), gather(w_down, 0),
    )
    past = history.shape[0]
    partial_mix = jnp.concatenate([jnp.sum(terms[:past], axis=1), jnp.sum(small[4:5], axis=1)])
    grad_mix = lax.psum(partial_mix, ("rep", "shard"))

    def owned(item, axis):
        part = lax.psum_scatter(item.astype(BF), "shard", scatter_dimension=axis, tiled=True)
        return lax.psum(part, "rep").astype(F32)

    norm_grads = owned(small[:4], 1)
    return (
        nxt, grad_input, grad_history, grad_mix,
        owned(gq, 0), owned(go, 0), owned(gu, 0), owned(gd, 0),
        norm_grads[0:2], norm_grads[2], norm_grads[3],
    )


def solution(mesh):
    token = P(("rep", "shard"), None)
    kept = P("shard", None)
    past = P(None, ("rep", "shard"), None)
    norm = P(None, "shard")
    return jax.shard_map(
        local,
        mesh=mesh,
        in_specs=(token, past, token, P(("rep", "shard")), kept, kept, kept, kept, norm, norm, P()),
        out_specs=(token, token, past, P(), kept, kept, kept, kept, norm, P("shard"), P("shard")),
        check_vma=False,
    )
```

time: 926 us -> 749 us (0.81); the launches traced: 911 us -> 748 us
  matrix products: 279 us -> 0 us
  waiting for transfers between devices: 267 us -> 494 us
  Pallas kernels: 0 us -> 157 us
  local copies, waits for them, and re-layouts: 133 us -> 3.56 us
  other arithmetic: 125 us -> 10.4 us
  blocking collectives: 84.4 us -> 67.6 us
    dot_general x27 -> x0, matrix products: 279 us -> none  [the longest x4 47.1 us: block_scores(): jnp.einsum('qhd,khd->hqk', query_block, key_rows, preferred_element_type=...]
    all_gather x4, waiting for transfers between devices: 0.03 us -> 162 us  [local(): lax.all_gather(item, 'shard', axis=axis, tiled=True)]
    pallas_call x0 -> x2, Pallas kernels: none -> 157 us  [the longest x1 147 us: block_pass(): pl.pallas_call(block_kernel, in_specs=[smem, smem, anys, anys, anys, vmem...]
    reduce_scatter x4, waiting for transfers between devices: 130 us -> 281 us  [owned(): lax.psum_scatter(item.astype(BF), 'shard', scatter_dimension=axis, tiled=...]
    unnamed x13 -> x11, waiting for transfers between devices: 106 us -> 19.4 us
    dynamic_update_slice x4 -> x0, local copies, waits for them, and re-layouts: 60.6 us -> none  [attend_backward(): lax.scan(one_block, (zero_rows, zero_rows), jnp.arange(block_count, dtype...]
    convert_element_type x11 -> x5, other arithmetic: 54.3 us -> 6.91 us  [owned(): return lax.psum(part, 'rep').astype(F32)]
    reduce_sum x7 -> x2, other arithmetic: 33 us -> 1.47 us  [the longest x1 1.35 us: local(): jnp.sum(small[4:5], axis=1)]
  transfers between devices with their start and end apart: 11 -> 10, of which waited for: 5 -> 10; matrix products, arithmetic and copies ran while one was open for 52% -> 1% of each run, Pallas kernels for 0% -> 1%
where the time goes in v1:
time: 749 us; the launch traced here: 748 us
  waiting for transfers between devices  494 us (66%)
  Pallas kernels  157 us (21%)
  blocking collectives  67.6 us (9%)
  between operations  14.9 us (2%)
  other arithmetic  10.4 us (1%)
    reduce_scatter x4, waiting for transfers between devices, owned(): lax.psum_scatter(item.astype(BF), 'shard', scatter_dimension=axis, tiled=...  281 us
    all_gather x4, waiting for transfers between devices, local(): lax.all_gather(item, 'shard', axis=axis, tiled=True)  162 us
    pallas_call x1, Pallas kernels, block_pass(): pl.pallas_call(block_kernel, in_specs=[smem, smem, anys, anys, anys, vmem...  147 us
    psum x1, blocking collectives, local(): grad_mix = lax.psum(partial_mix, ('rep', 'shard'))  39.5 us
    psum x1, waiting for transfers between devices, owned(): return lax.psum(part, 'rep').astype(F32)  31.2 us
    all_gather x1, blocking collectives, local(): lax.all_gather(item, 'shard', axis=axis, tiled=True)  23.1 us
    unnamed x11, waiting for transfers between devices  19.4 us
  transfers between devices with their start and end apart: 10, of which 10 were waited for; matrix products, arithmetic and copies ran while one was open for 1% of the time, Pallas kernels for 1%

profile of v1, /device:TPU:0, one launch (start us, length us, event | category | flops | bytes accessed | tf_op | source)
XLA Modules:
  0.0 747.8 jit_solution(5256141311733433400)
XLA Ops:
  7.2 0.0 all-gather.8.cloned.1.call-start
  7.2 0.7 all-gather.8.cloned.1.call-update
  7.9 0.0 all-gather.6.cloned.1.call-start
  8.0 0.7 all-gather.6.cloned.1.call-update
  8.7 0.0 all-gather.10.cloned.1.call-start
  8.7 0.7 all-gather.10.cloned.1.call-update
  9.4 0.0 all-gather.12.cloned.1.call-start
  9.4 0.5 all-gather.12.cloned.1.call-update
  10.0 0.0 reduce-scatter.10.cloned.1.call-start
  10.7 0.7 maximum_bitcast_fusion
  11.3 23.1 %all-gather = bf16[16,48,4]{1,2,0:T(4,128)(2,1)S(1)} all-gather(bf16[1,48,4]{1,2,0:T(4,128)(2,1)S(1)} %maximum_bitcast_fusion), channel_id=1, replica_groups=mesh['rep'=2,'shard'=16] {'shard'}, dimensions={0}, use_global_device_ids=true | all-gather | bytes 6528 | tf_op jit(solution)/shard_map/all_gather | solution.py:546
  34.5 0.1 reshape.24
  34.6 10.4 %history_pass.1 = (f32[4,1024,768]{2,1,0:T(8,128)}, bf16[1024,768]{1,0:T(8,128)(2,1)}, f32[8,768]{1,0:T(8,128)}) custom-call(f32[5]{0:T(128)} %mix_ref.3, bf16[4,1024,768]{2,1,0:T(8,128)(2,1)} %history_ref.1, bf16[1024,768]{1,0:T(8,128)(2,1)} %g_hbm.1), custom_call_target="tpu_custom_call" | custom-call | tf_op jit(solution)/shard_map/history_pass/pallas_call | solution.py:477
  44.9 0.6 maximum_convert_fusion.par_ref
  45.6 5.8 all-gather.8.cloned.1.call-done.wo_hbm
  51.3 48.3 %all-gather.6.cloned.1.call-done.wq_hbm = bf16[768,2304]{1,0:T(8,128)(2,1)} async-done(((bf16[48,2304]{1,0:T(8,128)(2,1)}), bf16[768,2304]{1,0:T(8,128)(2,1)}) %all-gather.6.cloned.1.call-update) | async-done | bytes 3538960 | tf_op jit(solution)/shard_map/all_gather | solution.py:546
  99.6 54.0 %all-gather.10.cloned.1.call-done.wu_hbm = bf16[768,3072]{1,0:T(8,128)(2,1)} async-done(((bf16[48,3072]{1,0:T(8,128)(2,1)}), bf16[768,3072]{1,0:T(8,128)(2,1)}) %all-gather.10.cloned.1.call-update) | async-done | bytes 4718608 | tf_op jit(solution)/shard_map/all_gather | solution.py:546
  153.7 53.8 %all-gather.12.cloned.1.call-done.wd_hbm = bf16[3072,768]{1,0:T(8,128)(2,1)} async-done(((bf16[192,768]{1,0:T(8,128)(2,1)}), bf16[3072,768]{1,0:T(8,128)(2,1)}) %all-gather.12.cloned.1.call-update) | async-done | bytes 4718608 | tf_op jit(solution)/shard_map/all_gather | solution.py:546
  207.5 147.0 %block_pass.1 = (bf16[1024,768]{1,0:T(8,128)(2,1)}, f32[1024,768]{1,0:T(8,128)}, bf16[768,2304]{1,0:T(8,128)(2,1)}, bf16[768,768]{1,0:T(8,128)(2,1)}, bf16[768,3...) custom-call(s32[1]{0:T(128)S(6)} %copy.32.start_ref, f32[5]{0:T(128)} %mix_ref.3, ...), custom_call_target="tpu_custom_call" | custom-call | tf_op jit(solution)/shard_map/block_pass/pallas_call | solution.py:511
  354.6 0.0 reduce-scatter.10.cloned.1.call-update
  354.6 0.0 reduce-scatter.8.cloned.1.call-start
  354.7 0.5 reduce-scatter.8.cloned.1.call-update
  355.2 0.0 reduce-scatter.12.cloned.1.call-start
  355.2 0.7 reduce-scatter.12.cloned.1.call-update
  356.0 0.0 reduce-scatter.14.cloned.1.call-start
  356.0 0.7 reduce-scatter.14.cloned.1.call-update
  356.7 0.0 reduce-scatter.16.cloned.1.call-start
  356.8 0.7 slice.31
  357.5 0.8 copy.26
  358.4 0.0 all-reduce.3.cloned.1.call-start
  358.4 53.1 %reduce-scatter.10.cloned.1.call-done = bf16[48,768]{1,0:T(8,128)(2,1)} async-done(((bf16[768,768]{1,0:T(8,128)(2,1)}), bf16[48,768]{1,0:T(8,128)(2,1)}) %reduce-scatter.10.cloned.1.call-update) | async-done | bytes 73744 | tf_op jit(solution)/shard_map/reduce_scatter | solution.py:559
  411.5 70.9 %reduce-scatter.8.cloned.1.call-done = bf16[48,2304]{1,0:T(8,128)(2,1)} async-done(((bf16[768,2304]{1,0:T(8,128)(2,1)}), bf16[48,2304]{1,0:T(8,128)(2,1)}) %reduce-scatter.8.cloned.1.call-update) | async-done | bytes 221200 | tf_op jit(solution)/shard_map/reduce_scatter | solution.py:559
  482.4 78.3 %reduce-scatter.12.cloned.1.call-done = bf16[48,3072]{1,0:T(8,128)(2,1)} async-done(((bf16[768,3072]{1,0:T(8,128)(2,1)}), bf16[48,3072]{1,0:T(8,128)(2,1)}) %reduce-scatter.12.cloned.1.call-update) | async-done | bytes 294928 | tf_op jit(solution)/shard_map/reduce_scatter | solution.py:559
  560.7 78.7 %reduce-scatter.14.cloned.1.call-done = bf16[192,768]{1,0:T(8,128)(2,1)} async-done(((bf16[3072,768]{1,0:T(8,128)(2,1)}), bf16[192,768]{1,0:T(8,128)(2,1)}) %reduce-scatter.14.cloned.1.call-update) | async-done | bytes 294928 | tf_op jit(solution)/shard_map/reduce_scatter | solution.py:559
  639.5 0.1 slice_reduce_fusion
  639.6 1.4 slice_reduce_fusion.1
  640.9 0.7 pad_maximum_fusion
  641.6 39.5 %psum.42 = f32[5]{0:T(128)} all-reduce(f32[5]{0:T(128)S(1)} %pad_maximum_fusion), channel_id=1, replica_groups=mesh['rep'=2,'shard'=16] {'rep','shard'}, use_global_device_ids=true, to_apply=%region_2.0 | all-reduce | flops 5 | bytes 40 | tf_op jit(solution)/shard_map/psum | solution.py:556
  681.2 14.9 %reduce-scatter.16.cloned.1.call-done = bf16[48,4]{1,0:T(8,128)(2,1)} async-done(((bf16[768,4]{1,0:T(8,128)(2,1)}), bf16[48,4]{1,0:T(8,128)(2,1)}) %reduce-scatter.16.cloned.1.call-update) | async-done | bytes 400
  696.0 0.8 copy.27
  696.8 4.9 psum.47
  701.7 0.6 slice.22
  702.3 0.5 slice_bitcast_fusion
  702.8 31.2 %all-reduce.3.cloned.1.call-done = (bf16[48,2304]{1,0:T(8,128)(2,1)}, bf16[48,768]{1,0:T(8,128)(2,1)}, bf16[48,3072]{1,0:T(8,128)(2,1)}, bf16[192,768]{1,0:T(8,128)(2,1)}) async-done(((bf16[48,2304]{1,0:T(8,128)(2,1)}, bf16[48,768]{1,0:T(8,128)(2,1)}, bf16[48,3072]{1,0:T(8,128)(2,1)}, bf16[192,768]{1,0:T(8,128)(2,1)}), (bf16[48,2304]{1,0:T(8,128)(2,1)}, bf16[48,768]{1,0:T(8,128)(2,1)}, ...) | async-done | bytes 884752 | tf_op jit(solution)/shard_map/psum | solution.py:560
  734.0 1.6 convert_element_type.18
  735.6 1.7 convert_element_type.17
  737.3 1.8 convert_element_type.19
  739.1 1.8 convert_element_type.20
  (6 shorter events, 0.0 us)
Async XLA Ops:
  7.2 44.1 %all-gather.8.cloned.1.call-start = ((), (), s32[]{:S(2)}) async-start(), calls=%async_computation.6 | async-start | bytes 1253376 | tf_op jit(solution)/shard_map/all_gather | solution.py:546
  7.9 91.7 %all-gather.6.cloned.1.call-start = ((), (), s32[]{:S(2)}) async-start(), calls=%async_computation.5 | async-start | bytes 3760128 | tf_op jit(solution)/shard_map/all_gather | solution.py:546
  8.7 145.0 %all-gather.10.cloned.1.call-start = ((), (), s32[]{:S(2)}) async-start(), calls=%async_computation.7 | async-start | bytes 5013504 | tf_op jit(solution)/shard_map/all_gather | solution.py:546
  9.4 198.1 %all-gather.12.cloned.1.call-start = ((), (), s32[]{:S(2)}) async-start(), calls=%async_computation.8 | async-start | bytes 5013504 | tf_op jit(solution)/shard_map/all_gather | solution.py:546
  10.0 401.6 %reduce-scatter.10.cloned.1.call-start = ((), (), s32[]{:S(2)}) async-start(), calls=%async_computation.10 | async-start | bytes 1253376 | tf_op jit(solution)/shard_map/reduce_scatter | solution.py:559
  354.6 127.8 %reduce-scatter.8.cloned.1.call-start = ((), (), s32[]{:S(2)}) async-start(), calls=%async_computation.9 | async-start | bytes 3760128 | tf_op jit(solution)/shard_map/reduce_scatter | solution.py:559
  355.2 205.6 %reduce-scatter.12.cloned.1.call-start = ((), (), s32[]{:S(2)}) async-start(), calls=%async_computation.11 | async-start | bytes 5013504 | tf_op jit(solution)/shard_map/reduce_scatter | solution.py:559
  355.9 283.5 %copy-start = (f32[8,768]{1,0:T(8,128)S(1)}, f32[8,768]{1,0:T(8,128)}, u32[]{:S(2)}) copy-start(f32[8,768]{1,0:T(8,128)} %get-tuple-element.25) | copy-start | bytes 73732
  356.0 283.5 %reduce-scatter.14.cloned.1.call-start = ((), (), s32[]{:S(2)}) async-start(), calls=%async_computation.12 | async-start | bytes 5013504 | tf_op jit(solution)/shard_map/reduce_scatter | solution.py:559
  356.7 339.3 %reduce-scatter.16.cloned.1.call-start = ((), (), s32[]{:S(2)}) async-start(), calls=%async_computation.13 | async-start | bytes 208896
  358.4 375.7 %all-reduce.3.cloned.1.call-start = ((), (), s32[]{:S(2)}) async-start(), calls=%async_computation.14 | async-start | bytes 1769472 | tf_op jit(solution)/shard_map/psum | solution.py:560
Sparse Core Ops, SparseCore 0:
  10.3 41.0 all-gather.7
  53.6 45.9 all-gather.5
  101.9 51.7 all-gather.9
  155.8 51.6 all-gather.11
  354.7 56.7 reduce-scatter.9
  415.3 67.1 reduce-scatter.7
  486.3 74.4 reduce-scatter.11
  564.6 74.7 reduce-scatter.13
  643.5 52.4 reduce-scatter.15
  698.4 35.5 all-reduce.2

commit v2 on v1

v2 whole, which is shorter than its diff:
```python
import functools
import jax
import jax.numpy as jnp
import numpy as np
from jax import lax
from jax.experimental import pallas as pl
from jax.experimental.pallas import tpu as pltpu
from jax.sharding import PartitionSpec as P

BF = jnp.bfloat16
F32 = jnp.float32
HEADS = 12
SPAN = 256
BL = 256
NEG = -1e30
EPS = 1e-05
FB = 256


def dot(a, b):
    return lax.dot_general(a, b, (((1,), (0,)), ((), ())), preferred_element_type=F32)


def dot_bt(a, b):
    return lax.dot_general(a, b, (((1,), (1,)), ((), ())), preferred_element_type=F32)


def dot_at(a, b):
    return lax.dot_general(a, b, (((0,), (0,)), ((), ())), preferred_element_type=F32)


def iota(shape, axis):
    return lax.broadcasted_iota(jnp.int32, shape, axis)


def cols(start, width=128):
    return pl.ds(pl.multiple_of(start, 128), width)


def rows(start, height):
    return pl.ds(pl.multiple_of(start, height), height)


def norm_parts(values):
    average = jnp.mean(values, axis=-1, keepdims=True)
    centered = values - average
    inverse_std = lax.rsqrt(jnp.mean(centered * centered, axis=-1, keepdims=True) + EPS)
    return centered * inverse_std, inverse_std


def norm_back(incoming, normed, inverse_std, gain_row):
    scaled = incoming * gain_row
    inner = (
        scaled
        - jnp.mean(scaled, axis=-1, keepdims=True)
        - normed * jnp.mean(scaled * normed, axis=-1, keepdims=True)
    )
    return inverse_std * inner


def fold8(values):
    return jnp.sum(values.reshape(values.shape[0] // 8, 8, values.shape[1]), axis=0)


def turn(values, low_quarter):
    return jnp.where(low_quarter, pltpu.roll(values, 96, 1), pltpu.roll(values, 32, 1))


def gelu_parts(upper):
    size = jnp.abs(upper)
    t = 1.0 / (1.0 + 0.2316419 * size)
    density = jnp.exp(-0.5 * upper * upper) * 0.3989422804014327
    poly = ((((1.330274429 * t - 1.821255978) * t + 1.781477937) * t - 0.356563782) * t + 0.319381530) * t
    tail = density * poly
    cdf = jnp.where(upper >= 0, 1.0 - tail, tail)
    return upper * cdf, cdf + upper * density


def split3(values):
    high = values.astype(BF)
    rest = values - high.astype(F32)
    mid = rest.astype(BF)
    return high, mid, (rest - mid.astype(F32)).astype(BF)


def block_bias(start, query0, key0, causal, transposed):
    query = query0 + iota((BL, BL), 1 if transposed else 0)
    key = key0 + iota((BL, BL), 0 if transposed else 1)
    inside = (query >= start) & (query < start + SPAN) & (key >= start) & (key < start + SPAN)
    seen = (inside | (key <= query)) if causal else inside
    return jnp.where(seen, 0.0, NEG).astype(F32)


def fill_bias(start, bias_ref, blocks, transposed):
    span_block = start // BL
    for i in range(blocks):
        bias_ref[i] = block_bias(start, i * BL, i * BL, True, transposed)
    extra = block_bias(start, span_block * BL, (span_block + 1) * BL, False, transposed)
    bias_ref[blocks] = jnp.where(span_block + 1 < blocks, extra, NEG)


def pick(span_block, blocks, load):
    value = load(0)
    for b in range(1, blocks - 1):
        value = lax.select(span_block == b, load(b), value)
    return value


def forward_pair(h, start, qkv_ref, bias_ref, out_ref, lse_ref):
    length, width = out_ref.shape
    blocks = length // BL
    span_block = start // BL
    first = iota((BL, 128), 1) < 64
    first_all = iota((length, 128), 1) < 64
    zero = jnp.zeros((), BF)
    one = jnp.ones((), BF)

    oc, qc, kc, vc = pair_columns(h)
    keys = qkv_ref[:, kc]
    values = qkv_ref[:, vc]
    with_ones = (jnp.where(first_all, values, one), jnp.where(first_all, one, values))
    qx = pick(span_block, blocks, lambda b: qkv_ref[pl.ds(b * BL, BL), qc])
    kx = pick(span_block, blocks, lambda b: qkv_ref[pl.ds((b + 1) * BL, BL), kc])
    vx = pick(span_block, blocks, lambda b: qkv_ref[pl.ds((b + 1) * BL, BL), vc])
    extra = []
    for head in (0, 1):
        mine = first if head == 0 else ~first
        s = dot_bt(jnp.where(mine, qx, zero), kx) + bias_ref[blocks]
        peak = jnp.max(s, axis=1, keepdims=True)
        extra.append((peak, dot(jnp.exp(s - peak).astype(BF), jnp.where(mine, vx, one))))
    for i in range(blocks):
        outs, peaks = [], []
        here = span_block == i
        qi = qkv_ref[pl.ds(i * BL, BL), qc]
        for head in (0, 1):
            mine = first if head == 0 else ~first
            qm = jnp.where(mine, qi, zero)
            extra_peak, extra_out = extra[head]
            diag = dot_bt(qm, keys[i * BL : (i + 1) * BL]) + bias_ref[i]
            peak = jnp.max(diag, axis=1, keepdims=True)
            if i > 0:
                left = dot_bt(qm, keys[: i * BL])
                peak = jnp.maximum(peak, jnp.max(left, axis=1, keepdims=True))
            if i < blocks - 1:
                peak = jnp.maximum(peak, jnp.where(here, extra_peak, NEG))
            out = dot(jnp.exp(diag - peak).astype(BF), with_ones[head][i * BL : (i + 1) * BL])
            if i > 0:
                out = out + dot(jnp.exp(left - peak).astype(BF), with_ones[head][: i * BL])
            if i < blocks - 1:
                out = out + jnp.where(here, jnp.exp(extra_peak - peak), 0.0) * extra_out
            outs.append(out)
            peaks.append(peak)
        top = jnp.where(first, outs[0], outs[1])
        total = pltpu.roll(jnp.where(first, outs[1], outs[0]), 64, 1)
        out_ref[pl.ds(i * BL, BL), oc] = (top / total).astype(BF)
        lse_ref[pl.ds(i * BL, BL), oc] = jnp.where(first, peaks[0], peaks[1]) + jnp.log(total)


def backward_pair(h, start, qkv_ref, do_ref, out_ref, lse_ref, cos_ref, sin_ref, bias_ref, dq_ref):
    length, width = out_ref.shape
    blocks = length // BL
    span_block = start // BL
    lane_all = iota((length, 128), 1)
    lane = iota((BL, 128), 1)
    first = lane < 64
    low_quarter = (lane % 64) < 32
    zero = jnp.zeros((), BF)
    one = jnp.ones((), BF)

    def extend(values, column, head, lanes):
        a, b, c = split3(-column)
        base = 64 * (1 - head)
        parts = jnp.where(
            lanes == base, a, jnp.where(lanes == base + 1, b, jnp.where(lanes == base + 2, c, zero))
        )
        return jnp.where(lanes < 64, values, parts) if head == 0 else jnp.where(lanes < 64, parts, values)

    def keep(values, head, lanes, other):
        return jnp.where(lanes < 64, values, other) if head == 0 else jnp.where(lanes < 64, other, values)

    def rotate_back(values, cosine, sine):
        return values * cosine - turn(values, low_quarter) * sine

    oc, qc, kc, vc = pair_columns(h)

    def query_side(load, lanes):
        q, do, lse, out = load(qkv_ref, qc), load(do_ref, oc), load(lse_ref, oc), load(out_ref, oc)
        product = do.astype(F32) * out.astype(F32)
        sides = []
        for head in (0, 1):
            mine = (lanes < 64) if head == 0 else (lanes >= 64)
            delta = jnp.sum(jnp.where(mine, product, 0.0), axis=1, keepdims=True)
            sides.append(
                (
                    extend(q, lse[:, 64 * head : 64 * head + 1], head, lanes),
                    keep(q, head, lanes, zero),
                    extend(do, delta, head, lanes),
                    keep(do, head, lanes, zero),
                )
            )
        return sides

    everything = query_side(lambda ref, at: ref[:, at], lane_all)
    extra_side = query_side(
        lambda ref, at: pick(span_block, blocks, lambda b: ref[pl.ds(b * BL, BL), at]), lane
    )
    kx = pick(span_block, blocks, lambda b: qkv_ref[pl.ds((b + 1) * BL, BL), kc])
    vx = pick(span_block, blocks, lambda b: qkv_ref[pl.ds((b + 1) * BL, BL), vc])

    def block(k, v, head, qa, qm, da, dm, bias):
        s = dot_bt(keep(k, head, lane, one), qa)
        if bias is not None:
            s = s + bias
        p = jnp.exp(s)
        ds = (p * dot_bt(keep(v, head, lane, one), da)).astype(BF)
        return dot(p.astype(BF), dm), dot(ds, qm), dot_at(ds, keep(k, head, lane, zero))

    parts = [block(kx, vx, head, *extra_side[head], bias_ref[blocks]) for head in (0, 1)]
    dvx, dkx, dqx = [a + b for a, b in zip(*parts)]
    for j in range(blocks):
        at = slice(j * BL, (j + 1) * BL)
        rest = slice((j + 1) * BL, length)
        kj = qkv_ref[at, kc]
        vj = qkv_ref[at, vc]
        dv = jnp.where(span_block + 1 == j, dvx, 0.0) if j > 0 else None
        dk = jnp.where(span_block + 1 == j, dkx, 0.0) if j > 0 else None
        dq = jnp.where(span_block == j, dqx, 0.0) if j < blocks - 1 else None
        dq_rest = None
        add = lambda old, new: new if old is None else old + new
        for head in (0, 1):
            side = everything[head]
            a, b, c = block(kj, vj, head, *[item[at] for item in side], bias_ref[j])
            dv, dk, dq = add(dv, a), add(dk, b), add(dq, c)
            if j < blocks - 1:
                a, b, c = block(kj, vj, head, *[item[rest] for item in side], None)
                dv, dk, dq_rest = add(dv, a), add(dk, b), add(dq_rest, c)
        cosine, sine = cos_ref[at], sin_ref[at]
        if j > 0:
            dq = dq + dq_ref[at]
        qkv_ref[at, vc] = dv.astype(BF)
        qkv_ref[at, kc] = rotate_back(dk, cosine, sine).astype(BF)
        qkv_ref[at, qc] = rotate_back(dq * 0.125, cosine, sine).astype(BF)
        if j < blocks - 1:
            dq_ref[rest] = dq_rest if j == 0 else dq_ref[rest] + dq_rest


MESH = pl.DeviceIdType.MESH
UNITS = 12
LAST = UNITS + 5


class Place:
    def __init__(self):
        self.y = lax.axis_index("rep")
        s = lax.axis_index("shard")
        self.z, self.x, self.c = s // 4, (s // 2) % 2, s % 2

    def at(self, y, z, x, c):
        return (y, (z * 2 + x) * 2 + c)

    def twin(self):
        return self.at(self.y, self.z, self.x, 1 - self.c)

    def across_x(self):
        return self.at(self.y, self.z, 1 - self.x, self.c)

    def across_y(self):
        return self.at(1 - self.y, self.z, self.x, self.c)

    def along_z(self, k):
        return self.at(self.y, (self.z + k) % 4, self.x, self.c)

    def peers(self):
        return [self.twin(), self.across_x(), self.across_y()] + [self.along_z(k) for k in (1, 2, 3)]


def half(y):
    return pl.ds(pl.multiple_of(y * 384, 128), 384)


def remote(src, dst, sems, slot, kind, device):
    return pltpu.make_async_remote_copy(
        src_ref=src,
        dst_ref=dst,
        send_sem=sems.at[0, slot, kind],
        recv_sem=sems.at[1, slot, kind],
        device_id=device,
        device_id_type=MESH,
    )


class Gather:
    def __init__(self, place, w_ref, sems):
        self.p, self.w, self.sems = place, w_ref, sems

    def copies(self, stage, u, mine):
        p, w = self.p, self.w
        slot = u % 2
        y, z, x, c = p.y, p.z, p.x, p.c

        def same(ref, kind, device):
            return remote(ref, ref, self.sems, slot, kind, device)

        if stage == 0:
            return [
                same(w.at[u, z if mine else (z + 4 - k) % 4, x, c, :, half(y)], k - 1, p.along_z(k)) for k in (1, 2, 3)
            ]
        if stage == 1:
            return [
                same(w.at[u, :, x if mine else 1 - x, c, :, half(y)], 3, p.across_x()),
                same(w.at[u, :, x, c, :, half(y if mine else 1 - y)], 4, p.across_y()),
            ]
        if stage == 2:
            return [
                same(w.at[u, 0:2, x if mine else 1 - x, c, :, half(1 - y)], 5, p.across_x()),
                same(w.at[u, 2:4, 1 - x, c, :, half(y if mine else 1 - y)], 6, p.across_y()),
            ]
        return [same(w.at[u, :, :, c if mine else 1 - c], 7, p.twin())]

    def step(self, stage, u):
        if stage > 0:
            for copy in self.copies(stage - 1, u, False):
                copy.wait_recv()
            for copy in self.copies(stage - 1, u, True):
                copy.wait_send()
        if stage < 4:
            for copy in self.copies(stage, u, True):
                copy.start()

    def tick(self, n):
        for stage in (4, 3, 2, 1, 0):
            u = n - stage
            if isinstance(n, int):
                if 0 <= u < UNITS:
                    self.step(stage, u)
            else:
                pl.when((u >= 0) & (u < UNITS))(functools.partial(self.step, stage, u))


class Reduce:
    def __init__(self, place, w_ref, own_ref, rc, rdx, rdy, rxx, rxy, rz, sems):
        self.p, self.w, self.own, self.sems = place, w_ref, own_ref, sems
        self.rc, self.rdx, self.rdy, self.rxx, self.rxy, self.rz = rc, rdx, rdy, rxx, rxy, rz

    def copies(self, stage, n, mine):
        p, w = self.p, self.w
        u = unit_of(n)
        slot = n % 2
        y, z, x, c = p.y, p.z, p.x, p.c

        def send(src, dst, kind, device):
            return remote(src, dst, self.sems, slot, kind, device)

        if stage == 0:
            return [send(w.at[u, :, :, 1 - c], self.rc.at[slot], 0, p.twin())]
        if stage == 1:
            return [
                send(w.at[u, 0:2, 1 - x, c, :, half(1 - y)], self.rdx.at[slot], 1, p.across_x()),
                send(w.at[u, 2:4, 1 - x, c, :, half(1 - y)], self.rdy.at[slot], 2, p.across_y()),
            ]
        if stage == 2:
            return [
                send(w.at[u, :, 1 - x, c, :, half(y)], self.rxx.at[slot], 3, p.across_x()),
                send(w.at[u, :, x, c, :, half(1 - y)], self.rxy.at[slot], 4, p.across_y()),
            ]
        if stage == 3:
            return [
                send(w.at[u, (z + k) % 4, x, c, :, half(y)], self.rz.at[slot, k - 1], 4 + k, p.along_z(k))
                for k in (1, 2, 3)
            ]
        there = self.own.at[u, :, half(y if mine else 1 - y)]
        return [send(there, there, 8, p.across_y())]

    def add(self, stage, n):
        p, w = self.p, self.w
        u = unit_of(n)
        slot = n % 2
        y, z, x, c = p.y, p.z, p.x, p.c
        f = lambda value: value.astype(F32)
        if stage == 1:

            def piece(zz, carry):
                w[u, zz, :, c] = (f(w[u, zz, :, c]) + f(self.rc[slot, zz])).astype(BF)
                return carry

            lax.fori_loop(0, 4, piece, 0)
        if stage == 2:
            w[u, 0:2, x, c, :, half(1 - y)] = (f(w[u, 0:2, x, c, :, half(1 - y)]) + f(self.rdx[slot])).astype(BF)
            w[u, 2:4, 1 - x, c, :, half(y)] = (f(w[u, 2:4, 1 - x, c, :, half(y)]) + f(self.rdy[slot])).astype(BF)
        if stage == 3:
            w[u, :, x, c, :, half(y)] = (
                f(w[u, :, x, c, :, half(y)]) + f(self.rxx[slot]) + f(self.rxy[slot])
            ).astype(BF)
        if stage == 4:
            total = f(w[u, z, x, c, :, half(y)])
            for k in (0, 1, 2):
                total = total + f(self.rz[slot, k])
            self.own[u, :, half(y)] = total.astype(BF)

    def step(self, stage, n):
        if stage > 0:
            for copy in self.copies(stage - 1, n, False):
                copy.wait_recv()
            for copy in self.copies(stage - 1, n, True):
                copy.wait_send()
            self.add(stage, n)
        if stage < 5:
            for copy in self.copies(stage, n, True):
                copy.start()

    def tick(self, t):
        for stage in (5, 4, 3, 2, 1, 0):
            n = t - stage
            if isinstance(t, int):
                if 0 <= n < UNITS:
                    self.step(stage, n)
            else:
                pl.when((n >= 0) & (n < UNITS))(functools.partial(self.step, stage, n))


def unit_of(n):
    if isinstance(n, int):
        return 8 + n if n < 4 else n if n < 8 else 3 if n == 8 else n - 9
    return jnp.where(n < 4, 8 + n, jnp.where(n < 8, n, jnp.where(n == 8, 3, n - 9)))


def small_sum(place, value, stage_ref, land_ref, z_ref, sems, with_y):
    steps = [(0, place.twin()), (1, place.across_x())] + ([(2, place.across_y())] if with_y else [])
    for i, device in steps:
        stage_ref[i] = value
        copy = remote(stage_ref.at[i], land_ref.at[i], sems, 0, i, device)
        copy.start()
        copy.wait()
        value = value + land_ref[i]
    z_ref[0] = value
    sent = [remote(z_ref.at[0], z_ref.at[k], sems, 0, 2 + k, place.along_z(k)) for k in (1, 2, 3)]
    for copy in sent:
        copy.start()
    for copy in sent:
        copy.wait()
    total = None
    for zz in range(4):
        part = z_ref[(place.z + 4 - zz) % 4]
        total = part if total is None else total + part
    return total


def history_kernel(mix_ref, history_ref, g_ref, grad_ref, earlier_ref, terms_ref):
    g = g_ref[...].astype(F32)
    earlier = None
    parts = []
    for k in range(history_ref.shape[0]):
        h = history_ref[k].astype(F32)
        grad_ref[k] = mix_ref[k] * g
        term = mix_ref[k] * h
        earlier = term if earlier is None else earlier + term
        parts.append(jnp.sum(fold8(h * g), axis=0, keepdims=True))
    earlier_ref[...] = earlier.astype(BF)
    new = jnp.concatenate(parts + [jnp.zeros((8 - len(parts), g.shape[1]), F32)], axis=0)

    @pl.when(pl.program_id(0) == 0)
    def _():
        terms_ref[...] = new

    @pl.when(pl.program_id(0) > 0)
    def _():
        terms_ref[...] += new


def history_pass(mix, history, g):
    past, length, width = history.shape
    height = 128
    return pl.pallas_call(
        history_kernel,
        grid=(length // height,),
        in_specs=[
            pl.BlockSpec(memory_space=pltpu.SMEM),
            pl.BlockSpec((past, height, width), lambda i: (0, i, 0)),
            pl.BlockSpec((height, width), lambda i: (i, 0)),
        ],
        out_specs=(
            pl.BlockSpec((past, height, width), lambda i: (0, i, 0)),
            pl.BlockSpec((height, width), lambda i: (i, 0)),
            pl.BlockSpec((8, width), lambda i: (0, 0)),
        ),
        out_shape=(
            jax.ShapeDtypeStruct((past, length, width), F32),
            jax.ShapeDtypeStruct((length, width), BF),
            jax.ShapeDtypeStruct((8, width), F32),
        ),
        name="history_pass",
    )(mix, history, g)


def first_norm(x_ref, par_ref, act_ref):
    height = 128

    def chunk(r, carry):
        at = rows(r * height, height)
        normed, _ = norm_parts(x_ref[at, :].astype(F32))
        act_ref[at, :] = (normed * par_ref[0:1, :] + par_ref[2:3, :]).astype(BF)
        return carry

    lax.fori_loop(0, x_ref.shape[0] // height, chunk, 0)


def pair_columns(h):
    base = (h // 2) * 768 + (h % 2) * 128
    return cols(h * 128), cols(base), cols(base + 256), cols(base + 512)


def unit(w_ref, u):
    return w_ref[u].reshape(768, 768)


def project(j, act_ref, w_ref, cos_ref, sin_ref, qkv_ref):
    height = 256
    low_quarter = (iota((height, 128), 1) % 64) < 32

    def chunk(r, carry):
        at = rows(r * height, height)
        out = dot(act_ref[at, :], unit(w_ref, j))
        cosine, sine = cos_ref[at, :], sin_ref[at, :]
        for piece in range(6):
            u = out[:, piece * 128 : piece * 128 + 128]
            if piece < 4:
                u = u * cosine + turn(u, low_quarter) * sine
            if piece < 2:
                u = u * 0.125
            qkv_ref[at, cols(j * 768 + piece * 128)] = u.astype(BF)
        return carry

    lax.fori_loop(0, act_ref.shape[0] // height, chunk, 0)


def attention_out(x_ref, mixed_ref, w_ref, par_ref, middle_ref, act_ref, actt_ref, out_ref, dact_ref):
    height = 256

    def chunk(r, carry):
        at = rows(r * height, height)
        middle = x_ref[at, :].astype(F32) + dot(mixed_ref[at, :], unit(w_ref, 3))
        middle_ref[at, :] = middle
        out_ref[at, :] = middle
        dact_ref[at, :] = jnp.zeros_like(middle)
        normed, _ = norm_parts(middle)
        act = (normed * par_ref[1:2, :] + par_ref[3:4, :]).astype(BF)
        act_ref[at, :] = act
        actt_ref[:, rows(r * height, height)] = act.T
        return carry

    lax.fori_loop(0, x_ref.shape[0] // height, chunk, 0)


def down_pieces():
    return [(x, c, q) for x in (0, 1) for c in (0, 1) for q in range(4)]


def feed_forward(z, act_ref, actt_ref, gb_ref, w_ref, hid_ref, gu_ref, out_ref, dact_ref):
    height = 256

    def chunk(r, carry):
        at = rows(r * height, height)
        up = unit(w_ref, 8 + z)
        down = jnp.concatenate([w_ref[4 + q, z, x, c] for x, c, q in down_pieces()], axis=0)
        hidden, slope = gelu_parts(dot(act_ref[at, :], up))
        hidden = hidden.astype(BF)
        hid_ref[at, :] = hidden
        gu = (dot_bt(gb_ref[at, :], down) * slope).astype(BF)
        gu_ref[at, :] = gu
        out_ref[at, :] += dot(hidden, down)
        dact_ref[at, :] += dot_bt(gu, up)
        return carry

    lax.fori_loop(0, act_ref.shape[0] // height, chunk, 0)
    grad = dot_at(hid_ref[...], gb_ref[...]).astype(BF)
    for i, (x, c, q) in enumerate(down_pieces()):
        w_ref[4 + q, z, x, c] = grad[48 * i : 48 * i + 48]
    w_ref[8 + z] = dot(actt_ref[...], gu_ref[...]).astype(BF).reshape(w_ref.shape[1:])


def branch_grad(mix4, g_ref, gb_ref):
    height = 256

    def chunk(r, carry):
        at = rows(r * height, height)
        gb_ref[at, :] = (mix4 * g_ref[at, :].astype(F32)).astype(BF)
        return carry

    lax.fori_loop(0, g_ref.shape[0] // height, chunk, 0)


def middle_back(mix4, g_ref, earlier_ref, middle_ref, out_ref, dact_ref, mixed_ref, w_ref, par_ref,
                next_ref, ga_ref, do_ref, small_ref):
    height = 256
    width = g_ref.shape[1]
    zero = jnp.zeros((8, width), F32)

    def chunk(r, carry):
        gain, bias, terms = carry
        at = rows(r * height, height)
        g = g_ref[at, :].astype(F32)
        output = out_ref[at, :]
        next_ref[at, :] = (earlier_ref[at, :].astype(F32) + mix4 * output).astype(BF)
        terms = terms + fold8(g * output)
        normed, inverse = norm_parts(middle_ref[at, :])
        dact = dact_ref[at, :]
        gain = gain + fold8(dact * normed)
        bias = bias + fold8(dact)
        grad = mix4 * g + norm_back(dact, normed, inverse, par_ref[1:2, :])
        dact_ref[at, :] = grad
        low = grad.astype(BF)
        ga_ref[at, :] = low
        do_ref[at, :] = dot_bt(low, unit(w_ref, 3)).astype(BF)
        return gain, bias, terms

    gain, bias, terms = lax.fori_loop(0, g_ref.shape[0] // height, chunk, (zero, zero, zero))
    small_ref[1:2, :] = jnp.sum(gain, axis=0, keepdims=True)
    small_ref[3:4, :] = jnp.sum(bias, axis=0, keepdims=True)
    small_ref[5:6, :] = jnp.sum(terms, axis=0, keepdims=True)
    w_ref[3] = dot_at(mixed_ref[...], ga_ref[...]).astype(BF).reshape(w_ref.shape[1:])


def project_back(j, actt_ref, qkv_ref, w_ref, out_ref):
    height = 256

    def chunk(r, carry):
        at = rows(r * height, height)
        share = dot_bt(qkv_ref[at, cols(j * 768, 768)], unit(w_ref, j))
        out_ref[at, :] = jnp.where(j == 0, 0.0, out_ref[at, :]) + share
        return carry

    lax.fori_loop(0, qkv_ref.shape[0] // height, chunk, 0)
    w_ref[j] = dot(actt_ref[...], qkv_ref[:, cols(j * 768, 768)]).astype(BF).reshape(w_ref.shape[1:])


def first_back(x_ref, dact_ref, par_ref, dmid_ref, small_ref):
    height = 128
    zero = jnp.zeros((8, x_ref.shape[1]), F32)

    def chunk(r, carry):
        gain, bias = carry
        at = rows(r * height, height)
        dact = dact_ref[at, :]
        normed, inverse = norm_parts(x_ref[at, :].astype(F32))
        gain = gain + fold8(dact * normed)
        bias = bias + fold8(dact)
        dmid_ref[at, :] += norm_back(dact, normed, inverse, par_ref[0:1, :])
        return gain, bias

    gain, bias = lax.fori_loop(0, x_ref.shape[0] // height, chunk, (zero, zero))
    small_ref[0:1, :] = jnp.sum(gain, axis=0, keepdims=True)
    small_ref[2:3, :] = jnp.sum(bias, axis=0, keepdims=True)


def fill_tables(table_ref, cos_ref, sin_ref):
    blocks = cos_ref.shape[0] // 32
    cb, sb, sign = table_ref[0], table_ref[1], table_ref[2]

    def block(a, carry):
        ca, sa = table_ref[3, pl.ds(a, 1), :], table_ref[4, pl.ds(a, 1), :]
        at = rows(a * 32, 32)
        cos_ref[at, :] = ca * cb - sa * sb
        sin_ref[at, :] = (sa * cb + ca * sb) * sign
        return carry

    lax.fori_loop(0, blocks, block, 0)


def rotary_table(length):
    freq = np.tile(np.exp(-np.log(10000.0) * np.arange(32) / 32.0), 4)[None, :]
    fine = np.arange(32)[:, None] * freq
    coarse = 32 * np.arange(32)[:, None] * freq
    sign = np.tile(np.repeat([-1.0, 1.0], 32), 2)[None, :] * np.ones((32, 1))
    return jnp.asarray(np.stack([np.cos(fine), np.sin(fine), sign, np.cos(coarse), np.sin(coarse)]), F32)


def block_kernel(joined, *refs):
    if joined:
        start_ref, mix_ref, x_hbm, g_hbm, earlier_hbm, par_in, terms_ref, table_ref, wq_hbm, wo_hbm, wu_hbm, wd_hbm = refs[:12]
        next_hbm, dx_hbm, own_hbm, small_out = refs[12:16]
        refs = refs[16:]
    else:
        start_ref, mix_ref, x_hbm, g_hbm, earlier_hbm, par_in, terms_ref, table_ref, w_hbm = refs[:9]
        next_hbm, dx_hbm, grad_hbm, small_out = refs[9:13]
        refs = refs[13:]
    x, g, gb, act1, act2, actt, mixed, earlier, hid, gu, qkv, lse, middle, out, dact = refs[:15]
    w, bias, dq, cosine, sine, small, par, loads = refs[15:23]
    start = start_ref[0]
    mix4 = mix_ref[4]

    load = lambda src, dst, i: pltpu.make_async_copy(src, dst, loads.at[i])
    first = [load(x_hbm, x, 0)]
    later = [load(g_hbm, g, 1), load(earlier_hbm, earlier, 2)]
    if joined:
        own, rc, rdx, rdy, rxx, rxy, rz, stage_ref, land_ref, z_ref, gsems, rsems, ssems = refs[23:]
        place = Place()
        home = w.at[:, place.z, place.x, place.c]
        for j in range(3):
            for t in range(3):
                first.append(
                    load(wq_hbm.at[:, pl.ds(768 * t + 256 * j, 256)], home.at[j, :, pl.ds(256 * t, 256)], 3 + 3 * j + t)
                )
        first.append(load(wo_hbm, home.at[3], 12))
        first.append(load(wd_hbm, home.at[4:8], 13))
        for k in range(4):
            first.append(load(wu_hbm.at[:, pl.ds(768 * k, 768)], home.at[8 + k], 14 + k))
    else:
        first.append(load(w_hbm, w, 3))
    for copy in first + later:
        copy.start()
    if joined:
        for copy in first[1:]:
            copy.wait()
        barrier = pltpu.get_barrier_semaphore()
        for peer in place.peers():
            pl.semaphore_signal(barrier, inc=1, device_id=peer, device_id_type=MESH)
        pl.semaphore_wait(barrier, 6)
        gather = Gather(place, w, gsems)
        reduce = Reduce(place, w, own, rc, rdx, rdy, rxx, rxy, rz, rsems)
        gather.tick(0)
    else:
        first[1].wait()
    first[0].wait()
    if joined:
        par[...] = small_sum(place, par_in[...], stage_ref.at[0], land_ref.at[0], z_ref.at[0], ssems.at[0], False)
        gather.tick(1)
    else:
        par[...] = par_in[...]
    small[...] = jnp.zeros_like(small)
    first_norm(x, par, act1)
    fill_tables(table_ref, cosine, sine)
    if joined:
        gather.tick(2)
    fill_bias(start, bias, x.shape[0] // BL, False)
    for copy in later:
        copy.wait()
    branch_grad(mix4, g, gb)
    if joined:
        gather.tick(3)
        gather.tick(4)

    def forward_group(j, carry):
        project(j, act1, w, cosine, sine, qkv)

        def inner(i, carry):
            forward_pair(2 * j + i, start, qkv, bias, mixed, lse)
            if joined:
                gather.tick(5 + 2 * j + i)
            return carry

        return lax.fori_loop(0, 2, inner, carry)

    lax.fori_loop(0, 3, forward_group, 0)
    attention_out(x, mixed, w, par, middle, act2, actt, out, dact)
    if joined:
        gather.tick(11)

    def ff_group(z, carry):
        if joined:
            gather.tick(12 + z)
        feed_forward(z, act2, actt, gb, w, hid, gu, out, dact)
        if joined:
            reduce.tick(z)
        return carry

    lax.fori_loop(0, 4, ff_group, 0)
    if joined:
        reduce.tick(4)
    ga, do, nxt = gb, act2, earlier
    middle_back(mix4, g, earlier, middle, out, dact, mixed, w, par, nxt, ga, do, small)
    store_next = load(nxt, next_hbm, 0)
    store_next.start()
    if joined:
        reduce.tick(5)
    fill_bias(start, bias, x.shape[0] // BL, True)
    actt[...] = act1[...].T

    def backward_group(j, carry):
        def inner(i, carry):
            backward_pair(2 * j + i, start, qkv, do, mixed, lse, cosine, sine, bias, dq)

            @pl.when(i == 1)
            def _():
                project_back(j, actt, qkv, w, out)

            if joined:
                reduce.tick(6 + 2 * j + i)
            return carry

        return lax.fori_loop(0, 2, inner, carry)

    lax.fori_loop(0, 3, backward_group, 0)
    first_back(x, out, par, dact, small)
    store_dx = load(dact, dx_hbm, 1)
    store_dx.start()
    for k in range(4):
        small[4:5, 128 * k : 128 * k + 128] = fold_lanes(terms_ref[k : k + 1, :])
    small[4:5, 512:640] = fold_lanes(small[5:6, :])
    small[5:6, :] = jnp.zeros_like(small[5:6, :])
    if joined:
        reduce.tick(12)
        small_out[...] = small_sum(place, small[...], stage_ref.at[1], land_ref.at[1], z_ref.at[1], ssems.at[1], True)
        for t in range(13, LAST):
            reduce.tick(t)
        store_grad = load(own, own_hbm, 2)
    else:
        small_out[...] = small[...]
        store_grad = load(w, grad_hbm, 2)
    store_grad.start()
    store_next.wait()
    store_dx.wait()
    store_grad.wait()


def fold_lanes(row):
    total = row[:, 0:128]
    for i in range(1, row.shape[1] // 128):
        total = total + row[:, 128 * i : 128 * i + 128]
    return total


VMEM_LIMIT = 67043328
UNIT = (4, 2, 2, 48, 768)


def block_pass(joined, start, mix, x, g, earlier, par, terms, *weights):
    length, width = x.shape
    smem = pl.BlockSpec(memory_space=pltpu.SMEM)
    vmem = pl.BlockSpec(memory_space=pltpu.VMEM)
    anys = pl.BlockSpec(memory_space=pl.ANY)
    low = pltpu.VMEM((length, width), BF)
    full = pltpu.VMEM((length, width), F32)
    dma = pltpu.SemaphoreType.DMA
    small = (8, width)
    scratch = [low] * 5 + [pltpu.VMEM((width, length), BF)] + [low] * 4 + [pltpu.VMEM((length, 3 * width), BF)]
    scratch += [full] * 4
    scratch += [
        pltpu.VMEM((UNITS,) + UNIT, BF),
        pltpu.VMEM((length // BL + 1, BL, BL), F32),
        pltpu.VMEM((length, 128), F32),
        pltpu.VMEM((length, 128), F32),
        pltpu.VMEM((length, 128), F32),
        pltpu.VMEM(small, F32),
        pltpu.VMEM(small, F32),
        dma((18,)),
    ]
    grads = (UNITS,) + UNIT
    if joined:
        grads = (UNITS, 48, width)
        scratch += [
            pltpu.VMEM(grads, BF),
            pltpu.VMEM((2, 4, 2, 48, width), BF),
            pltpu.VMEM((2, 2, 48, width // 2), BF),
            pltpu.VMEM((2, 2, 48, width // 2), BF),
            pltpu.VMEM((2, 4, 48, width // 2), BF),
            pltpu.VMEM((2, 4, 48, width // 2), BF),
            pltpu.VMEM((2, 3, 48, width // 2), BF),
            pltpu.VMEM((2, 3) + small, F32),
            pltpu.VMEM((2, 3) + small, F32),
            pltpu.VMEM((2, 4) + small, F32),
            dma((2, 2, 8)),
            dma((2, 2, 9)),
            dma((2, 2, 1, 6)),
        ]
    params = dict(vmem_limit_bytes=VMEM_LIMIT)
    if joined:
        params.update(collective_id=0, has_side_effects=True)
    return pl.pallas_call(
        functools.partial(block_kernel, joined),
        in_specs=[smem, smem, anys, anys, anys, vmem, vmem, vmem] + [anys] * len(weights),
        out_specs=(anys, anys, anys, vmem),
        out_shape=(
            jax.ShapeDtypeStruct((length, width), BF),
            jax.ShapeDtypeStruct((length, width), F32),
            jax.ShapeDtypeStruct(grads, BF),
            jax.ShapeDtypeStruct(small, F32),
        ),
        scratch_shapes=scratch,
        compiler_params=pltpu.CompilerParams(**params),
        name="block_pass",
    )(start, mix, x, g, earlier, par, terms, rotary_table(length), *weights)


def to_units(wq, wo, wu, wd):
    d = wo.shape[0]
    parts = [
        wq.reshape(d, 3, 3, 256).transpose(2, 0, 1, 3).reshape(3, d, d),
        wo[None],
        wd.reshape(16, 4, 48, d).transpose(1, 0, 2, 3).reshape(4, d, d),
        wu.reshape(d, 4, d).transpose(1, 0, 2),
    ]
    return jnp.concatenate(parts).reshape((UNITS,) + UNIT)


def from_units(units, height):
    d = units.shape[-1]
    units = units.reshape(UNITS, -1, d)
    r = units.shape[1]
    gq = units[0:3].reshape(3, r, 3, 256).transpose(1, 2, 0, 3).reshape(r, 3 * d)
    gd = units[4:8].reshape(4, r // height, height, d).transpose(1, 0, 2, 3).reshape(4 * r, d)
    return gq, units[3], units[8:12].transpose(1, 0, 2).reshape(r, 4 * d), gd


def local(block_input, history, cotangent, span_start, w_qkv, w_out, w_up, w_down, ln_gains, ln_biases, mix_weights, joined):
    shard = lax.axis_index("shard")
    width = block_input.shape[1]
    own = ln_gains.shape[1]
    grad_history, earlier, terms = history_pass(mix_weights, history, cotangent)
    mine = jnp.concatenate([ln_gains, ln_biases]).astype(F32)
    if joined:
        par = lax.dynamic_update_slice(jnp.zeros((8, width), F32), mine, (0, shard * own))
        nxt, grad_input, units, small = block_pass(
            True, span_start, mix_weights, block_input, cotangent, earlier, par, terms,
            w_qkv, w_out, w_up, w_down.reshape(4, own, width),
        )
        gq, go, gu, gd = [item.astype(F32) for item in from_units(units, own)]
        norm_grads = lax.dynamic_slice(small, (0, shard * own), (4, own))
        grad_mix = jnp.sum(small[4, : 5 * 128].reshape(5, 128), axis=1)
    else:
        gather = lambda item, axis: lax.all_gather(item, "shard", axis=axis, tiled=True)
        par = jnp.concatenate([gather(mine.astype(BF), 1).astype(F32), jnp.zeros((4, width), F32)])
        weights = to_units(gather(w_qkv, 0), gather(w_out, 0), gather(w_up, 0), gather(w_down, 0))
        nxt, grad_input, units, small = block_pass(
            False, span_start, mix_weights, block_input, cotangent, earlier, par, terms, weights
        )

        def owned(item, axis):
            part = lax.psum_scatter(item.astype(BF), "shard", scatter_dimension=axis, tiled=True)
            return lax.psum(part, "rep").astype(F32)

        gq, go, gu, gd = [owned(item, 0) for item in from_units(units, 48)]
        norm_grads = owned(small[:4], 1)
        grad_mix = lax.psum(jnp.sum(small[4, : 5 * 128].reshape(5, 128), axis=1), ("rep", "shard"))
    return nxt, grad_input, grad_history, grad_mix, gq, go, gu, gd, norm_grads[0:2], norm_grads[2], norm_grads[3]


def solution(mesh):
    token = P(("rep", "shard"), None)
    kept = P("shard", None)
    past = P(None, ("rep", "shard"), None)
    norm = P(None, "shard")
    joined = mesh.shape["rep"] == 2 and mesh.shape["shard"] == 16
    return jax.shard_map(
        functools.partial(local, joined=joined),
        mesh=mesh,
        in_specs=(token, past, token, P(("rep", "shard")), kept, kept, kept, kept, norm, norm, P()),
        out_specs=(token, token, past, P(), kept, kept, kept, kept, norm, P("shard"), P("shard")),
        check_vma=False,
    )
```

time: 749 us -> 253 us (0.34)
  waiting for transfers between devices: 494 us -> 0 us
  Pallas kernels: 157 us -> 237 us
  blocking collectives: 67.6 us -> 0 us
  between operations: 14.9 us -> 1.39 us
  local copies, waits for them, and re-layouts: 3.56 us -> 11.2 us
    reduce_scatter x4 -> x0, waiting for transfers between devices: 281 us -> none  [owned(): lax.psum_scatter(item.astype(BF), 'shard', scatter_dimension=axis, tiled=...]
    all_gather x4 -> x0, waiting for transfers between devices: 162 us -> none  [local(): lax.all_gather(item, 'shard', axis=axis, tiled=True)]
    pallas_call x1, Pallas kernels: 147 us -> 226 us  [block_pass(): pl.pallas_call(functools.partial(block_kernel, joined), in_specs=[smem, s...]
    psum x2 -> x0, blocking collectives: 44.4 us -> none  [the longest x1 39.5 us: local(): grad_mix = lax.psum(partial_mix, ('rep', 'shard'))]
    psum x1 -> x0, waiting for transfers between devices: 31.2 us -> none  [owned(): return lax.psum(part, 'rep').astype(F32)]
    all_gather x1 -> x0, blocking collectives: 23.1 us -> none  [local(): lax.all_gather(item, 'shard', axis=axis, tiled=True)]
    unnamed x11 -> x0, waiting for transfers between devices: 19.4 us -> none
  transfers between devices with their start and end apart: 10 -> 0, of which waited for: 10 -> 0; matrix products, arithmetic and copies ran while one was open for 1% -> 0% of each run, Pallas kernels for 1% -> 0%
where the time goes in v2:
time: 253 us; the launch traced here: 252 us
  Pallas kernels  237 us (94%)
  local copies, waits for them, and re-layouts  11.2 us (4%)
  other arithmetic  3.2 us (1%)
    pallas_call x1, Pallas kernels, block_pass(): pl.pallas_call(functools.partial(block_kernel, joined), in_specs=[smem, s...  226 us
    pallas_call x1, Pallas kernels, history_pass(): pl.pallas_call(history_kernel, grid=(length // height,), in_specs=[pl.Blo...  10.4 us

profile of v2, /device:TPU:0, one launch (start us, length us, event | category | flops | bytes accessed | tf_op | source)
XLA Modules:
  0.0 252.3 jit_solution(4534413490377778613)
XLA Ops:
  1.3 0.0 copy-start.3
  1.3 0.0 copy-start.4
  1.3 10.4 %history_pass.1 = (f32[4,1024,768]{2,1,0:T(8,128)}, bf16[1024,768]{1,0:T(8,128)(2,1)}, f32[8,768]{1,0:T(8,128)}) custom-call(f32[5]{0:T(128)} %refs_1_.1, bf16[4,1024,768]{2,1,0:T(8,128)(2,1)} %history_ref.1, bf16[1024,768]{1,0:T(8,128)(2,1)} %refs_3_.1), custom_call_target="tpu_custom_call" | custom-call | tf_op jit(solution)/shard_map/history_pass/pallas_call | solution.py:473
  11.7 0.0 copy-done.3
  11.7 0.0 copy-done.4
  11.7 0.6 broadcast_in_dim.3
  12.3 1.4 dynamic_update_slice.3.refs_5_
  13.7 226.2 %block_pass.1 = (bf16[1024,768]{1,0:T(8,128)(2,1)}, f32[1024,768]{1,0:T(8,128)}, bf16[12,48,768]{2,1,0:T(8,128)(2,1)}, f32[8,768]{1,0:T(8,128)}) custom-call(s32[1]{0:T(128)S(6)} %copy.30.refs_0_, f32[5]{0:T(128)} %refs_1_.1, bf16[1024,768]{1,0:T(8,128)(2,1)} %refs_2_.1, bf16[1024,768]{1,0:T(8,128)(2,1)} %refs_3_.1, ...), custom_call_target="tpu_custom_call" | custom-call | tf_op jit(solution)/shard_map/block_pass/pallas_call | solution.py:868
  239.9 0.7 slice_reduce_fusion
  240.6 0.6 bitcast_reduce_fusion
  241.2 1.0 slice_convert_fusion
  242.2 0.0 copy-start.2
  242.2 0.2 reshape.43
  242.5 0.3 copy.24
  242.8 1.1 reshape.39
  243.8 0.0 copy-done.2
  243.8 0.7 bitcast_convert_fusion.1
  244.5 0.0 copy-start.1
  244.5 0.1 fusion
  244.6 0.9 copy.26
  245.4 0.9 bitcast_convert_fusion
  246.3 0.8 constant_dynamic-slice_fusion
  247.1 0.6 slice.29
  247.7 0.5 slice_bitcast_fusion
  248.2 0.0 copy-done.1
  248.2 0.0 copy-start
  248.2 1.1 copy.31
  249.3 1.3 copy-done
  250.6 1.7 copy.32
  (1 shorter events, 0.0 us)
Async XLA Ops:
  1.3 10.4 %copy-start.3 = (bf16[2,48]{1,0:T(2,128)(2,1)S(1)}, bf16[2,48]{1,0:T(2,128)(2,1)}, u32[]{:S(2)}) copy-start(bf16[2,48]{1,0:T(2,128)(2,1)} %param.21) | copy-start | bytes 580
  1.3 10.4 %copy-start.4 = (bf16[2,48]{1,0:T(2,128)(2,1)S(1)}, bf16[2,48]{1,0:T(2,128)(2,1)}, u32[]{:S(2)}) copy-start(bf16[2,48]{1,0:T(2,128)(2,1)} %param.20) | copy-start | bytes 580
  242.2 1.6 copy-start.2
  244.5 3.7 %copy-start.1 = (bf16[1024,768]{1,0:T(8,128)(2,1)S(1)}, bf16[1024,768]{1,0:T(8,128)(2,1)}, u32[]{:S(2)}) copy-start(bf16[1024,768]{1,0:T(8,128)(2,1)} %get-tuple-element.40) | copy-start | bytes 4718596
  248.2 2.5 copy-start

commit v3 on v2

--- a/solution.py
+++ b/solution.py
@@ -106,7 +106,7 @@
     return value
 
 
-def forward_pair(h, start, qkv_ref, bias_ref, out_ref, lse_ref):
+def forward_pair(h, start, qkv_ref, bias_ref, out_ref, lse_ref, after):
     length, width = out_ref.shape
     blocks = length // BL
     span_block = start // BL
@@ -154,9 +154,10 @@
         total = pltpu.roll(jnp.where(first, outs[1], outs[0]), 64, 1)
         out_ref[pl.ds(i * BL, BL), oc] = (top / total).astype(BF)
         lse_ref[pl.ds(i * BL, BL), oc] = jnp.where(first, peaks[0], peaks[1]) + jnp.log(total)
-
-
-def backward_pair(h, start, qkv_ref, do_ref, out_ref, lse_ref, cos_ref, sin_ref, bias_ref, dq_ref):
+        after(i)
+
+
+def backward_pair(h, start, qkv_ref, do_ref, out_ref, lse_ref, cos_ref, sin_ref, bias_ref, dq_ref, after):
     length, width = out_ref.shape
     blocks = length // BL
     span_block = start // BL
@@ -242,11 +243,15 @@
         qkv_ref[at, qc] = rotate_back(dq * 0.125, cosine, sine).astype(BF)
         if j < blocks - 1:
             dq_ref[rest] = dq_rest if j == 0 else dq_ref[rest] + dq_rest
+        after(j)
 
 
 MESH = pl.DeviceIdType.MESH
 UNITS = 12
-LAST = UNITS + 5
+PIECE = 48
+GAP = 4
+GATHER_AT = (0, 2, 5, 7, 9)
+REDUCE_AT = (0, 2, 5, 7, 10, 12)
 
 
 class Place:
@@ -270,8 +275,12 @@
     def along_z(self, k):
         return self.at(self.y, (self.z + k) % 4, self.x, self.c)
 
-    def peers(self):
-        return [self.twin(), self.across_x(), self.across_y()] + [self.along_z(k) for k in (1, 2, 3)]
+    def flat(self):
+        return ((self.y * 4 + self.z) * 2 + self.x) * 2 + self.c
+
+    def other(self, k):
+        there = (self.flat() + k) % 32
+        return there // 16, there % 16
 
 
 def half(y):
@@ -295,7 +304,7 @@
 
     def copies(self, stage, u, mine):
         p, w = self.p, self.w
-        slot = u % 2
+        slot = u
         y, z, x, c = p.y, p.z, p.x, p.c
 
         def same(ref, kind, device):
@@ -327,14 +336,15 @@
             for copy in self.copies(stage, u, True):
                 copy.start()
 
-    def tick(self, n):
+    def half_tick(self, m, odd):
         for stage in (4, 3, 2, 1, 0):
-            u = n - stage
-            if isinstance(n, int):
-                if 0 <= u < UNITS:
-                    self.step(stage, u)
-            else:
-                pl.when((u >= 0) & (u < UNITS))(functools.partial(self.step, stage, u))
+            if GATHER_AT[stage] % 2 == odd:
+                u = m - GATHER_AT[stage] // 2
+                if isinstance(u, int):
+                    if 0 <= u < UNITS:
+                        self.step(stage, u)
+                else:
+                    pl.when((u >= 0) & (u < UNITS))(functools.partial(self.step, stage, u))
 
 
 class Reduce:
@@ -344,15 +354,15 @@
 
     def copies(self, stage, n, mine):
         p, w = self.p, self.w
-        u = unit_of(n)
-        slot = n % 2
+        u = held_in(n)
+        slot = n % GAP
         y, z, x, c = p.y, p.z, p.x, p.c
 
         def send(src, dst, kind, device):
             return remote(src, dst, self.sems, slot, kind, device)
 
         if stage == 0:
-            return [send(w.at[u, :, :, 1 - c], self.rc.at[slot], 0, p.twin())]
+            return [send(w.at[u, :, :, 1 - c], self.rc.at[n % 2], 0, p.twin())]
         if stage == 1:
             return [
                 send(w.at[u, 0:2, 1 - x, c, :, half(1 - y)], self.rdx.at[slot], 1, p.across_x()),
@@ -368,19 +378,19 @@
                 send(w.at[u, (z + k) % 4, x, c, :, half(y)], self.rz.at[slot, k - 1], 4 + k, p.along_z(k))
                 for k in (1, 2, 3)
             ]
-        there = self.own.at[u, :, half(y if mine else 1 - y)]
+        there = self.own.at[unit_of(n), :, half(y if mine else 1 - y)]
         return [send(there, there, 8, p.across_y())]
 
     def add(self, stage, n):
         p, w = self.p, self.w
-        u = unit_of(n)
-        slot = n % 2
+        u = held_in(n)
+        slot = n % GAP
         y, z, x, c = p.y, p.z, p.x, p.c
         f = lambda value: value.astype(F32)
         if stage == 1:
 
             def piece(zz, carry):
-                w[u, zz, :, c] = (f(w[u, zz, :, c]) + f(self.rc[slot, zz])).astype(BF)
+                w[u, zz, :, c] = (f(w[u, zz, :, c]) + f(self.rc[n % 2, zz])).astype(BF)
                 return carry
 
             lax.fori_loop(0, 4, piece, 0)
@@ -395,7 +405,7 @@
             total = f(w[u, z, x, c, :, half(y)])
             for k in (0, 1, 2):
                 total = total + f(self.rz[slot, k])
-            self.own[u, :, half(y)] = total.astype(BF)
+            self.own[unit_of(n), :, half(y)] = total.astype(BF)
 
     def step(self, stage, n):
         if stage > 0:
@@ -408,41 +418,111 @@
             for copy in self.copies(stage, n, True):
                 copy.start()
 
-    def tick(self, t):
+    def half_tick(self, m, odd):
         for stage in (5, 4, 3, 2, 1, 0):
-            n = t - stage
-            if isinstance(t, int):
-                if 0 <= n < UNITS:
-                    self.step(stage, n)
-            else:
-                pl.when((n >= 0) & (n < UNITS))(functools.partial(self.step, stage, n))
+            if REDUCE_AT[stage] % 2 == odd:
+                place = m - REDUCE_AT[stage] // 2
+                if isinstance(place, int):
+                    if place in PLACES:
+                        self.step(stage, PLACES.index(place))
+                else:
+                    late = (place >= 11) & (place < 20) & ((place - 11) % 4 == 0)
+                    n = jnp.where(place < 9, place, 9 + (place - 11) // 4)
+                    pl.when(((place >= 0) & (place < 9)) | late)(functools.partial(self.step, stage, n))
+
+
+PLACES = (0, 1, 2, 3, 4, 5, 6, 7, 8, 11, 15, 19)
 
 
 def unit_of(n):
     if isinstance(n, int):
-        return 8 + n if n < 4 else n if n < 8 else 3 if n == 8 else n - 9
-    return jnp.where(n < 4, 8 + n, jnp.where(n < 8, n, jnp.where(n == 8, 3, n - 9)))
-
-
-def small_sum(place, value, stage_ref, land_ref, z_ref, sems, with_y):
-    steps = [(0, place.twin()), (1, place.across_x())] + ([(2, place.across_y())] if with_y else [])
-    for i, device in steps:
-        stage_ref[i] = value
-        copy = remote(stage_ref.at[i], land_ref.at[i], sems, 0, i, device)
-        copy.start()
-        copy.wait()
-        value = value + land_ref[i]
-    z_ref[0] = value
-    sent = [remote(z_ref.at[0], z_ref.at[k], sems, 0, 2 + k, place.along_z(k)) for k in (1, 2, 3)]
-    for copy in sent:
-        copy.start()
-    for copy in sent:
-        copy.wait()
+        return 4 + n if n < 8 else 3 if n == 8 else n - 9
+    return jnp.where(n < 8, 4 + n, jnp.where(n == 8, 3, n - 9))
+
+
+def held_in(n):
+    if isinstance(n, int):
+        return 4 + n if n < 8 else 3 if n == 8 else n - 5
+    return jnp.where(n < 8, 4 + n, jnp.where(n == 8, 3, n - 5))
+
+
+def assemble(tile, pieces, load):
     total = None
-    for zz in range(4):
-        part = z_ref[(place.z + 4 - zz) % 4]
-        total = part if total is None else total + part
+    for dst, key, src, length in pieces:
+        at = max(dst, 128 * tile)
+        while at < min(dst + length, 128 * tile + 128):
+            lane = src + at - dst
+            count = min(dst + length, 128 * tile + 128, at + 128 - lane % 128) - at
+            value = load(key, lane // 128)
+            shift = (at - lane) % 128
+            value = value if shift == 0 else pltpu.roll(value, shift, 1)
+            lanes = iota(value.shape, 1)
+            low = at - 128 * tile
+            inside = (lanes >= low) & (lanes < low + count)
+            total = jnp.where(inside, value, 0.0 if total is None else total)
+            at += count
     return total
+
+
+def split_up(raw_ref, home_ref):
+    load = lambda key, t: raw_ref[:, 128 * t : 128 * t + 128].astype(F32)
+    for q in range(4):
+        pieces = [(PIECE * s, 0, 4 * PIECE * s + PIECE * q, PIECE) for s in range(16)]
+        for t in range(6):
+            home_ref[5 + 2 * q, :, 128 * t : 128 * t + 128] = assemble(t, pieces, load).astype(BF)
+
+
+def merge_up(own_ref, raw_ref):
+    load = lambda q, t: own_ref[5 + 2 * q, :, 128 * t : 128 * t + 128].astype(F32)
+    pieces = [(4 * PIECE * s + PIECE * q, q, PIECE * s, PIECE) for s in range(16) for q in range(4)]
+    for t in range(24):
+        here = [p for p in pieces if p[0] < 128 * t + 128 and p[0] + PIECE > 128 * t]
+        raw_ref[:, 128 * t : 128 * t + 128] = assemble(t, here, load).astype(BF)
+
+
+class Exchange:
+    def __init__(self, place, sent_ref, land_ref, sems, everywhere):
+        self.p, self.sent, self.land, self.sems, self.everywhere = place, sent_ref, land_ref, sems, everywhere
+
+    def copy(self, k, mine):
+        p = self.p
+        if self.everywhere:
+            count = 32
+            y, s = p.other(k)
+            src, me = self.sent.at[s], p.flat()
+        else:
+            count = 16
+            me = p.flat() % 16
+            y, s = p.y, (me + k) % 16
+            src = self.sent
+        return pltpu.make_async_remote_copy(
+            src_ref=src,
+            dst_ref=self.land.at[me if mine else (me + count - k) % count],
+            send_sem=self.sems.at[0, k],
+            recv_sem=self.sems.at[1, k],
+            device_id=(y, s),
+            device_id_type=MESH,
+        )
+
+    def start(self):
+        def send(k, carry):
+            self.copy(k, True).start()
+            return carry
+
+        lax.fori_loop(1, self.land.shape[0], send, 0)
+
+    def finish(self):
+        def wait(k, carry):
+            self.copy(k, False).wait_recv()
+            self.copy(k, True).wait_send()
+            return carry
+
+        lax.fori_loop(1, self.land.shape[0], wait, 0)
+
+
+def own_part(value, s):
+    load = lambda key, t: value[:, 128 * t : 128 * t + 128]
+    return assemble(0, [(0, 0, PIECE * s, PIECE)], load)
 
 
 def history_kernel(mix_ref, history_ref, g_ref, grad_ref, earlier_ref, terms_ref):
@@ -551,17 +631,12 @@
     lax.fori_loop(0, x_ref.shape[0] // height, chunk, 0)
 
 
-def down_pieces():
-    return [(x, c, q) for x in (0, 1) for c in (0, 1) for q in range(4)]
-
-
-def feed_forward(z, act_ref, actt_ref, gb_ref, w_ref, hid_ref, gu_ref, out_ref, dact_ref):
+def feed_forward(z, act_ref, actt_ref, gb_ref, w_ref, hid_ref, gu_ref, out_ref, dact_ref, after):
     height = 256
 
     def chunk(r, carry):
         at = rows(r * height, height)
-        up = unit(w_ref, 8 + z)
-        down = jnp.concatenate([w_ref[4 + q, z, x, c] for x, c, q in down_pieces()], axis=0)
+        down, up = unit(w_ref, 4 + 2 * z), unit(w_ref, 5 + 2 * z)
         hidden, slope = gelu_parts(dot(act_ref[at, :], up))
         hidden = hidden.astype(BF)
         hid_ref[at, :] = hidden
@@ -569,13 +644,12 @@
         gu_ref[at, :] = gu
         out_ref[at, :] += dot(hidden, down)
         dact_ref[at, :] += dot_bt(gu, up)
+        after(r)
         return carry
 
     lax.fori_loop(0, act_ref.shape[0] // height, chunk, 0)
-    grad = dot_at(hid_ref[...], gb_ref[...]).astype(BF)
-    for i, (x, c, q) in enumerate(down_pieces()):
-        w_ref[4 + q, z, x, c] = grad[48 * i : 48 * i + 48]
-    w_ref[8 + z] = dot(actt_ref[...], gu_ref[...]).astype(BF).reshape(w_ref.shape[1:])
+    w_ref[4 + 2 * z] = dot_at(hid_ref[...], gb_ref[...]).astype(BF).reshape(w_ref.shape[1:])
+    w_ref[5 + 2 * z] = dot(actt_ref[...], gu_ref[...]).astype(BF).reshape(w_ref.shape[1:])
 
 
 def branch_grad(mix4, g_ref, gb_ref):
@@ -620,8 +694,9 @@
     w_ref[3] = dot_at(mixed_ref[...], ga_ref[...]).astype(BF).reshape(w_ref.shape[1:])
 
 
-def project_back(j, actt_ref, qkv_ref, w_ref, out_ref):
+def project_back(j, actt_ref, qkv_ref, w_ref, out_ref, grad_ref):
     height = 256
+    grad_ref[...] = dot(actt_ref[...], qkv_ref[:, cols(j * 768, 768)]).astype(BF).reshape(grad_ref.shape)
 
     def chunk(r, carry):
         at = rows(r * height, height)
@@ -629,22 +704,24 @@
         out_ref[at, :] = jnp.where(j == 0, 0.0, out_ref[at, :]) + share
         return carry
 
-    lax.fori_loop(0, qkv_ref.shape[0] // height, chunk, 0)
-    w_ref[j] = dot(actt_ref[...], qkv_ref[:, cols(j * 768, 768)]).astype(BF).reshape(w_ref.shape[1:])
-
-
-def first_back(x_ref, dact_ref, par_ref, dmid_ref, small_ref):
-    height = 128
+    @pl.when(j < 2)
+    def _():
+        lax.fori_loop(0, qkv_ref.shape[0] // height, chunk, 0)
+
+
+def first_back(x_ref, qkv_ref, w_ref, dact_ref, par_ref, dmid_ref, small_ref, after):
+    height = 256
     zero = jnp.zeros((8, x_ref.shape[1]), F32)
 
     def chunk(r, carry):
         gain, bias = carry
         at = rows(r * height, height)
-        dact = dact_ref[at, :]
+        dact = dact_ref[at, :] + dot_bt(qkv_ref[at, cols(2 * 768, 768)], unit(w_ref, 2))
         normed, inverse = norm_parts(x_ref[at, :].astype(F32))
         gain = gain + fold8(dact * normed)
         bias = bias + fold8(dact)
         dmid_ref[at, :] += norm_back(dact, normed, inverse, par_ref[0:1, :])
+        after(r, at)
         return gain, bias
 
     gain, bias = lax.fori_loop(0, x_ref.shape[0] // height, chunk, (zero, zero))
@@ -676,9 +753,10 @@
 
 def block_kernel(joined, *refs):
     if joined:
-        start_ref, mix_ref, x_hbm, g_hbm, earlier_hbm, par_in, terms_ref, table_ref, wq_hbm, wo_hbm, wu_hbm, wd_hbm = refs[:12]
-        next_hbm, dx_hbm, own_hbm, small_out = refs[12:16]
-        refs = refs[16:]
+        start_ref, mix_ref, x_hbm, g_hbm, earlier_hbm, gains_ref, biases_ref, terms_ref, table_ref = refs[:9]
+        wq_hbm, wo_hbm, wu_hbm, wd_hbm = refs[9:13]
+        next_hbm, dx_hbm, gq_hbm, go_hbm, gu_hbm, gd_hbm, small_out = refs[13:20]
+        refs = refs[20:]
     else:
         start_ref, mix_ref, x_hbm, g_hbm, earlier_hbm, par_in, terms_ref, table_ref, w_hbm = refs[:9]
         next_hbm, dx_hbm, grad_hbm, small_out = refs[9:13]
@@ -687,12 +765,13 @@
     w, bias, dq, cosine, sine, small, par, loads = refs[15:23]
     start = start_ref[0]
     mix4 = mix_ref[4]
+    length = x.shape[0]
 
     load = lambda src, dst, i: pltpu.make_async_copy(src, dst, loads.at[i])
     first = [load(x_hbm, x, 0)]
     later = [load(g_hbm, g, 1), load(earlier_hbm, earlier, 2)]
     if joined:
-        own, rc, rdx, rdy, rxx, rxy, rz, stage_ref, land_ref, z_ref, gsems, rsems, ssems = refs[23:]
+        own, rc, rdx, rdy, rxx, rxy, rz, raw, msg_p, land_p, msg_g, land_g, gsems, rsems, psems, ssems = refs[23:]
         place = Place()
         home = w.at[:, place.z, place.x, place.c]
         for j in range(3):
@@ -701,10 +780,11 @@
                     load(wq_hbm.at[:, pl.ds(768 * t + 256 * j, 256)], home.at[j, :, pl.ds(256 * t, 256)], 3 + 3 * j + t)
                 )
         first.append(load(wo_hbm, home.at[3], 12))
-        first.append(load(wd_hbm, home.at[4:8], 13))
         for k in range(4):
-            first.append(load(wu_hbm.at[:, pl.ds(768 * k, 768)], home.at[8 + k], 14 + k))
+            first.append(load(wd_hbm.at[k], home.at[4 + 2 * k], 13 + k))
+        first.append(load(wu_hbm, raw, 17))
     else:
+        spare = refs[23]
         first.append(load(w_hbm, w, 3))
     for copy in first + later:
         copy.start()
@@ -712,115 +792,161 @@
         for copy in first[1:]:
             copy.wait()
         barrier = pltpu.get_barrier_semaphore()
-        for peer in place.peers():
-            pl.semaphore_signal(barrier, inc=1, device_id=peer, device_id_type=MESH)
-        pl.semaphore_wait(barrier, 6)
-        gather = Gather(place, w, gsems)
-        reduce = Reduce(place, w, own, rc, rdx, rdy, rxx, rxy, rz, rsems)
-        gather.tick(0)
+
+        def greet(k, carry):
+            pl.semaphore_signal(barrier, inc=1, device_id=place.other(k), device_id_type=MESH)
+            return carry
+
+        lax.fori_loop(1, 32, greet, 0)
+        pl.semaphore_wait(barrier, 31)
+        gather = Gather(place, w, gsems).half_tick
+        reduce = Reduce(place, w, own, rc, rdx, rdy, rxx, rxy, rz, rsems).half_tick
+        params = Exchange(place, msg_p, land_p, psems, False)
+        sums = Exchange(place, msg_g, land_g, ssems, True)
+        gather(0, 0)
+        msg_p[...] = jnp.zeros_like(msg_p)
+        msg_p[0:2, 0:PIECE] = gains_ref[...].astype(F32)
+        msg_p[2:4, 0:PIECE] = biases_ref[...].astype(F32)
+        params.start()
+        land_p[place.flat() % 16] = msg_p[...]
+        fill_tables(table_ref, cosine, sine)
+        gather(1, 0)
+        split_up(raw, home)
     else:
+        gather = reduce = lambda m, odd: None
         first[1].wait()
-    first[0].wait()
-    if joined:
-        par[...] = small_sum(place, par_in[...], stage_ref.at[0], land_ref.at[0], z_ref.at[0], ssems.at[0], False)
-        gather.tick(1)
-    else:
         par[...] = par_in[...]
+        fill_tables(table_ref, cosine, sine)
     small[...] = jnp.zeros_like(small)
-    first_norm(x, par, act1)
-    fill_tables(table_ref, cosine, sine)
-    if joined:
-        gather.tick(2)
-    fill_bias(start, bias, x.shape[0] // BL, False)
-    for copy in later:
+    fill_bias(start, bias, length // BL, False)
+    gather(2, 0)
+    gather(2, 1)
+    for copy in [first[0]] + later:
         copy.wait()
     branch_grad(mix4, g, gb)
     if joined:
-        gather.tick(3)
-        gather.tick(4)
+        params.finish()
+        pieces = [(PIECE * s, s, 0, PIECE) for s in range(16)]
+        for t in range(6):
+            here = [p for p in pieces if p[0] < 128 * t + 128 and p[0] + PIECE > 128 * t]
+            par[:, 128 * t : 128 * t + 128] = assemble(t, here, lambda s, _: land_p[s])
+    gather(3, 0)
+    gather(3, 1)
+    first_norm(x, par, act1)
+    gather(4, 0)
+    gather(4, 1)
 
     def forward_group(j, carry):
         project(j, act1, w, cosine, sine, qkv)
 
         def inner(i, carry):
-            forward_pair(2 * j + i, start, qkv, bias, mixed, lse)
-            if joined:
-                gather.tick(5 + 2 * j + i)
+            m = 5 + 2 * j + i
+            forward_pair(
+                2 * j + i, start, qkv, bias, mixed, lse, lambda b: gather(m, b // 2) if b % 2 else None
+            )
             return carry
 
         return lax.fori_loop(0, 2, inner, carry)
 
     lax.fori_loop(0, 3, forward_group, 0)
     attention_out(x, mixed, w, par, middle, act2, actt, out, dact)
-    if joined:
-        gather.tick(11)
 
     def ff_group(z, carry):
-        if joined:
-            gather.tick(12 + z)
-        feed_forward(z, act2, actt, gb, w, hid, gu, out, dact)
-        if joined:
-            reduce.tick(z)
+        def after(r):
+            for odd in (0, 1):
+
+                @pl.when(r % 2 == odd)
+                def _():
+                    gather(11 + 2 * z + r // 2, odd)
+                    reduce(2 * z - 2 + r // 2, odd)
+
+        feed_forward(z, act2, actt, gb, w, hid, gu, out, dact, after if joined else lambda r: None)
         return carry
 
     lax.fori_loop(0, 4, ff_group, 0)
-    if joined:
-        reduce.tick(4)
+    reduce(6, 0)
     ga, do, nxt = gb, act2, earlier
     middle_back(mix4, g, earlier, middle, out, dact, mixed, w, par, nxt, ga, do, small)
     store_next = load(nxt, next_hbm, 0)
     store_next.start()
-    if joined:
-        reduce.tick(5)
-    fill_bias(start, bias, x.shape[0] // BL, True)
+    reduce(6, 1)
+    fill_bias(start, bias, length // BL, True)
     actt[...] = act1[...].T
 
     def backward_group(j, carry):
         def inner(i, carry):
-            backward_pair(2 * j + i, start, qkv, do, mixed, lse, cosine, sine, bias, dq)
+            m = 7 + 2 * (2 * j + i)
+            backward_pair(
+                2 * j + i, start, qkv, do, mixed, lse, cosine, sine, bias, dq, lambda b: reduce(m + b // 2, b % 2)
+            )
 
             @pl.when(i == 1)
             def _():
-                project_back(j, actt, qkv, w, out)
-
-            if joined:
-                reduce.tick(6 + 2 * j + i)
+                project_back(j, actt, qkv, w, out, w.at[4 + j] if joined else spare.at[j])
+
             return carry
 
         return lax.fori_loop(0, 2, inner, carry)
 
     lax.fori_loop(0, 3, backward_group, 0)
-    first_back(x, out, par, dact, small)
-    store_dx = load(dact, dx_hbm, 1)
-    store_dx.start()
+    reduce(19, 0)
+
+    def store_dx(r, at):
+        reduce(19 + r, 1)
+        reduce(20 + r, 0)
+
+    first_back(x, qkv, w, out, par, dact, small, store_dx)
+    stores = [load(dact, dx_hbm, 1)]
+    stores[0].start()
+    totals = jnp.sum(terms_ref[...], axis=1, keepdims=True)
+    lane = iota((1, 128), 1)
+    mix_row = jnp.where(lane == 4, jnp.sum(small[5:6, :], axis=1, keepdims=True), 0.0)
     for k in range(4):
-        small[4:5, 128 * k : 128 * k + 128] = fold_lanes(terms_ref[k : k + 1, :])
-    small[4:5, 512:640] = fold_lanes(small[5:6, :])
-    small[5:6, :] = jnp.zeros_like(small[5:6, :])
+        mix_row = jnp.where(lane == k, totals[k : k + 1, :], mix_row)
     if joined:
-        reduce.tick(12)
-        small_out[...] = small_sum(place, small[...], stage_ref.at[1], land_ref.at[1], z_ref.at[1], ssems.at[1], True)
-        for t in range(13, LAST):
-            reduce.tick(t)
-        store_grad = load(own, own_hbm, 2)
+        values = small[...]
+        for s in range(16):
+            msg_g[s] = own_part(values, s)
+            msg_g[s, 4:5, :] = mix_row
+        sums.start()
+        land_g[place.flat()] = msg_g[place.flat() % 16]
+        merge_up(own, raw)
+        stores += [load(own.at[3], go_hbm, 2), load(raw, gu_hbm, 3)]
+        stores += [load(own.at[4 + 2 * k], gd_hbm.at[k], 4 + k) for k in range(4)]
+        for copy in stores[1:]:
+            copy.start()
+        reduce(23, 1)
+        reduce(24, 0)
+        sums.finish()
+
+        def add(k, total):
+            return total + land_g[k]
+
+        small_out[...] = lax.fori_loop(0, 32, add, jnp.zeros(small_out.shape, F32))
+        reduce(24, 1)
+        reduce(25, 0)
+        units = [
+            load(own.at[j, :, pl.ds(256 * t, 256)], gq_hbm.at[:, pl.ds(768 * t + 256 * j, 256)], 8 + 3 * j + t)
+            for j in range(3)
+            for t in range(3)
+        ]
+        for copy in units:
+            copy.start()
+        stores += units
     else:
+        small[4:5, 0:128] = mix_row
+        small[4:5, 128:] = jnp.zeros_like(small[4:5, 128:])
         small_out[...] = small[...]
-        store_grad = load(w, grad_hbm, 2)
-    store_grad.start()
+        stores += [load(spare, grad_hbm.at[0:3], 2), load(w.at[3:], grad_hbm.at[3:], 3)]
+        for copy in stores[1:]:
+            copy.start()
     store_next.wait()
-    store_dx.wait()
-    store_grad.wait()
-
-
-def fold_lanes(row):
-    total = row[:, 0:128]
-    for i in range(1, row.shape[1] // 128):
-        total = total + row[:, 128 * i : 128 * i + 128]
-    return total
+    for copy in stores:
+        copy.wait()
 
 
 VMEM_LIMIT = 67043328
-UNIT = (4, 2, 2, 48, 768)
+UNIT = (4, 2, 2, PIECE, 768)
 
 
 def block_pass(joined, start, mix, x, g, earlier, par, terms, *weights):
@@ -844,93 +970,96 @@
         pltpu.VMEM(small, F32),
         dma((18,)),
     ]
-    grads = (UNITS,) + UNIT
+    grads = [((UNITS,) + UNIT, BF), (small, F32)]
     if joined:
-        grads = (UNITS, 48, width)
+        grads = [
+            ((PIECE, 3 * width), BF), ((PIECE, width), BF), ((PIECE, 4 * width), BF), ((4, PIECE, width), BF), ((8, 128), F32)
+        ]
         scratch += [
-            pltpu.VMEM(grads, BF),
-            pltpu.VMEM((2, 4, 2, 48, width), BF),
-            pltpu.VMEM((2, 2, 48, width // 2), BF),
-            pltpu.VMEM((2, 2, 48, width // 2), BF),
-            pltpu.VMEM((2, 4, 48, width // 2), BF),
-            pltpu.VMEM((2, 4, 48, width // 2), BF),
-            pltpu.VMEM((2, 3, 48, width // 2), BF),
-            pltpu.VMEM((2, 3) + small, F32),
-            pltpu.VMEM((2, 3) + small, F32),
-            pltpu.VMEM((2, 4) + small, F32),
-            dma((2, 2, 8)),
-            dma((2, 2, 9)),
-            dma((2, 2, 1, 6)),
+            pltpu.VMEM((UNITS, PIECE, width), BF),
+            pltpu.VMEM((2, 4, 2, PIECE, width), BF),
+            pltpu.VMEM((GAP, 2, PIECE, width // 2), BF),
+            pltpu.VMEM((GAP, 2, PIECE, width // 2), BF),
+            pltpu.VMEM((GAP, 4, PIECE, width // 2), BF),
+            pltpu.VMEM((GAP, 4, PIECE, width // 2), BF),
+            pltpu.VMEM((GAP, 3, PIECE, width // 2), BF),
+            pltpu.VMEM((PIECE, 4 * width), BF),
+            pltpu.VMEM((8, 128), F32),
+            pltpu.VMEM((16, 8, 128), F32),
+            pltpu.VMEM((16, 8, 128), F32),
+            pltpu.VMEM((32, 8, 128), F32),
+            dma((2, UNITS, 8)),
+            dma((2, GAP, 9)),
+            dma((2, 16)),
+            dma((2, 32)),
         ]
+    else:
+        scratch += [pltpu.VMEM((3,) + UNIT, BF)]
     params = dict(vmem_limit_bytes=VMEM_LIMIT)
     if joined:
         params.update(collective_id=0, has_side_effects=True)
+    outs = [((length, width), BF), ((length, width), F32)] + grads
     return pl.pallas_call(
         functools.partial(block_kernel, joined),
-        in_specs=[smem, smem, anys, anys, anys, vmem, vmem, vmem] + [anys] * len(weights),
-        out_specs=(anys, anys, anys, vmem),
-        out_shape=(
-            jax.ShapeDtypeStruct((length, width), BF),
-            jax.ShapeDtypeStruct((length, width), F32),
-            jax.ShapeDtypeStruct(grads, BF),
-            jax.ShapeDtypeStruct(small, F32),
-        ),
+        in_specs=[smem, smem, anys, anys, anys] + [vmem] * (len(par) + 2) + [anys] * len(weights),
+        out_specs=[anys] * (len(outs) - 1) + [vmem],
+        out_shape=[jax.ShapeDtypeStruct(shape, dtype) for shape, dtype in outs],
         scratch_shapes=scratch,
         compiler_params=pltpu.CompilerParams(**params),
         name="block_pass",
-    )(start, mix, x, g, earlier, par, terms, rotary_table(length), *weights)
+    )(start, mix, x, g, earlier, *par, terms, rotary_table(length), *weights)
 
 
 def to_units(wq, wo, wu, wd):
     d = wo.shape[0]
+    down = wd.reshape(16, 4, PIECE, d).transpose(1, 0, 2, 3).reshape(4, d, d)
+    up = wu.reshape(d, 16, 4, PIECE).transpose(2, 0, 1, 3).reshape(4, d, d)
     parts = [
         wq.reshape(d, 3, 3, 256).transpose(2, 0, 1, 3).reshape(3, d, d),
         wo[None],
-        wd.reshape(16, 4, 48, d).transpose(1, 0, 2, 3).reshape(4, d, d),
-        wu.reshape(d, 4, d).transpose(1, 0, 2),
+        jnp.stack([down, up], axis=1).reshape(8, d, d),
     ]
     return jnp.concatenate(parts).reshape((UNITS,) + UNIT)
 
 
-def from_units(units, height):
+def from_units(units):
     d = units.shape[-1]
-    units = units.reshape(UNITS, -1, d)
-    r = units.shape[1]
-    gq = units[0:3].reshape(3, r, 3, 256).transpose(1, 2, 0, 3).reshape(r, 3 * d)
-    gd = units[4:8].reshape(4, r // height, height, d).transpose(1, 0, 2, 3).reshape(4 * r, d)
-    return gq, units[3], units[8:12].transpose(1, 0, 2).reshape(r, 4 * d), gd
+    units = units.reshape(UNITS, d, d)
+    gq = units[0:3].reshape(3, d, 3, 256).transpose(1, 2, 0, 3).reshape(d, 3 * d)
+    both = units[4:].reshape(4, 2, d, d)
+    gd = both[:, 0].reshape(4, 16, PIECE, d).transpose(1, 0, 2, 3).reshape(4 * d, d)
+    gu = both[:, 1].reshape(4, d, 16, PIECE).transpose(1, 2, 0, 3).reshape(d, 4 * d)
+    return gq, units[3], gu, gd
 
 
 def local(block_input, history, cotangent, span_start, w_qkv, w_out, w_up, w_down, ln_gains, ln_biases, mix_weights, joined):
-    shard = lax.axis_index("shard")
     width = block_input.shape[1]
     own = ln_gains.shape[1]
     grad_history, earlier, terms = history_pass(mix_weights, history, cotangent)
-    mine = jnp.concatenate([ln_gains, ln_biases]).astype(F32)
     if joined:
-        par = lax.dynamic_update_slice(jnp.zeros((8, width), F32), mine, (0, shard * own))
-        nxt, grad_input, units, small = block_pass(
-            True, span_start, mix_weights, block_input, cotangent, earlier, par, terms,
+        nxt, grad_input, gq, go, gu, gd, small = block_pass(
+            True, span_start, mix_weights, block_input, cotangent, earlier, [ln_gains, ln_biases], terms,
             w_qkv, w_out, w_up, w_down.reshape(4, own, width),
         )
-        gq, go, gu, gd = [item.astype(F32) for item in from_units(units, own)]
-        norm_grads = lax.dynamic_slice(small, (0, shard * own), (4, own))
-        grad_mix = jnp.sum(small[4, : 5 * 128].reshape(5, 128), axis=1)
+        gq, go, gu, gd = [item.astype(F32) for item in (gq, go, gu, gd.reshape(4 * own, width))]
+        norm_grads = small[:4, :own]
+        grad_mix = small[4, :5]
     else:
         gather = lambda item, axis: lax.all_gather(item, "shard", axis=axis, tiled=True)
-        par = jnp.concatenate([gather(mine.astype(BF), 1).astype(F32), jnp.zeros((4, width), F32)])
+        mine = jnp.concatenate([ln_gains, ln_biases])
+        par = jnp.concatenate([gather(mine, 1).astype(F32), jnp.zeros((4, width), F32)])
         weights = to_units(gather(w_qkv, 0), gather(w_out, 0), gather(w_up, 0), gather(w_down, 0))
         nxt, grad_input, units, small = block_pass(
-            False, span_start, mix_weights, block_input, cotangent, earlier, par, terms, weights
+            False, span_start, mix_weights, block_input, cotangent, earlier, [par], terms, weights
         )
 
         def owned(item, axis):
             part = lax.psum_scatter(item.astype(BF), "shard", scatter_dimension=axis, tiled=True)
             return lax.psum(part, "rep").astype(F32)
 
-        gq, go, gu, gd = [owned(item, 0) for item in from_units(units, 48)]
+        gq, go, gu, gd = [owned(item, 0) for item in from_units(units)]
         norm_grads = owned(small[:4], 1)
-        grad_mix = lax.psum(jnp.sum(small[4, : 5 * 128].reshape(5, 128), axis=1), ("rep", "shard"))
+        grad_mix = lax.psum(small[4, :5], ("rep", "shard"))
     return nxt, grad_input, grad_history, grad_mix, gq, go, gu, gd, norm_grads[0:2], norm_grads[2], norm_grads[3]
 
 

time: 253 us -> 234 us (0.925)
  Pallas kernels: 237 us -> 218 us
  local copies, waits for them, and re-layouts: 11.2 us -> 7.87 us
  other arithmetic: 3.2 us -> 6.03 us
    pallas_call x1, Pallas kernels: 226 us -> 208 us  [block_pass(): pl.pallas_call(functools.partial(block_kernel, joined), in_specs=[smem, s...]
    convert_element_type x4, other arithmetic: 2.52 us -> 6.03 us  [local(): item.astype(F32)]
where the time goes in v3:
time: 234 us
  Pallas kernels  218 us (93%)
  local copies, waits for them, and re-layouts  7.87 us (3%)
  other arithmetic  6.03 us (3%)
    pallas_call x1, Pallas kernels, block_pass(): pl.pallas_call(functools.partial(block_kernel, joined), in_specs=[smem, s...  208 us
    pallas_call x1, Pallas kernels, history_pass(): pl.pallas_call(history_kernel, grid=(length // height,), in_specs=[pl.Blo...  10.4 us
    convert_element_type x4, other arithmetic, local(): item.astype(F32)  6.03 us

profile of v3, /device:TPU:0, one launch (start us, length us, event | category | flops | bytes accessed | tf_op | source)
XLA Modules:
  0.0 233.6 jit_solution(1455757433572469447)
XLA Ops:
  0.6 10.4 %history_pass.1 = (f32[4,1024,768]{2,1,0:T(8,128)}, bf16[1024,768]{1,0:T(8,128)(2,1)}, f32[8,768]{1,0:T(8,128)}) custom-call(f32[5]{0:T(128)} %refs_1_.1, bf16[4,1024,768]{2,1,0:T(8,128)(2,1)} %history_ref.1, bf16[1024,768]{1,0:T(8,128)(2,1)} %refs_3_.1), custom_call_target="tpu_custom_call" | custom-call | tf_op jit(solution)/shard_map/history_pass/pallas_call | solution.py:553
  11.6 208.0 %block_pass.1 = (bf16[1024,768]{1,0:T(8,128)(2,1)}, f32[1024,768]{1,0:T(8,128)}, bf16[48,2304]{1,0:T(8,128)(2,1)}, bf16[48,768]{1,0:T(8,128)(2,1)}, bf16[48,3072...) custom-call(s32[1]{0:T(128)S(6)} %copy.25.refs_0_, f32[5]{0:T(128)} %refs_1_.1, ...), custom_call_target="tpu_custom_call" | custom-call | tf_op jit(solution)/shard_map/block_pass/pallas_call | solution.py:1002
  219.6 0.0 copy-start.2
  219.7 0.0 copy-start.1
  219.7 1.3 slice_bitcast_fusion
  221.0 1.2 slice.17
  222.2 1.2 slice_bitcast_fusion.2
  223.4 1.8 bitcast_convert_fusion
  225.2 1.8 convert_element_type.17
  227.0 1.7 convert_element_type.15
  228.8 0.0 copy-done.2
  228.8 0.7 convert_element_type.16
  229.4 0.0 copy-done.1
  229.4 0.0 copy-start
  229.4 1.1 copy.26
  230.6 1.3 copy-done
  231.9 1.7 copy.27
Async XLA Ops:
  219.6 9.1 %copy-start.2 = (bf16[48,768]{1,0:T(8,128)(2,1)S(1)}, bf16[48,768]{1,0:T(8,128)(2,1)}, u32[]{:S(2)}) copy-start(bf16[48,768]{1,0:T(8,128)(2,1)} %get-tuple-element.28) | copy-start | bytes 221188
  219.7 9.8 %copy-start.1 = (bf16[1024,768]{1,0:T(8,128)(2,1)S(1)}, bf16[1024,768]{1,0:T(8,128)(2,1)}, u32[]{:S(2)}) copy-start(bf16[1024,768]{1,0:T(8,128)(2,1)} %get-tuple-element.44) | copy-start | bytes 4718596
  229.4 2.5 %copy-start = (f32[1024,768]{1,0:T(8,128)S(1)}, f32[1024,768]{1,0:T(8,128)}, u32[]{:S(2)}) copy-start(f32[1024,768]{1,0:T(8,128)} %get-tuple-element.45) | copy-start | bytes 9437188

commit v4 on v3

--- a/solution.py
+++ b/solution.py
@@ -250,8 +250,14 @@
 UNITS = 12
 PIECE = 48
 GAP = 4
-GATHER_AT = (0, 2, 5, 7, 9)
-REDUCE_AT = (0, 2, 5, 7, 10, 12)
+GATHER_AT = (-1, 7, 12, 16, 19)
+GATHER_FROM = (4, 2, 2, 2, 2)
+REDUCE_AT = (0, 2, 6, 11, 15, 18)
+LATE_BEAT, LAST_BEAT = 11, 15
+
+
+def at_tick(stages, beat, phase):
+    return [(stage, beat - at // 4) for stage, at in reversed(list(enumerate(stages))) if at % 4 == phase]
 
 
 class Place:
@@ -336,15 +342,9 @@
             for copy in self.copies(stage, u, True):
                 copy.start()
 
-    def half_tick(self, m, odd):
-        for stage in (4, 3, 2, 1, 0):
-            if GATHER_AT[stage] % 2 == odd:
-                u = m - GATHER_AT[stage] // 2
-                if isinstance(u, int):
-                    if 0 <= u < UNITS:
-                        self.step(stage, u)
-                else:
-                    pl.when((u >= 0) & (u < UNITS))(functools.partial(self.step, stage, u))
+    def tick(self, beat, phase):
+        for stage, u in at_tick(GATHER_AT, beat, phase):
+            pl.when((u >= GATHER_FROM[stage]) & (u < UNITS))(functools.partial(self.step, stage, u))
 
 
 class Reduce:
@@ -390,13 +390,13 @@
         if stage == 1:
 
             def piece(zz, carry):
-                w[u, zz, :, c] = (f(w[u, zz, :, c]) + f(self.rc[n % 2, zz])).astype(BF)
+                w[u, zz, :, c] = w[u, zz, :, c] + self.rc[n % 2, zz]
                 return carry
 
             lax.fori_loop(0, 4, piece, 0)
         if stage == 2:
-            w[u, 0:2, x, c, :, half(1 - y)] = (f(w[u, 0:2, x, c, :, half(1 - y)]) + f(self.rdx[slot])).astype(BF)
-            w[u, 2:4, 1 - x, c, :, half(y)] = (f(w[u, 2:4, 1 - x, c, :, half(y)]) + f(self.rdy[slot])).astype(BF)
+            w[u, 0:2, x, c, :, half(1 - y)] = w[u, 0:2, x, c, :, half(1 - y)] + self.rdx[slot]
+            w[u, 2:4, 1 - x, c, :, half(y)] = w[u, 2:4, 1 - x, c, :, half(y)] + self.rdy[slot]
         if stage == 3:
             w[u, :, x, c, :, half(y)] = (
                 f(w[u, :, x, c, :, half(y)]) + f(self.rxx[slot]) + f(self.rxy[slot])
@@ -418,20 +418,17 @@
             for copy in self.copies(stage, n, True):
                 copy.start()
 
-    def half_tick(self, m, odd):
-        for stage in (5, 4, 3, 2, 1, 0):
-            if REDUCE_AT[stage] % 2 == odd:
-                place = m - REDUCE_AT[stage] // 2
-                if isinstance(place, int):
-                    if place in PLACES:
-                        self.step(stage, PLACES.index(place))
-                else:
-                    late = (place >= 11) & (place < 20) & ((place - 11) % 4 == 0)
-                    n = jnp.where(place < 9, place, 9 + (place - 11) // 4)
-                    pl.when(((place >= 0) & (place < 9)) | late)(functools.partial(self.step, stage, n))
-
-
-PLACES = (0, 1, 2, 3, 4, 5, 6, 7, 8, 11, 15, 19)
+    def tick(self, beat, phase):
+        for stage, place in at_tick(REDUCE_AT, beat, phase):
+            if isinstance(place, int):
+                if place == LAST_BEAT:
+                    self.step(stage, UNITS - 1)
+            else:
+                last = place == LAST_BEAT
+                late = place == LATE_BEAT
+                n = jnp.where(last, UNITS - 1, jnp.where(late, UNITS - 2, place))
+                here = ((place >= 0) & (place < UNITS - 2)) | late | last
+                pl.when(here)(functools.partial(self.step, stage, n))
 
 
 def unit_of(n):
@@ -472,12 +469,13 @@
             home_ref[5 + 2 * q, :, 128 * t : 128 * t + 128] = assemble(t, pieces, load).astype(BF)
 
 
-def merge_up(own_ref, raw_ref):
+def merge_up(own_ref, out_ref):
     load = lambda q, t: own_ref[5 + 2 * q, :, 128 * t : 128 * t + 128].astype(F32)
     pieces = [(4 * PIECE * s + PIECE * q, q, PIECE * s, PIECE) for s in range(16) for q in range(4)]
     for t in range(24):
         here = [p for p in pieces if p[0] < 128 * t + 128 and p[0] + PIECE > 128 * t]
-        raw_ref[:, 128 * t : 128 * t + 128] = assemble(t, here, load).astype(BF)
+        at = PIECE * (t // 6)
+        out_ref[at : at + PIECE, 128 * (t % 6) : 128 * (t % 6) + 128] = assemble(t, here, load)
 
 
 class Exchange:
@@ -525,51 +523,47 @@
     return assemble(0, [(0, 0, PIECE * s, PIECE)], load)
 
 
-def history_kernel(mix_ref, history_ref, g_ref, grad_ref, earlier_ref, terms_ref):
+def history_kernel(mix_ref, g_ref, grad_ref):
     g = g_ref[...].astype(F32)
-    earlier = None
-    parts = []
-    for k in range(history_ref.shape[0]):
-        h = history_ref[k].astype(F32)
+    for k in range(grad_ref.shape[0]):
         grad_ref[k] = mix_ref[k] * g
-        term = mix_ref[k] * h
-        earlier = term if earlier is None else earlier + term
-        parts.append(jnp.sum(fold8(h * g), axis=0, keepdims=True))
-    earlier_ref[...] = earlier.astype(BF)
-    new = jnp.concatenate(parts + [jnp.zeros((8 - len(parts), g.shape[1]), F32)], axis=0)
-
-    @pl.when(pl.program_id(0) == 0)
-    def _():
-        terms_ref[...] = new
-
-    @pl.when(pl.program_id(0) > 0)
-    def _():
-        terms_ref[...] += new
-
-
-def history_pass(mix, history, g):
-    past, length, width = history.shape
+
+
+def history_grad(mix, g, past):
+    length, width = g.shape
     height = 128
     return pl.pallas_call(
         history_kernel,
         grid=(length // height,),
-        in_specs=[
-            pl.BlockSpec(memory_space=pltpu.SMEM),
-            pl.BlockSpec((past, height, width), lambda i: (0, i, 0)),
-            pl.BlockSpec((height, width), lambda i: (i, 0)),
-        ],
-        out_specs=(
-            pl.BlockSpec((past, height, width), lambda i: (0, i, 0)),
-            pl.BlockSpec((height, width), lambda i: (i, 0)),
-            pl.BlockSpec((8, width), lambda i: (0, 0)),
-        ),
-        out_shape=(
-            jax.ShapeDtypeStruct((past, length, width), F32),
-            jax.ShapeDtypeStruct((length, width), BF),
-            jax.ShapeDtypeStruct((8, width), F32),
-        ),
-        name="history_pass",
-    )(mix, history, g)
+        in_specs=[pl.BlockSpec(memory_space=pltpu.SMEM), pl.BlockSpec((height, width), lambda i: (i, 0))],
+        out_specs=pl.BlockSpec((past, height, width), lambda i: (0, i, 0)),
+        out_shape=jax.ShapeDtypeStruct((past, length, width), F32),
+        name="history_grad",
+    )(mix, g)
+
+
+def average(mix_ref, history, g_ref, out_ref, next_ref, small_ref, after):
+    height = 256
+    past = len(history)
+    zero = jnp.zeros((8, g_ref.shape[1]), F32)
+
+    def chunk(r, terms):
+        at = rows(r * height, height)
+        g = g_ref[at, :].astype(F32)
+        output = out_ref[at, :]
+        total = mix_ref[past] * output
+        new = []
+        for k in range(past):
+            h = history[k][at, :].astype(F32)
+            total = total + mix_ref[k] * h
+            new.append(terms[k] + fold8(g * h))
+        next_ref[at, :] = total.astype(BF)
+        after(r)
+        return tuple(new) + (terms[past] + fold8(g * output),)
+
+    terms = lax.fori_loop(0, g_ref.shape[0] // height, chunk, (zero,) * (past + 1))
+    for k in range(past + 1):
+        small_ref[k : k + 1, :] = jnp.sum(terms[k], axis=0, keepdims=True)
 
 
 def first_norm(x_ref, par_ref, act_ref):
@@ -613,7 +607,7 @@
     lax.fori_loop(0, act_ref.shape[0] // height, chunk, 0)
 
 
-def attention_out(x_ref, mixed_ref, w_ref, par_ref, middle_ref, act_ref, actt_ref, out_ref, dact_ref):
+def attention_out(x_ref, mixed_ref, w_ref, par_ref, middle_ref, act_ref, actt_ref, out_ref, dact_ref, after):
     height = 256
 
     def chunk(r, carry):
@@ -626,6 +620,7 @@
         act = (normed * par_ref[1:2, :] + par_ref[3:4, :]).astype(BF)
         act_ref[at, :] = act
         actt_ref[:, rows(r * height, height)] = act.T
+        after(r)
         return carry
 
     lax.fori_loop(0, x_ref.shape[0] // height, chunk, 0)
@@ -663,65 +658,47 @@
     lax.fori_loop(0, g_ref.shape[0] // height, chunk, 0)
 
 
-def middle_back(mix4, g_ref, earlier_ref, middle_ref, out_ref, dact_ref, mixed_ref, w_ref, par_ref,
-                next_ref, ga_ref, do_ref, small_ref):
+def middle_back(mix4, g_ref, middle_ref, dact_ref, mixed_ref, w_ref, par_ref, ga_ref, do_ref, small_ref, after):
     height = 256
-    width = g_ref.shape[1]
-    zero = jnp.zeros((8, width), F32)
+    zero = jnp.zeros((8, g_ref.shape[1]), F32)
 
     def chunk(r, carry):
-        gain, bias, terms = carry
+        gain, bias = carry
         at = rows(r * height, height)
-        g = g_ref[at, :].astype(F32)
-        output = out_ref[at, :]
-        next_ref[at, :] = (earlier_ref[at, :].astype(F32) + mix4 * output).astype(BF)
-        terms = terms + fold8(g * output)
         normed, inverse = norm_parts(middle_ref[at, :])
         dact = dact_ref[at, :]
         gain = gain + fold8(dact * normed)
         bias = bias + fold8(dact)
-        grad = mix4 * g + norm_back(dact, normed, inverse, par_ref[1:2, :])
+        grad = mix4 * g_ref[at, :].astype(F32) + norm_back(dact, normed, inverse, par_ref[1:2, :])
         dact_ref[at, :] = grad
         low = grad.astype(BF)
         ga_ref[at, :] = low
         do_ref[at, :] = dot_bt(low, unit(w_ref, 3)).astype(BF)
-        return gain, bias, terms
-
-    gain, bias, terms = lax.fori_loop(0, g_ref.shape[0] // height, chunk, (zero, zero, zero))
+        after(r)
+        return gain, bias
+
+    gain, bias = lax.fori_loop(0, g_ref.shape[0] // height, chunk, (zero, zero))
     small_ref[1:2, :] = jnp.sum(gain, axis=0, keepdims=True)
     small_ref[3:4, :] = jnp.sum(bias, axis=0, keepdims=True)
-    small_ref[5:6, :] = jnp.sum(terms, axis=0, keepdims=True)
     w_ref[3] = dot_at(mixed_ref[...], ga_ref[...]).astype(BF).reshape(w_ref.shape[1:])
 
 
-def project_back(j, actt_ref, qkv_ref, w_ref, out_ref, grad_ref):
-    height = 256
-    grad_ref[...] = dot(actt_ref[...], qkv_ref[:, cols(j * 768, 768)]).astype(BF).reshape(grad_ref.shape)
-
-    def chunk(r, carry):
-        at = rows(r * height, height)
-        share = dot_bt(qkv_ref[at, cols(j * 768, 768)], unit(w_ref, j))
-        out_ref[at, :] = jnp.where(j == 0, 0.0, out_ref[at, :]) + share
-        return carry
-
-    @pl.when(j < 2)
-    def _():
-        lax.fori_loop(0, qkv_ref.shape[0] // height, chunk, 0)
-
-
-def first_back(x_ref, qkv_ref, w_ref, dact_ref, par_ref, dmid_ref, small_ref, after):
+def first_back(x_ref, qkv_ref, w_ref, par_ref, dmid_ref, small_ref, after):
     height = 256
     zero = jnp.zeros((8, x_ref.shape[1]), F32)
 
     def chunk(r, carry):
         gain, bias = carry
         at = rows(r * height, height)
-        dact = dact_ref[at, :] + dot_bt(qkv_ref[at, cols(2 * 768, 768)], unit(w_ref, 2))
+        dact = None
+        for j in range(3):
+            share = dot_bt(qkv_ref[at, cols(j * 768, 768)], unit(w_ref, j))
+            dact = share if dact is None else dact + share
         normed, inverse = norm_parts(x_ref[at, :].astype(F32))
         gain = gain + fold8(dact * normed)
         bias = bias + fold8(dact)
         dmid_ref[at, :] += norm_back(dact, normed, inverse, par_ref[0:1, :])
-        after(r, at)
+        after(r)
         return gain, bias
 
     gain, bias = lax.fori_loop(0, x_ref.shape[0] // height, chunk, (zero, zero))
@@ -753,25 +730,25 @@
 
 def block_kernel(joined, *refs):
     if joined:
-        start_ref, mix_ref, x_hbm, g_hbm, earlier_hbm, gains_ref, biases_ref, terms_ref, table_ref = refs[:9]
-        wq_hbm, wo_hbm, wu_hbm, wd_hbm = refs[9:13]
-        next_hbm, dx_hbm, gq_hbm, go_hbm, gu_hbm, gd_hbm, small_out = refs[13:20]
-        refs = refs[20:]
+        start_ref, mix_ref, x_hbm, g_hbm, history_hbm, gains_ref, biases_ref, table_ref = refs[:8]
+        wq_hbm, wo_hbm, wu_hbm, wd_hbm = refs[8:12]
+        next_hbm, dx_hbm, gq_hbm, go_hbm, gu_hbm, gd_hbm, mix_out, gains_out, first_out, second_out = refs[12:22]
+        refs = refs[22:]
     else:
-        start_ref, mix_ref, x_hbm, g_hbm, earlier_hbm, par_in, terms_ref, table_ref, w_hbm = refs[:9]
-        next_hbm, dx_hbm, grad_hbm, small_out = refs[9:13]
-        refs = refs[13:]
-    x, g, gb, act1, act2, actt, mixed, earlier, hid, gu, qkv, lse, middle, out, dact = refs[:15]
-    w, bias, dq, cosine, sine, small, par, loads = refs[15:23]
+        start_ref, mix_ref, x_hbm, g_hbm, history_hbm, par_in, table_ref, w_hbm = refs[:8]
+        next_hbm, dx_hbm, grad_hbm, small_out = refs[8:12]
+        refs = refs[12:]
+    x, g, gb, act1, act2, actt, mixed, nxt, hid, gu, qkv, lse, middle, out, dact = refs[:15]
+    w, bias, dq, cosine, sine, small, par, terms, loads = refs[15:24]
     start = start_ref[0]
     mix4 = mix_ref[4]
     length = x.shape[0]
 
     load = lambda src, dst, i: pltpu.make_async_copy(src, dst, loads.at[i])
     first = [load(x_hbm, x, 0)]
-    later = [load(g_hbm, g, 1), load(earlier_hbm, earlier, 2)]
+    later = [load(g_hbm, g, 1)]
     if joined:
-        own, rc, rdx, rdy, rxx, rxy, rz, raw, msg_p, land_p, msg_g, land_g, gsems, rsems, psems, ssems = refs[23:]
+        own, rc, rdx, rdy, rxx, rxy, rz, raw, msg_p, land_p, msg_g, land_g, gsems, rsems, psems, ssems = refs[24:]
         place = Place()
         home = w.at[:, place.z, place.x, place.c]
         for j in range(3):
@@ -784,7 +761,7 @@
             first.append(load(wd_hbm.at[k], home.at[4 + 2 * k], 13 + k))
         first.append(load(wu_hbm, raw, 17))
     else:
-        spare = refs[23]
+        spare = refs[24]
         first.append(load(w_hbm, w, 3))
     for copy in first + later:
         copy.start()
@@ -799,28 +776,29 @@
 
         lax.fori_loop(1, 32, greet, 0)
         pl.semaphore_wait(barrier, 31)
-        gather = Gather(place, w, gsems).half_tick
-        reduce = Reduce(place, w, own, rc, rdx, rdy, rxx, rxy, rz, rsems).half_tick
+        units = Gather(place, w, gsems)
+        gather = units.tick
+        reduce = Reduce(place, w, own, rc, rdx, rdy, rxx, rxy, rz, rsems).tick
         params = Exchange(place, msg_p, land_p, psems, False)
         sums = Exchange(place, msg_g, land_g, ssems, True)
-        gather(0, 0)
+        units.step(0, 0)
         msg_p[...] = jnp.zeros_like(msg_p)
         msg_p[0:2, 0:PIECE] = gains_ref[...].astype(F32)
         msg_p[2:4, 0:PIECE] = biases_ref[...].astype(F32)
         params.start()
         land_p[place.flat() % 16] = msg_p[...]
         fill_tables(table_ref, cosine, sine)
-        gather(1, 0)
         split_up(raw, home)
+        units.step(1, 0)
+        for u in (1, 2, 3):
+            units.step(0, u)
     else:
-        gather = reduce = lambda m, odd: None
+        gather = reduce = lambda beat, phase: None
         first[1].wait()
         par[...] = par_in[...]
         fill_tables(table_ref, cosine, sine)
     small[...] = jnp.zeros_like(small)
     fill_bias(start, bias, length // BL, False)
-    gather(2, 0)
-    gather(2, 1)
     for copy in [first[0]] + later:
         copy.wait()
     branch_grad(mix4, g, gb)
@@ -830,78 +808,124 @@
         for t in range(6):
             here = [p for p in pieces if p[0] < 128 * t + 128 and p[0] + PIECE > 128 * t]
             par[:, 128 * t : 128 * t + 128] = assemble(t, here, lambda s, _: land_p[s])
-    gather(3, 0)
-    gather(3, 1)
+        units.step(2, 0)
     first_norm(x, par, act1)
-    gather(4, 0)
-    gather(4, 1)
+    if joined:
+        units.step(3, 0)
+        units.step(1, 1)
+        units.step(4, 0)
 
     def forward_group(j, carry):
         project(j, act1, w, cosine, sine, qkv)
 
         def inner(i, carry):
-            m = 5 + 2 * j + i
-            forward_pair(
-                2 * j + i, start, qkv, bias, mixed, lse, lambda b: gather(m, b // 2) if b % 2 else None
-            )
+            p = 2 * j + i
+
+            def after(b):
+                for stage, pair, at in ((2, 0, 3), (3, 1, 2), (4, 1, 3)):
+                    if joined and b == at:
+                        pl.when(p == pair)(functools.partial(units.step, stage, 1))
+                gather(3 + p, b)
+
+            forward_pair(p, start, qkv, bias, mixed, lse, after)
             return carry
 
         return lax.fori_loop(0, 2, inner, carry)
 
     lax.fori_loop(0, 3, forward_group, 0)
-    attention_out(x, mixed, w, par, middle, act2, actt, out, dact)
+
+    def after_rows(r):
+        for phase in (0, 3):
+            pl.when(r == phase)(lambda: gather(r - phase + 9, phase))
+
+    attention_out(x, mixed, w, par, middle, act2, actt, out, dact, after_rows)
 
     def ff_group(z, carry):
         def after(r):
-            for odd in (0, 1):
-
-                @pl.when(r % 2 == odd)
-                def _():
-                    gather(11 + 2 * z + r // 2, odd)
-                    reduce(2 * z - 2 + r // 2, odd)
-
-        feed_forward(z, act2, actt, gb, w, hid, gu, out, dact, after if joined else lambda r: None)
+            @pl.when(r % 2 == 0)
+            def _():
+                gather(10 + 2 * z + r // 2, 0)
+                reduce(2 * z - 4 + r // 2, 0)
+
+            @pl.when(r % 2 == 1)
+            def _():
+                gather(10 + 2 * z + r // 2, 3)
+                reduce(2 * z - 4 + r // 2, 2)
+                reduce(2 * z - 4 + r // 2, 3)
+
+        feed_forward(z, act2, actt, gb, w, hid, gu, out, dact, after)
         return carry
 
     lax.fori_loop(0, 4, ff_group, 0)
-    reduce(6, 0)
-    ga, do, nxt = gb, act2, earlier
-    middle_back(mix4, g, earlier, middle, out, dact, mixed, w, par, nxt, ga, do, small)
-    store_next = load(nxt, next_hbm, 0)
-    store_next.start()
-    reduce(6, 1)
+
+    def after_middle(r):
+        for phase in (0, 2, 3):
+            pl.when(r == phase)(lambda: reduce(r - phase + 4, phase))
+
+    ga, do = gb, act2
+    middle_back(mix4, g, middle, dact, mixed, w, par, ga, do, small, after_middle)
     fill_bias(start, bias, length // BL, True)
     actt[...] = act1[...].T
+    history = [hid, gu, gb, act1]
+    past = [load(history_hbm.at[k], history[k], 12 + k) for k in range(4)]
+    for copy in past:
+        copy.start()
 
     def backward_group(j, carry):
         def inner(i, carry):
-            m = 7 + 2 * (2 * j + i)
-            backward_pair(
-                2 * j + i, start, qkv, do, mixed, lse, cosine, sine, bias, dq, lambda b: reduce(m + b // 2, b % 2)
-            )
+            p = 2 * j + i
+
+            def after(b):
+                early = p < 2
+                beat = jnp.where(early, 5 + p, 3 + 2 * p + b // 2)
+                if b == 0:
+                    reduce(beat, 0)
+                elif b == 2:
+                    pl.when(early)(lambda: reduce(beat, 2))
+                    pl.when(jnp.logical_not(early))(lambda: reduce(beat, 0))
+                else:
+                    pl.when(jnp.logical_not(early))(lambda: reduce(beat, 2))
+                    pl.when((b == 3) | jnp.logical_not(early))(lambda: reduce(beat, 3))
+
+            backward_pair(p, start, qkv, do, mixed, lse, cosine, sine, bias, dq, after)
 
             @pl.when(i == 1)
             def _():
-                project_back(j, actt, qkv, w, out, w.at[4 + j] if joined else spare.at[j])
+                grad = dot(actt[...], qkv[:, cols(j * 768, 768)]).astype(BF).reshape(UNIT)
+                if joined:
+                    w[4 + j] = grad
+                else:
+                    spare[j] = grad
 
             return carry
 
         return lax.fori_loop(0, 2, inner, carry)
 
     lax.fori_loop(0, 3, backward_group, 0)
-    reduce(19, 0)
-
-    def store_dx(r, at):
-        reduce(19 + r, 1)
-        reduce(20 + r, 0)
-
-    first_back(x, qkv, w, out, par, dact, small, store_dx)
-    stores = [load(dact, dx_hbm, 1)]
+    reduce(LAST_BEAT, 0)
+
+    def after_first(r):
+        @pl.when(r % 2 == 0)
+        def _():
+            reduce(LAST_BEAT + r // 2, 2)
+            reduce(LAST_BEAT + r // 2, 3)
+
+    first_back(x, qkv, w, par, dact, small, after_first)
+    stores = [load(dact, dx_hbm, 1), load(nxt, next_hbm, 0)]
     stores[0].start()
-    totals = jnp.sum(terms_ref[...], axis=1, keepdims=True)
+    for copy in past:
+        copy.wait()
+
+    def after_average(r):
+        pl.when(r == 0)(lambda: reduce(r + LAST_BEAT + 2, 3))
+        pl.when(r == 3)(lambda: reduce(r + LAST_BEAT, 3))
+
+    average(mix_ref, history, g, out, nxt, terms, after_average)
+    stores[1].start()
+    totals = jnp.sum(terms[...], axis=1, keepdims=True)
     lane = iota((1, 128), 1)
-    mix_row = jnp.where(lane == 4, jnp.sum(small[5:6, :], axis=1, keepdims=True), 0.0)
-    for k in range(4):
+    mix_row = jnp.zeros((1, 128), F32)
+    for k in range(5):
         mix_row = jnp.where(lane == k, totals[k : k + 1, :], mix_row)
     if joined:
         values = small[...]
@@ -910,37 +934,39 @@
             msg_g[s, 4:5, :] = mix_row
         sums.start()
         land_g[place.flat()] = msg_g[place.flat() % 16]
-        merge_up(own, raw)
-        stores += [load(own.at[3], go_hbm, 2), load(raw, gu_hbm, 3)]
-        stores += [load(own.at[4 + 2 * k], gd_hbm.at[k], 4 + k) for k in range(4)]
-        for copy in stores[1:]:
+        merge_up(own, lse)
+        part = lambda i: pl.ds(PIECE * i, PIECE)
+        for u in (3, 4, 6, 8, 10):
+            middle[part(u)] = own[u].astype(F32)
+        stores += [load(middle.at[part(3)], go_hbm, 2)]
+        stores += [load(lse.at[part(k)], gu_hbm.at[:, pl.ds(768 * k, 768)], 3 + k) for k in range(4)]
+        stores += [load(middle.at[part(4 + 2 * k)], gd_hbm.at[part(k)], 7 + k) for k in range(4)]
+        for copy in stores[2:]:
             copy.start()
-        reduce(23, 1)
-        reduce(24, 0)
         sums.finish()
 
         def add(k, total):
             return total + land_g[k]
 
-        small_out[...] = lax.fori_loop(0, 32, add, jnp.zeros(small_out.shape, F32))
-        reduce(24, 1)
-        reduce(25, 0)
-        units = [
-            load(own.at[j, :, pl.ds(256 * t, 256)], gq_hbm.at[:, pl.ds(768 * t + 256 * j, 256)], 8 + 3 * j + t)
-            for j in range(3)
-            for t in range(3)
-        ]
-        for copy in units:
-            copy.start()
-        stores += units
+        total = lax.fori_loop(0, 32, add, jnp.zeros(land_g.shape[1:], F32))
+        gains_out[...] = total[0:2, 0:PIECE]
+        first_out[...] = total[2:3, 0:PIECE]
+        second_out[...] = total[3:4, 0:PIECE]
+        mix_out[...] = total[4:5, 0:5]
+        reduce(LAST_BEAT + 4, 2)
+        for j in range(3):
+            middle[part(j)] = own[j].astype(F32)
+            for t in range(3):
+                src, dst = middle.at[part(j), pl.ds(256 * t, 256)], gq_hbm.at[:, pl.ds(768 * t + 256 * j, 256)]
+                stores.append(load(src, dst, 11 + 3 * j + t))
+                stores[-1].start()
     else:
         small[4:5, 0:128] = mix_row
         small[4:5, 128:] = jnp.zeros_like(small[4:5, 128:])
         small_out[...] = small[...]
         stores += [load(spare, grad_hbm.at[0:3], 2), load(w.at[3:], grad_hbm.at[3:], 3)]
-        for copy in stores[1:]:
+        for copy in stores[2:]:
             copy.start()
-    store_next.wait()
     for copy in stores:
         copy.wait()
 
@@ -949,7 +975,7 @@
 UNIT = (4, 2, 2, PIECE, 768)
 
 
-def block_pass(joined, start, mix, x, g, earlier, par, terms, *weights):
+def block_pass(joined, start, mix, x, g, history, par, *weights):
     length, width = x.shape
     smem = pl.BlockSpec(memory_space=pltpu.SMEM)
     vmem = pl.BlockSpec(memory_space=pltpu.VMEM)
@@ -968,13 +994,13 @@
         pltpu.VMEM((length, 128), F32),
         pltpu.VMEM(small, F32),
         pltpu.VMEM(small, F32),
-        dma((18,)),
+        pltpu.VMEM(small, F32),
+        dma((20,)),
     ]
-    grads = [((UNITS,) + UNIT, BF), (small, F32)]
+    grads, sums = [((UNITS,) + UNIT, BF)], [(small, F32)]
     if joined:
-        grads = [
-            ((PIECE, 3 * width), BF), ((PIECE, width), BF), ((PIECE, 4 * width), BF), ((4, PIECE, width), BF), ((8, 128), F32)
-        ]
+        grads = [(shape, F32) for shape in ((PIECE, 3 * width), (PIECE, width), (PIECE, 4 * width), (4 * PIECE, width))]
+        sums = [(shape, F32) for shape in ((1, 5), (2, PIECE), (1, PIECE), (1, PIECE))]
         scratch += [
             pltpu.VMEM((UNITS, PIECE, width), BF),
             pltpu.VMEM((2, 4, 2, PIECE, width), BF),
@@ -998,16 +1024,16 @@
     params = dict(vmem_limit_bytes=VMEM_LIMIT)
     if joined:
         params.update(collective_id=0, has_side_effects=True)
-    outs = [((length, width), BF), ((length, width), F32)] + grads
+    outs = [((length, width), BF), ((length, width), F32)] + grads + sums
     return pl.pallas_call(
         functools.partial(block_kernel, joined),
-        in_specs=[smem, smem, anys, anys, anys] + [vmem] * (len(par) + 2) + [anys] * len(weights),
-        out_specs=[anys] * (len(outs) - 1) + [vmem],
+        in_specs=[smem, smem, anys, anys, anys] + [vmem] * (len(par) + 1) + [anys] * len(weights),
+        out_specs=[anys] * (2 + len(grads)) + [vmem] * len(sums),
         out_shape=[jax.ShapeDtypeStruct(shape, dtype) for shape, dtype in outs],
         scratch_shapes=scratch,
         compiler_params=pltpu.CompilerParams(**params),
         name="block_pass",
-    )(start, mix, x, g, earlier, *par, terms, rotary_table(length), *weights)
+    )(start, mix, x, g, history, *par, rotary_table(length), *weights)
 
 
 def to_units(wq, wo, wu, wd):
@@ -1035,22 +1061,20 @@
 def local(block_input, history, cotangent, span_start, w_qkv, w_out, w_up, w_down, ln_gains, ln_biases, mix_weights, joined):
     width = block_input.shape[1]
     own = ln_gains.shape[1]
-    grad_history, earlier, terms = history_pass(mix_weights, history, cotangent)
+    grad_history = history_grad(mix_weights, cotangent, history.shape[0])
     if joined:
-        nxt, grad_input, gq, go, gu, gd, small = block_pass(
-            True, span_start, mix_weights, block_input, cotangent, earlier, [ln_gains, ln_biases], terms,
+        nxt, grad_input, gq, go, gu, gd, mix, gains, first, second = block_pass(
+            True, span_start, mix_weights, block_input, cotangent, history, [ln_gains, ln_biases],
             w_qkv, w_out, w_up, w_down.reshape(4, own, width),
         )
-        gq, go, gu, gd = [item.astype(F32) for item in (gq, go, gu, gd.reshape(4 * own, width))]
-        norm_grads = small[:4, :own]
-        grad_mix = small[4, :5]
+        return nxt, grad_input, grad_history, mix[0], gq, go, gu, gd, gains, first[0], second[0]
     else:
         gather = lambda item, axis: lax.all_gather(item, "shard", axis=axis, tiled=True)
         mine = jnp.concatenate([ln_gains, ln_biases])
         par = jnp.concatenate([gather(mine, 1).astype(F32), jnp.zeros((4, width), F32)])
         weights = to_units(gather(w_qkv, 0), gather(w_out, 0), gather(w_up, 0), gather(w_down, 0))
         nxt, grad_input, units, small = block_pass(
-            False, span_start, mix_weights, block_input, cotangent, earlier, [par], terms, weights
+            False, span_start, mix_weights, block_input, cotangent, history, [par], weights
         )
 
         def owned(item, axis):

time: 234 us -> 223 us (0.953)
  other arithmetic: 6.03 us -> 0 us
  Pallas kernels: 218 us -> 212 us
    convert_element_type x4 -> x0, other arithmetic: 6.03 us -> none  [local(): item.astype(F32)]
    unnamed x8 -> x30, local copies, waits for them, and re-layouts: 4.13 us -> 9.31 us
    pallas_call x1, Pallas kernels: 208 us -> 205 us  [block_pass(): pl.pallas_call(functools.partial(block_kernel, joined), in_specs=[smem, s...]
    pallas_call x1, Pallas kernels: 10.4 us -> 7.66 us  [history_grad(): pl.pallas_call(history_kernel, grid=(length // height,), in_specs=[pl.Blo...]
    squeeze x2 -> x0, local copies, waits for them, and re-layouts: 2.5 us -> none  [the longest x1 1.32 us: local(): norm_grads[3]]
where the time goes in v4:
time: 223 us
  Pallas kernels  212 us (95%)
  local copies, waits for them, and re-layouts  9.31 us (4%)
    pallas_call x1, Pallas kernels, block_pass(): pl.pallas_call(functools.partial(block_kernel, joined), in_specs=[smem, s...  205 us
    unnamed x30, local copies, waits for them, and re-layouts  9.31 us
    pallas_call x1, Pallas kernels, history_grad(): pl.pallas_call(history_kernel, grid=(length // height,), in_specs=[pl.Blo...  7.66 us

profile of v4, /device:TPU:0, one launch (start us, length us, event | category | flops | bytes accessed | tf_op | source)
XLA Modules:
  0.0 222.9 jit_solution(15942949878429133134)
XLA Ops:
  1.3 204.6 %block_pass.1 = (bf16[1024,768]{1,0:T(8,128)(2,1)}, f32[1024,768]{1,0:T(8,128)}, f32[48,2304]{1,0:T(8,128)}, f32[48,768]{1,0:T(8,128)}, f32[48,3072]{1,0:T(8,128...) custom-call(s32[1]{0:T(128)S(6)} %copy.33.refs_0_, ...), custom_call_target="tpu_custom_call" | custom-call | tf_op jit(solution)/shard_map/block_pass/pallas_call | solution.py:1028
  205.9 0.0 copy-start.1
  205.9 7.7 %history_grad.1 = f32[4,1024,768]{2,1,0:T(8,128)} custom-call(f32[5]{0:T(128)} %mix_ref.1, bf16[1024,768]{1,0:T(8,128)(2,1)} %g_ref.1), custom_call_target="tpu_custom_call" | custom-call | tf_op jit(solution)/shard_map/history_grad/pallas_call | solution.py:535
  213.6 0.0 copy-done.1
  213.6 0.0 copy-start
  213.6 1.1 copy.34
  214.7 1.3 copy-done
  216.0 0.0 copy-start.9
  216.0 0.0 copy-start.4
  216.0 0.0 copy-start.5
  216.0 0.0 copy-start.3
  216.0 0.0 copy-start.2
  216.0 1.7 copy.35
  217.7 0.0 copy-done.9
  217.7 0.0 copy-start.6
  217.7 0.0 copy-start.8
  217.7 0.0 copy-start.7
  217.7 0.5 copy.36
  218.2 0.0 copy-done.4
  218.2 0.8 copy.37
  219.0 0.0 copy-done.5
  219.0 0.7 copy.38
  219.7 0.0 copy-done.3
  219.7 0.8 copy.39
  220.5 0.0 copy-done.2
  220.5 0.8 copy.40
  221.3 0.0 copy-done.6
  221.3 0.6 copy.41
  221.9 0.0 copy-done.8
  221.9 0.5 copy.42
  222.4 0.0 copy-done.7
  222.4 0.5 copy.43
Async XLA Ops:
  205.9 7.7 %copy-start.1 = (bf16[1024,768]{1,0:T(8,128)(2,1)S(1)}, bf16[1024,768]{1,0:T(8,128)(2,1)}, u32[]{:S(2)}) copy-start(bf16[1024,768]{1,0:T(8,128)(2,1)} %get-tuple-element.42) | copy-start | bytes 4718596
  213.6 2.5 %copy-start = (f32[1024,768]{1,0:T(8,128)S(1)}, f32[1024,768]{1,0:T(8,128)}, u32[]{:S(2)}) copy-start(f32[1024,768]{1,0:T(8,128)} %get-tuple-element.43) | copy-start | bytes 9437188
  216.0 1.7 copy-start.9
  216.0 2.2 copy-start.4
  216.0 3.0 %copy-start.5 = (f32[48,768]{1,0:T(8,128)S(1)}, f32[48,768]{1,0:T(8,128)}, u32[]{:S(2)}) copy-start(f32[48,768]{1,0:T(8,128)} %get-tuple-element.47) | copy-start | bytes 442372
  216.0 3.6 %copy-start.3 = (f32[48,3072]{1,0:T(8,128)S(1)}, f32[48,3072]{1,0:T(8,128)}, u32[]{:S(2)}) copy-start(f32[48,3072]{1,0:T(8,128)} %get-tuple-element.48) | copy-start | bytes 1769476
  216.0 4.5 %copy-start.2 = (f32[192,768]{1,0:T(8,128)S(1)}, f32[192,768]{1,0:T(8,128)}, u32[]{:S(2)}) copy-start(f32[192,768]{1,0:T(8,128)} %get-tuple-element.49) | copy-start | bytes 1769476
  217.7 3.6 %copy-start.6 = (f32[2,48]{1,0:T(2,128)S(1)}, f32[2,48]{1,0:T(2,128)}, u32[]{:S(2)}) copy-start(f32[2,48]{1,0:T(2,128)} %get-tuple-element.50) | copy-start | bytes 1156
  217.7 4.2 %copy-start.8 = (f32[1,48]{1,0:T(1,128)S(1)}, f32[1,48]{1,0:T(1,128)}, u32[]{:S(2)}) copy-start(f32[1,48]{1,0:T(1,128)} %get-tuple-element.29) | copy-start | bytes 580
  217.7 4.7 %copy-start.7 = (f32[1,48]{1,0:T(1,128)S(1)}, f32[1,48]{1,0:T(1,128)}, u32[]{:S(2)}) copy-start(f32[1,48]{1,0:T(1,128)} %get-tuple-element.30) | copy-start | bytes 580

commit v5 on v4

--- a/solution.py
+++ b/solution.py
@@ -531,7 +531,7 @@
 
 def history_grad(mix, g, past):
     length, width = g.shape
-    height = 128
+    height = 256
     return pl.pallas_call(
         history_kernel,
         grid=(length // height,),

time: 223 us -> 222 us (level)
  no operation moved by 1% of the time
where the time goes in v5:
time: 222 us
  Pallas kernels  211 us (95%)
  local copies, waits for them, and re-layouts  9.31 us (4%)
    pallas_call x1, Pallas kernels, block_pass(): pl.pallas_call(functools.partial(block_kernel, joined), in_specs=[smem, s...  205 us
    unnamed x30, local copies, waits for them, and re-layouts  9.31 us
    pallas_call x1, Pallas kernels, history_grad(): pl.pallas_call(history_kernel, grid=(length // height,), in_specs=[pl.Blo...  6.26 us

profile of v5, /device:TPU:0, one launch (start us, length us, event | category | flops | bytes accessed | tf_op | source)
XLA Modules:
  0.0 221.5 jit_solution(14767055900808257187)
XLA Ops:
  1.3 204.6 %block_pass.1 = (bf16[1024,768]{1,0:T(8,128)(2,1)}, f32[1024,768]{1,0:T(8,128)}, f32[48,2304]{1,0:T(8,128)}, f32[48,768]{1,0:T(8,128)}, f32[48,3072]{1,0:T(8,128...) custom-call(s32[1]{0:T(128)S(6)} %copy.33.refs_0_, ...), custom_call_target="tpu_custom_call" | custom-call | tf_op jit(solution)/shard_map/block_pass/pallas_call | solution.py:1028
  205.9 0.0 copy-start.1
  205.9 6.3 %history_grad.1 = f32[4,1024,768]{2,1,0:T(8,128)} custom-call(f32[5]{0:T(128)} %mix_ref.1, bf16[1024,768]{1,0:T(8,128)(2,1)} %g_ref.1), custom_call_target="tpu_custom_call" | custom-call | tf_op jit(solution)/shard_map/history_grad/pallas_call | solution.py:535
  212.2 0.0 copy-done.1
  212.2 0.0 copy-start
  212.2 1.1 copy.34
  213.3 1.3 copy-done
  214.6 0.0 copy-start.9
  214.6 0.0 copy-start.4
  214.6 0.0 copy-start.5
  214.6 0.0 copy-start.3
  214.6 0.0 copy-start.2
  214.7 1.7 copy.35
  216.3 0.0 copy-done.9
  216.3 0.0 copy-start.6
  216.3 0.0 copy-start.8
  216.3 0.0 copy-start.7
  216.3 0.5 copy.36
  216.8 0.0 copy-done.4
  216.8 0.8 copy.37
  217.6 0.0 copy-done.5
  217.6 0.7 copy.38
  218.3 0.0 copy-done.3
  218.3 0.8 copy.39
  219.1 0.0 copy-done.2
  219.1 0.8 copy.40
  219.9 0.0 copy-done.6
  219.9 0.6 copy.41
  220.5 0.0 copy-done.8
  220.5 0.5 copy.42
  221.0 0.0 copy-done.7
  221.0 0.5 copy.43
Async XLA Ops:
  205.9 6.3 %copy-start.1 = (bf16[1024,768]{1,0:T(8,128)(2,1)S(1)}, bf16[1024,768]{1,0:T(8,128)(2,1)}, u32[]{:S(2)}) copy-start(bf16[1024,768]{1,0:T(8,128)(2,1)} %get-tuple-element.42) | copy-start | bytes 4718596
  212.2 2.5 %copy-start = (f32[1024,768]{1,0:T(8,128)S(1)}, f32[1024,768]{1,0:T(8,128)}, u32[]{:S(2)}) copy-start(f32[1024,768]{1,0:T(8,128)} %get-tuple-element.43) | copy-start | bytes 9437188
  214.6 1.7 copy-start.9
  214.6 2.2 copy-start.4
  214.6 3.0 %copy-start.5 = (f32[48,768]{1,0:T(8,128)S(1)}, f32[48,768]{1,0:T(8,128)}, u32[]{:S(2)}) copy-start(f32[48,768]{1,0:T(8,128)} %get-tuple-element.47) | copy-start | bytes 442372
  214.6 3.6 %copy-start.3 = (f32[48,3072]{1,0:T(8,128)S(1)}, f32[48,3072]{1,0:T(8,128)}, u32[]{:S(2)}) copy-start(f32[48,3072]{1,0:T(8,128)} %get-tuple-element.48) | copy-start | bytes 1769476
  214.6 4.5 %copy-start.2 = (f32[192,768]{1,0:T(8,128)S(1)}, f32[192,768]{1,0:T(8,128)}, u32[]{:S(2)}) copy-start(f32[192,768]{1,0:T(8,128)} %get-tuple-element.49) | copy-start | bytes 1769476
  216.3 3.6 %copy-start.6 = (f32[2,48]{1,0:T(2,128)S(1)}, f32[2,48]{1,0:T(2,128)}, u32[]{:S(2)}) copy-start(f32[2,48]{1,0:T(2,128)} %get-tuple-element.50) | copy-start | bytes 1156
  216.3 4.2 %copy-start.8 = (f32[1,48]{1,0:T(1,128)S(1)}, f32[1,48]{1,0:T(1,128)}, u32[]{:S(2)}) copy-start(f32[1,48]{1,0:T(1,128)} %get-tuple-element.29) | copy-start | bytes 580
  216.3 4.7 %copy-start.7 = (f32[1,48]{1,0:T(1,128)S(1)}, f32[1,48]{1,0:T(1,128)}, u32[]{:S(2)}) copy-start(f32[1,48]{1,0:T(1,128)} %get-tuple-element.30) | copy-start | bytes 580
